TPU v7x, 512 devices: a whole 4x8x8 slice. The times are simulated.
512 devices in a mesh: section: 16 (over z_lo, y), seq: 32 (over z_hi, x, core).
Axes of the slice: x: 4, y: 8, z: 8 (z_hi: 4, z_lo: 2; z = z_hi * 2 + z_lo), core: 2. Of those that a mesh axis runs over, the one named last changes fastest.
Arguments:
- query_heads: bfloat16 [16, 4096, 4096], P('section', 'seq'), may hold values from -24 to 24
- key_heads: bfloat16 [16, 4096, 512], P('section', 'seq'), may hold values from -6 to 6
- value_heads: bfloat16 [16, 4096, 512], P('section', 'seq'), may hold values from -6 to 6
- section_cotangent: bfloat16 [16, 4096, 4096], P('section', 'seq'), may hold values from -6 to 6
- block_mask: int32 [32, 7], P('seq'), may hold values 0 or 1
Outputs:
- query_grad: bfloat16 [16, 4096, 4096], P('section', 'seq')
- key_grad: bfloat16 [16, 4096, 512], P('section', 'seq')
- value_grad: bfloat16 [16, 4096, 512], P('section', 'seq')
All inputs are finite; a program needn't handle non-finite values. No bound on the sum of `block_mask` on one device may be relied on, other than what follows from the above.
Results may differ from a plain program's by a relative error of at most 0.0058.
Values may be sent and summed in bfloat16 or wider, within the bound.
No kernel may reach another device: no remote copies, remote signals or barrier semaphores. Data moves between devices by JAX's collectives and lax.ppermute only.
A program may use at most 128 MiB of HBM per device.

v0:
```python
import math

import jax
import jax.numpy as jnp
from jax import lax
from jax.sharding import PartitionSpec as P

HQ = 32
HK = 4
HD = 128
W = 3


def passed_along(x, axis, by):
    peers = lax.axis_size(axis)
    return lax.ppermute(x, axis, [(i, (i + by) % peers) for i in range(peers)])


def from_behind(value, axis, steps):
    count = lax.axis_size(axis)
    leading, last = (max(0, -steps), min(count, count - steps))
    return lax.ppermute(value, axis, [(source, source + steps) for source in range(leading, last)])


def shards(query_heads, key_heads, value_heads, section_cotangent, block_mask):
    seq_count = lax.axis_size("seq")
    seq_index = lax.axis_index("seq")
    block_len = query_heads.shape[1]
    groups = HQ // HK
    window_len = 2 * W + 1
    score_scale = 1.0 / math.sqrt(HD)
    grad_out = passed_along(section_cotangent, "section", -1)
    own_keys = key_heads[0]
    own_values = value_heads[0]
    by_offset = {0: (own_keys, own_values)}
    for offset in range(-W, W + 1):
        if offset != 0:
            by_offset[offset] = from_behind((own_keys, own_values), "seq", -offset)
    near_pairs = [by_offset[offset] for offset in range(-W, W + 1)]
    flags = []
    for offset in range(-W, W + 1):
        inside = (seq_index + offset >= 0) & (seq_index + offset < seq_count)
        if offset == 0:
            flags.append(inside)
        else:
            flags.append(inside & (block_mask[0, offset + W] == 1))
    column_flags = jnp.repeat(jnp.stack(flags), block_len)
    near_keys = jnp.stack([pair[0] for pair in near_pairs])
    near_values = jnp.stack([pair[1] for pair in near_pairs])
    query_pieces = []
    key_pieces = []
    value_pieces = []
    for group in range(HK):
        low_col = group * groups * HD
        high_col = (group + 1) * groups * HD
        q_group = query_heads[0][:, low_col:high_col].reshape(block_len, groups, HD)
        g_group = grad_out[0][:, low_col:high_col].reshape(block_len, groups, HD)
        k_group = near_keys[:, :, group * HD : (group + 1) * HD]
        v_group = near_values[:, :, group * HD : (group + 1) * HD]
        scores = jnp.einsum("qgd,jkd->gqjk", q_group, k_group, preferred_element_type=jnp.float32)
        scores = scores.reshape(groups, block_len, window_len * block_len)
        grad_probs = jnp.einsum(
            "qgd,jkd->gqjk", g_group, v_group, preferred_element_type=jnp.float32
        )
        grad_probs = grad_probs.reshape(groups, block_len, window_len * block_len)
        scores = jnp.where(column_flags, scores * score_scale, -jnp.inf)
        row_peak = jnp.max(scores, axis=-1, keepdims=True)
        weights = jnp.exp(scores - row_peak)
        probs = weights / jnp.sum(weights, axis=-1, keepdims=True)
        row_delta = jnp.sum(probs * grad_probs, axis=-1, keepdims=True)
        dscore = (probs * (grad_probs - row_delta)).astype(jnp.bfloat16)
        probs_b = probs.astype(jnp.bfloat16)
        query_part = jnp.einsum(
            "gqk,kd->qgd",
            dscore,
            k_group.reshape(window_len * block_len, HD),
            preferred_element_type=jnp.float32,
        )
        key_part = jnp.einsum(
            "gqjk,qgd->jkd",
            dscore.reshape(groups, block_len, window_len, block_len),
            q_group,
            preferred_element_type=jnp.float32,
        )
        value_part = jnp.einsum(
            "gqjk,qgd->jkd",
            probs_b.reshape(groups, block_len, window_len, block_len),
            g_group,
            preferred_element_type=jnp.float32,
        )
        query_pieces.append(query_part.reshape(block_len, groups * HD))
        key_pieces.append(key_part)
        value_pieces.append(value_part)
    query_grad = (jnp.concatenate(query_pieces, axis=1) * score_scale).astype(jnp.bfloat16)
    key_parts = (jnp.concatenate(key_pieces, axis=2) * score_scale).astype(jnp.bfloat16)
    value_parts = jnp.concatenate(value_pieces, axis=2).astype(jnp.bfloat16)
    key_total = key_parts[W].astype(jnp.float32)
    value_total = value_parts[W].astype(jnp.float32)
    for offset in range(-W, W + 1):
        if offset != 0:
            arrived_keys, arrived_values = from_behind(
                (key_parts[offset + W], value_parts[offset + W]), "seq", offset
            )
            key_total = key_total + arrived_keys.astype(jnp.float32)
            value_total = value_total + arrived_values.astype(jnp.float32)
    return (
        query_grad[None],
        key_total.astype(jnp.bfloat16)[None],
        value_total.astype(jnp.bfloat16)[None],
    )


def solution(mesh):
    in_specs = (
        P("section", "seq", None),
        P("section", "seq", None),
        P("section", "seq", None),
        P("section", "seq", None),
        P("seq", None),
    )
    out_specs = (P("section", "seq", None), P("section", "seq", None), P("section", "seq", None))
    return jax.shard_map(shards, mesh=mesh, in_specs=in_specs, out_specs=out_specs, check_vma=False)
```

profile of v0, /device:TPU:377, one launch (start us, length us, event | category | flops | bytes accessed | tf_op | source)
XLA Modules:
  0.0 188.9 jit_solution(6043900726841575822)
XLA Ops:
  0.7 5.3 %collective-permute-start = (bf16[128,512]{1,0:T(8,128)(2,1)}, bf16[128,512]{1,0:T(8,128)(2,1)}, u32[]{:S(2)}, u32[]{:S(2)}) collective-permute-start(bf16[128,512]{1,0:T(8,128)(2,1)} %bitcast.385), channel_id=1, source_target_pairs={{0,3},{1,4},{2,5},{3,6},{4,7},{5,8},{6,9},{7,10},{8,11},{9,12},{10... | collective-permute-start | bytes 393224 | tf_op jit(solution)/shard_map/ppermute | solution.py:22
  6.0 2.2 %collective-permute-start.1 = (bf16[128,512]{1,0:T(8,128)(2,1)}, bf16[128,512]{1,0:T(8,128)(2,1)}, u32[]{:S(2)}, u32[]{:S(2)}) collective-permute-start(bf16[128,512]{1,0:T(8,128)(2,1)} %bitcast.386), channel_id=1, source_target_pairs={{0,2},{1,3},{2,4},{3,5},{4,6},{5,7},{6,8},{7,9},{8,10},{9,11},{10,... | collective-permute-start | bytes 393224 | tf_op jit(solution)/shard_map/ppermute | solution.py:22
  8.2 2.2 %collective-permute-start.2 = (bf16[128,512]{1,0:T(8,128)(2,1)}, bf16[128,512]{1,0:T(8,128)(2,1)}, u32[]{:S(2)}, u32[]{:S(2)}) collective-permute-start(bf16[128,512]{1,0:T(8,128)(2,1)} %bitcast.387), channel_id=1, source_target_pairs={{0,1},{1,2},{2,3},{3,4},{4,5},{5,6},{6,7},{7,8},{8,9},{9,10},{10,1... | collective-permute-start | bytes 393224 | tf_op jit(solution)/shard_map/ppermute | solution.py:22
  10.4 2.1 %collective-permute-start.3 = (bf16[128,512]{1,0:T(8,128)(2,1)}, bf16[128,512]{1,0:T(8,128)(2,1)}, u32[]{:S(2)}, u32[]{:S(2)}) collective-permute-start(bf16[128,512]{1,0:T(8,128)(2,1)} %bitcast.388), channel_id=1, source_target_pairs={{1,0},{2,1},{3,2},{4,3},{5,4},{6,5},{7,6},{8,7},{9,8},{10,9},{11,1... | collective-permute-start | bytes 393224 | tf_op jit(solution)/shard_map/ppermute | solution.py:22
  12.6 7.3 %collective-permute-start.4 = (bf16[128,512]{1,0:T(8,128)(2,1)}, bf16[128,512]{1,0:T(8,128)(2,1)S(1)}, u32[]{:S(2)}, u32[]{:S(2)}) collective-permute-start(bf16[128,512]{1,0:T(8,128)(2,1)} %bitcast.389), channel_id=1, source_target_pairs={{2,0},{3,1},{4,2},{5,3},{6,4},{7,5},{8,6},{9,7},{10,8},{11,9},{12,... | collective-permute-start | bytes 393224 | tf_op jit(solution)/shard_map/ppermute | solution.py:22
  28.8 2.1 %collective-permute-start.5 = (bf16[128,512]{1,0:T(8,128)(2,1)S(1)}, bf16[128,512]{1,0:T(8,128)(2,1)S(1)}, u32[]{:S(2)}, u32[]{:S(2)}) collective-permute-start(bf16[128,512]{1,0:T(8,128)(2,1)S(1)} %bitcast.390), channel_id=1, source_target_pairs={{3,0},{4,1},{5,2},{6,3},{7,4},{8,5},{9,6},{10,7},{11,8},{12,9},{13... | collective-permute-start | bytes 393224 | tf_op jit(solution)/shard_map/ppermute | solution.py:22
  31.9 4.9 %collective-permute-start.6 = (bf16[128,512]{1,0:T(8,128)(2,1)S(1)}, bf16[128,512]{1,0:T(8,128)(2,1)S(1)}, u32[]{:S(2)}, u32[]{:S(2)}) collective-permute-start(bf16[128,512]{1,0:T(8,128)(2,1)S(1)} %bitcast.391), channel_id=1, source_target_pairs={{0,3},{1,4},{2,5},{3,6},{4,7},{5,8},{6,9},{7,10},{8,11},{9,12},{10... | collective-permute-start | bytes 393224 | tf_op jit(solution)/shard_map/ppermute | solution.py:22
  40.6 1.9 %collective-permute-start.8 = (bf16[128,512]{1,0:T(8,128)(2,1)S(1)}, bf16[128,512]{1,0:T(8,128)(2,1)S(1)}, u32[]{:S(2)}, u32[]{:S(2)}) collective-permute-start(bf16[128,512]{1,0:T(8,128)(2,1)S(1)} %bitcast.393), channel_id=1, source_target_pairs={{0,1},{1,2},{2,3},{3,4},{4,5},{5,6},{6,7},{7,8},{8,9},{9,10},{10,1... | collective-permute-start | bytes 393224 | tf_op jit(solution)/shard_map/ppermute | solution.py:22
  43.5 2.4 %collective-permute-start.9 = (bf16[128,512]{1,0:T(8,128)(2,1)S(1)}, bf16[128,512]{1,0:T(8,128)(2,1)S(1)}, u32[]{:S(2)}, u32[]{:S(2)}) collective-permute-start(bf16[128,512]{1,0:T(8,128)(2,1)S(1)} %bitcast.394), channel_id=1, source_target_pairs={{1,0},{2,1},{3,2},{4,3},{5,4},{6,5},{7,6},{8,7},{9,8},{10,9},{11,1... | collective-permute-start | bytes 393224 | tf_op jit(solution)/shard_map/ppermute | solution.py:22
  45.9 7.6 %collective-permute-start.10 = (bf16[128,512]{1,0:T(8,128)(2,1)S(1)}, bf16[128,512]{1,0:T(8,128)(2,1)S(1)}, u32[]{:S(2)}, u32[]{:S(2)}) collective-permute-start(bf16[128,512]{1,0:T(8,128)(2,1)S(1)} %bitcast.395), channel_id=1, source_target_pairs={{2,0},{3,1},{4,2},{5,3},{6,4},{7,5},{8,6},{9,7},{10,8},{11,9},{12,... | collective-permute-start | bytes 393224 | tf_op jit(solution)/shard_map/ppermute | solution.py:22
  54.8 2.4 %collective-permute-start.11 = (bf16[128,512]{1,0:T(8,128)(2,1)S(1)}, bf16[128,512]{1,0:T(8,128)(2,1)S(1)}, u32[]{:S(2)}, u32[]{:S(2)}) collective-permute-start(bf16[128,512]{1,0:T(8,128)(2,1)S(1)} %bitcast.396), channel_id=1, source_target_pairs={{3,0},{4,1},{5,2},{6,3},{7,4},{8,5},{9,6},{10,7},{11,8},{12,9},{13... | collective-permute-start | bytes 393224 | tf_op jit(solution)/shard_map/ppermute | solution.py:22
  57.3 3.0 %collective-permute-start.12 = (bf16[1,128,4096]{1,2,0:T(8,128)(2,1)S(1)}, bf16[1,128,4096]{1,2,0:T(8,128)(2,1)S(1)}, u32[]{:S(2)}, u32[]{:S(2)}) collective-permute-start(bf16[1,128,4096]{1,2,0:T(8,128)(2,1)S(1)} %copy.40), channel_id=1, source_target_pairs={{0,480},{32,0},{64,32},{96,64},{128,96},{160,128},{192,160},{224,1... | collective-permute-start | bytes 3145736 | tf_op jit(solution)/shard_map/ppermute | solution.py:16
  60.4 2.2 %collective-permute-done.11 = bf16[128,512]{1,0:T(8,128)(2,1)S(1)} collective-permute-done((bf16[128,512]{1,0:T(8,128)(2,1)S(1)}, bf16[128,512]{1,0:T(8,128)(2,1)S(1)}, u32[]{:S(2)}, u32[]{:S(2)}) %collective-permute-start.11) | collective-permute-done | bytes 131104 | tf_op jit(solution)/shard_map/ppermute | solution.py:22
  64.7 21.3 %collective-permute-done.12 = bf16[1,128,4096]{1,2,0:T(8,128)(2,1)S(1)} collective-permute-done((bf16[1,128,4096]{1,2,0:T(8,128)(2,1)S(1)}, bf16[1,128,4096]{1,2,0:T(8,128)(2,1)S(1)}, u32[]{:S(2)}, u32[]{:S(2)}) %collective-permute-start.12) | collective-permute-done | bytes 1048608 | tf_op jit(solution)/shard_map/ppermute | solution.py:16
  87.9 3.6 %fusion.12 = (f32[8,128]{1,0:T(8,128)S(1)}, f32[8,128]{1,0:T(8,128)S(1)}, f32[8,128]{1,0:T(8,128)S(1)}, f32[8,128]{1,0:T(8,128)S(1)}, f32[7,128,128,8]{2,1,3,0:T(8,128)}) fusion(f32[8,128]{1,0:T(8,128)S(1)} %fusion.17, f32[8,128]{1,0:T(8,128)S(1)} %get-tuple-element.47, f32[7,128,128,8]{2,1,3,0:T(8,128)S(1)} %get-tuple-element.48, ...), kind=kOutput, calls=%fused_computation.26 | convolution fusion | flops 248639488 | bytes 18866688 | tf_op jit(solution)/shard_map/qgd,jkd->gqjk/dot_general | solution.py:62
  94.8 4.0 %fusion.8 = (f32[8,128]{1,0:T(8,128)S(1)}, f32[8,128]{1,0:T(8,128)S(1)}, f32[8,128]{1,0:T(8,128)S(1)}, f32[7,128,128,8]{2,1,3,0:T(8,128)}) fusion(f32[8,128]{1,0:T(8,128)S(1)} %fusion.19, f32[8,128]{1,0:T(8,128)S(1)} %get-tuple-element.10, f32[7,128,128,8]{2,1,3,0:T(8,128)S(1)} %fusion.76, pred[7]{0:T(512)(128)(4,1)S(1)} %stack.80, ...), kind=kOutput, calls=%fused_computation.18 | convolution fusion | flops 247723008 | bytes 15200768 | tf_op jit(solution)/shard_map/qgd,jkd->gqjk/dot_general | solution.py:62
  102.4 3.4 %fusion.4 = (f32[8,128]{1,0:T(8,128)S(1)}, f32[8,128]{1,0:T(8,128)S(1)}, f32[7,128,128,8]{2,1,3,0:T(8,128)}) fusion(f32[8,128]{1,0:T(8,128)S(1)} %get-tuple-element.14, f32[8,128]{1,0:T(8,128)S(1)} %get-tuple-element.11, f32[7,128,128,8]{2,1,3,0:T(8,128)S(1)} %fusion.78, pred[7]{0:T(512)(128)(4,1)S(1)} %stack.80, f32[7,128,128,8]{2,1,3,0:T(8,128)S(1)} %fusion.70, ...), kind=kOutput, calls=%fused_computation.10 | convolution fusion | flops 245889024 | bytes 15196672 | tf_op jit(solution)/shard_map/qgd,jkd->gqjk/dot_general | solution.py:62
  105.8 5.8 %fusion.14 = (bf16[8,128,7,128]{1,3,0,2:T(8,128)(2,1)S(1)}, bf16[8,128,7,128]{1,3,0,2:T(8,128)(2,1)S(1)}, bf16[8,128,7,128]{1,3,0,2:T(8,128)(2,1)S(1)}) fusion(f32[7,128,128,8]{2,1,3,0:T(8,128)} %get-tuple-element.49, f32[8,128]{1,0:T(8,128)S(1)} %get-tuple-element.9, f32[8,128]{1,0:T(8,128)S(1)} %fusion.17, f32[8,128]{1,0:T(8,128)S(1)} %get-tuple-element.47, ...), kind=kLoop, calls=%fused_computation.28 | loop fusion | flops 19267584 | bytes 27561992 | tf_op jit(solution)/shard_map/convert_element_type | solution.py:71
  121.7 12.6 %collective-permute-start.19 = (bf16[128,512]{0,1:T(8,128)(2,1)}, bf16[128,512]{0,1:T(8,128)(2,1)}, u32[]{:S(2)}, u32[]{:S(2)}) collective-permute-start(bf16[128,512]{0,1:T(8,128)(2,1)} %get-tuple-element.26), channel_id=1, source_target_pairs={{3,0},{4,1},{5,2},{6,3},{7,4},{8,5},{9,6},{10,7},{11,8},{12,9},{13... | collective-permute-start | bytes 393224 | tf_op jit(solution)/shard_map/ppermute | solution.py:22
  134.2 1.9 %collective-permute-start.20 = (bf16[128,512]{0,1:T(8,128)(2,1)}, bf16[128,512]{0,1:T(8,128)(2,1)}, u32[]{:S(2)}, u32[]{:S(2)}) collective-permute-start(bf16[128,512]{0,1:T(8,128)(2,1)} %get-tuple-element.31), channel_id=1, source_target_pairs={{2,0},{3,1},{4,2},{5,3},{6,4},{7,5},{8,6},{9,7},{10,8},{11,9},{12,... | collective-permute-start | bytes 393224 | tf_op jit(solution)/shard_map/ppermute | solution.py:22
  136.2 2.3 %collective-permute-start.21 = (bf16[128,512]{0,1:T(8,128)(2,1)}, bf16[128,512]{0,1:T(8,128)(2,1)}, u32[]{:S(2)}, u32[]{:S(2)}) collective-permute-start(bf16[128,512]{0,1:T(8,128)(2,1)} %get-tuple-element.30), channel_id=1, source_target_pairs={{1,0},{2,1},{3,2},{4,3},{5,4},{6,5},{7,6},{8,7},{9,8},{10,9},{11,1... | collective-permute-start | bytes 393224 | tf_op jit(solution)/shard_map/ppermute | solution.py:22
  138.5 3.4 %collective-permute-start.22 = (bf16[128,512]{0,1:T(8,128)(2,1)}, bf16[128,512]{0,1:T(8,128)(2,1)}, u32[]{:S(2)}, u32[]{:S(2)}) collective-permute-start(bf16[128,512]{0,1:T(8,128)(2,1)} %get-tuple-element.29), channel_id=1, source_target_pairs={{0,1},{1,2},{2,3},{3,4},{4,5},{5,6},{6,7},{7,8},{8,9},{9,10},{10,1... | collective-permute-start | bytes 393224 | tf_op jit(solution)/shard_map/ppermute | solution.py:22
  141.9 3.2 %collective-permute-start.23 = (bf16[128,512]{0,1:T(8,128)(2,1)}, bf16[128,512]{0,1:T(8,128)(2,1)}, u32[]{:S(2)}, u32[]{:S(2)}) collective-permute-start(bf16[128,512]{0,1:T(8,128)(2,1)} %get-tuple-element.28), channel_id=1, source_target_pairs={{0,2},{1,3},{2,4},{3,5},{4,6},{5,7},{6,8},{7,9},{8,10},{9,11},{10,... | collective-permute-start | bytes 393224 | tf_op jit(solution)/shard_map/ppermute | solution.py:22
  151.5 2.2 %collective-permute-start.24 = (bf16[128,512]{0,1:T(8,128)(2,1)S(1)}, bf16[128,512]{0,1:T(8,128)(2,1)S(1)}, u32[]{:S(2)}, u32[]{:S(2)}) collective-permute-start(bf16[128,512]{0,1:T(8,128)(2,1)S(1)} %get-tuple-element.27), channel_id=1, source_target_pairs={{0,3},{1,4},{2,5},{3,6},{4,7},{5,8},{6,9},{7,10},{8,11},{9,12},{10... | collective-permute-start | bytes 393224 | tf_op jit(solution)/shard_map/ppermute | solution.py:22
  153.8 7.5 %collective-permute-start.13 = (bf16[128,512]{0,1:T(8,128)(2,1)S(1)}, bf16[128,512]{0,1:T(8,128)(2,1)S(1)}, u32[]{:S(2)}, u32[]{:S(2)}) collective-permute-start(bf16[128,512]{0,1:T(8,128)(2,1)S(1)} %get-tuple-element.32), channel_id=1, source_target_pairs={{3,0},{4,1},{5,2},{6,3},{7,4},{8,5},{9,6},{10,7},{11,8},{12,9},{13... | collective-permute-start | bytes 393224 | tf_op jit(solution)/shard_map/ppermute | solution.py:22
  162.5 2.1 %collective-permute-start.14 = (bf16[128,512]{0,1:T(8,128)(2,1)}, bf16[128,512]{0,1:T(8,128)(2,1)S(1)}, u32[]{:S(2)}, u32[]{:S(2)}) collective-permute-start(bf16[128,512]{0,1:T(8,128)(2,1)} %get-tuple-element.37), channel_id=1, source_target_pairs={{2,0},{3,1},{4,2},{5,3},{6,4},{7,5},{8,6},{9,7},{10,8},{11,9},{12,... | collective-permute-start | bytes 393224 | tf_op jit(solution)/shard_map/ppermute | solution.py:22
  164.6 3.0 %collective-permute-start.15 = (bf16[128,512]{0,1:T(8,128)(2,1)S(1)}, bf16[128,512]{0,1:T(8,128)(2,1)S(1)}, u32[]{:S(2)}, u32[]{:S(2)}) collective-permute-start(bf16[128,512]{0,1:T(8,128)(2,1)S(1)} %get-tuple-element.36), channel_id=1, source_target_pairs={{1,0},{2,1},{3,2},{4,3},{5,4},{6,5},{7,6},{8,7},{9,8},{10,9},{11,1... | collective-permute-start | bytes 393224 | tf_op jit(solution)/shard_map/ppermute | solution.py:22
  167.6 2.6 %collective-permute-start.16 = (bf16[128,512]{0,1:T(8,128)(2,1)S(1)}, bf16[128,512]{0,1:T(8,128)(2,1)S(1)}, u32[]{:S(2)}, u32[]{:S(2)}) collective-permute-start(bf16[128,512]{0,1:T(8,128)(2,1)S(1)} %get-tuple-element.35), channel_id=1, source_target_pairs={{0,1},{1,2},{2,3},{3,4},{4,5},{5,6},{6,7},{7,8},{8,9},{9,10},{10,1... | collective-permute-start | bytes 393224 | tf_op jit(solution)/shard_map/ppermute | solution.py:22
  170.2 3.2 %collective-permute-start.17 = (bf16[128,512]{0,1:T(8,128)(2,1)S(1)}, bf16[128,512]{0,1:T(8,128)(2,1)S(1)}, u32[]{:S(2)}, u32[]{:S(2)}) collective-permute-start(bf16[128,512]{0,1:T(8,128)(2,1)S(1)} %get-tuple-element.34), channel_id=1, source_target_pairs={{0,2},{1,3},{2,4},{3,5},{4,6},{5,7},{6,8},{7,9},{8,10},{9,11},{10,... | collective-permute-start | bytes 393224 | tf_op jit(solution)/shard_map/ppermute | solution.py:22
  173.5 2.3 %collective-permute-start.18 = (bf16[128,512]{0,1:T(8,128)(2,1)S(1)}, bf16[128,512]{0,1:T(8,128)(2,1)S(1)}, u32[]{:S(2)}, u32[]{:S(2)}) collective-permute-start(bf16[128,512]{0,1:T(8,128)(2,1)S(1)} %get-tuple-element.33), channel_id=1, source_target_pairs={{0,3},{1,4},{2,5},{3,6},{4,7},{5,8},{6,9},{7,10},{8,11},{9,12},{10... | collective-permute-start | bytes 393224 | tf_op jit(solution)/shard_map/ppermute | solution.py:22
  177.8 3.7 %collective-permute-done.17 = bf16[128,512]{0,1:T(8,128)(2,1)S(1)} collective-permute-done((bf16[128,512]{0,1:T(8,128)(2,1)S(1)}, bf16[128,512]{0,1:T(8,128)(2,1)S(1)}, u32[]{:S(2)}, u32[]{:S(2)}) %collective-permute-start.17) | collective-permute-done | bytes 131104 | tf_op jit(solution)/shard_map/ppermute | solution.py:22
  181.5 5.5 %collective-permute-done.18 = bf16[128,512]{0,1:T(8,128)(2,1)S(1)} collective-permute-done((bf16[128,512]{0,1:T(8,128)(2,1)S(1)}, bf16[128,512]{0,1:T(8,128)(2,1)S(1)}, u32[]{:S(2)}, u32[]{:S(2)}) %collective-permute-start.18) | collective-permute-done | bytes 131104 | tf_op jit(solution)/shard_map/ppermute | solution.py:22
  (99 shorter events, 44.2 us)
Async XLA Ops:
  0.6 28.2 %copy-start.9 = (bf16[1,128,512]{2,1,0:T(8,128)(2,1)S(1)}, bf16[1,128,512]{2,1,0:T(8,128)(2,1)}, u32[]{:S(2)}) copy-start(bf16[1,128,512]{2,1,0:T(8,128)(2,1)} %param.6) | copy-start | bytes 393220
  0.6 31.3 %copy-start.10 = (bf16[1,128,512]{2,1,0:T(8,128)(2,1)S(1)}, bf16[1,128,512]{2,1,0:T(8,128)(2,1)}, u32[]{:S(2)}) copy-start(bf16[1,128,512]{2,1,0:T(8,128)(2,1)} %param.7) | copy-start | bytes 393220
  0.7 28.1 %collective-permute-start = (bf16[128,512]{1,0:T(8,128)(2,1)}, bf16[128,512]{1,0:T(8,128)(2,1)}, u32[]{:S(2)}, u32[]{:S(2)}) collective-permute-start(bf16[128,512]{1,0:T(8,128)(2,1)} %bitcast.385), channel_id=1, source_target_pairs={{0,3},{1,4},{2,5},{3,6},{4,7},{5,8},{6,9},{7,10},{8,11},{9,12},{10... | collective-permute-start | bytes 393224 | tf_op jit(solution)/shard_map/ppermute | solution.py:22
  6.0 25.9 %collective-permute-start.1 = (bf16[128,512]{1,0:T(8,128)(2,1)}, bf16[128,512]{1,0:T(8,128)(2,1)}, u32[]{:S(2)}, u32[]{:S(2)}) collective-permute-start(bf16[128,512]{1,0:T(8,128)(2,1)} %bitcast.386), channel_id=1, source_target_pairs={{0,2},{1,3},{2,4},{3,5},{4,6},{5,7},{6,8},{7,9},{8,10},{9,11},{10,... | collective-permute-start | bytes 393224 | tf_op jit(solution)/shard_map/ppermute | solution.py:22
  8.2 29.5 %collective-permute-start.2 = (bf16[128,512]{1,0:T(8,128)(2,1)}, bf16[128,512]{1,0:T(8,128)(2,1)}, u32[]{:S(2)}, u32[]{:S(2)}) collective-permute-start(bf16[128,512]{1,0:T(8,128)(2,1)} %bitcast.387), channel_id=1, source_target_pairs={{0,1},{1,2},{2,3},{3,4},{4,5},{5,6},{6,7},{7,8},{8,9},{9,10},{10,1... | collective-permute-start | bytes 393224 | tf_op jit(solution)/shard_map/ppermute | solution.py:22
  10.4 30.2 %collective-permute-start.3 = (bf16[128,512]{1,0:T(8,128)(2,1)}, bf16[128,512]{1,0:T(8,128)(2,1)}, u32[]{:S(2)}, u32[]{:S(2)}) collective-permute-start(bf16[128,512]{1,0:T(8,128)(2,1)} %bitcast.388), channel_id=1, source_target_pairs={{1,0},{2,1},{3,2},{4,3},{5,4},{6,5},{7,6},{8,7},{9,8},{10,9},{11,1... | collective-permute-start | bytes 393224 | tf_op jit(solution)/shard_map/ppermute | solution.py:22
  12.6 30.9 %collective-permute-start.4 = (bf16[128,512]{1,0:T(8,128)(2,1)}, bf16[128,512]{1,0:T(8,128)(2,1)S(1)}, u32[]{:S(2)}, u32[]{:S(2)}) collective-permute-start(bf16[128,512]{1,0:T(8,128)(2,1)} %bitcast.389), channel_id=1, source_target_pairs={{2,0},{3,1},{4,2},{5,3},{6,4},{7,5},{8,6},{9,7},{10,8},{11,9},{12,... | collective-permute-start | bytes 393224 | tf_op jit(solution)/shard_map/ppermute | solution.py:22
  28.8 17.1 %collective-permute-start.5 = (bf16[128,512]{1,0:T(8,128)(2,1)S(1)}, bf16[128,512]{1,0:T(8,128)(2,1)S(1)}, u32[]{:S(2)}, u32[]{:S(2)}) collective-permute-start(bf16[128,512]{1,0:T(8,128)(2,1)S(1)} %bitcast.390), channel_id=1, source_target_pairs={{3,0},{4,1},{5,2},{6,3},{7,4},{8,5},{9,6},{10,7},{11,8},{12,9},{13... | collective-permute-start | bytes 393224 | tf_op jit(solution)/shard_map/ppermute | solution.py:22
  31.9 22.9 %collective-permute-start.6 = (bf16[128,512]{1,0:T(8,128)(2,1)S(1)}, bf16[128,512]{1,0:T(8,128)(2,1)S(1)}, u32[]{:S(2)}, u32[]{:S(2)}) collective-permute-start(bf16[128,512]{1,0:T(8,128)(2,1)S(1)} %bitcast.391), channel_id=1, source_target_pairs={{0,3},{1,4},{2,5},{3,6},{4,7},{5,8},{6,9},{7,10},{8,11},{9,12},{10... | collective-permute-start | bytes 393224 | tf_op jit(solution)/shard_map/ppermute | solution.py:22
  37.8 19.5 %collective-permute-start.7 = (bf16[128,512]{1,0:T(8,128)(2,1)S(1)}, bf16[128,512]{1,0:T(8,128)(2,1)S(1)}, u32[]{:S(2)}, u32[]{:S(2)}) collective-permute-start(bf16[128,512]{1,0:T(8,128)(2,1)S(1)} %bitcast.392), channel_id=1, source_target_pairs={{0,2},{1,3},{2,4},{3,5},{4,6},{5,7},{6,8},{7,9},{8,10},{9,11},{10,... | collective-permute-start | bytes 393224 | tf_op jit(solution)/shard_map/ppermute | solution.py:22
  40.6 19.7 %collective-permute-start.8 = (bf16[128,512]{1,0:T(8,128)(2,1)S(1)}, bf16[128,512]{1,0:T(8,128)(2,1)S(1)}, u32[]{:S(2)}, u32[]{:S(2)}) collective-permute-start(bf16[128,512]{1,0:T(8,128)(2,1)S(1)} %bitcast.393), channel_id=1, source_target_pairs={{0,1},{1,2},{2,3},{3,4},{4,5},{5,6},{6,7},{7,8},{8,9},{9,10},{10,1... | collective-permute-start | bytes 393224 | tf_op jit(solution)/shard_map/ppermute | solution.py:22
  43.5 16.8 %collective-permute-start.9 = (bf16[128,512]{1,0:T(8,128)(2,1)S(1)}, bf16[128,512]{1,0:T(8,128)(2,1)S(1)}, u32[]{:S(2)}, u32[]{:S(2)}) collective-permute-start(bf16[128,512]{1,0:T(8,128)(2,1)S(1)} %bitcast.394), channel_id=1, source_target_pairs={{1,0},{2,1},{3,2},{4,3},{5,4},{6,5},{7,6},{8,7},{9,8},{10,9},{11,1... | collective-permute-start | bytes 393224 | tf_op jit(solution)/shard_map/ppermute | solution.py:22
  45.9 14.4 %collective-permute-start.10 = (bf16[128,512]{1,0:T(8,128)(2,1)S(1)}, bf16[128,512]{1,0:T(8,128)(2,1)S(1)}, u32[]{:S(2)}, u32[]{:S(2)}) collective-permute-start(bf16[128,512]{1,0:T(8,128)(2,1)S(1)} %bitcast.395), channel_id=1, source_target_pairs={{2,0},{3,1},{4,2},{5,3},{6,4},{7,5},{8,6},{9,7},{10,8},{11,9},{12,... | collective-permute-start | bytes 393224 | tf_op jit(solution)/shard_map/ppermute | solution.py:22
  54.8 7.8 %collective-permute-start.11 = (bf16[128,512]{1,0:T(8,128)(2,1)S(1)}, bf16[128,512]{1,0:T(8,128)(2,1)S(1)}, u32[]{:S(2)}, u32[]{:S(2)}) collective-permute-start(bf16[128,512]{1,0:T(8,128)(2,1)S(1)} %bitcast.396), channel_id=1, source_target_pairs={{3,0},{4,1},{5,2},{6,3},{7,4},{8,5},{9,6},{10,7},{11,8},{12,9},{13... | collective-permute-start | bytes 393224 | tf_op jit(solution)/shard_map/ppermute | solution.py:22
  57.3 28.7 %collective-permute-start.12 = (bf16[1,128,4096]{1,2,0:T(8,128)(2,1)S(1)}, bf16[1,128,4096]{1,2,0:T(8,128)(2,1)S(1)}, u32[]{:S(2)}, u32[]{:S(2)}) collective-permute-start(bf16[1,128,4096]{1,2,0:T(8,128)(2,1)S(1)} %copy.40), channel_id=1, source_target_pairs={{0,480},{32,0},{64,32},{96,64},{128,96},{160,128},{192,160},{224,1... | collective-permute-start | bytes 3145736 | tf_op jit(solution)/shard_map/ppermute | solution.py:16
  118.2 2.5 %copy-start.8 = (bf16[7,128,128]{1,2,0:T(8,128)(2,1)S(1)}, bf16[7,128,128]{1,2,0:T(8,128)(2,1)}, u32[]{:S(2)}) copy-start(bf16[7,128,128]{1,2,0:T(8,128)(2,1)} %fusion.49) | copy-start | bytes 688132
  121.7 29.9 %collective-permute-start.19 = (bf16[128,512]{0,1:T(8,128)(2,1)}, bf16[128,512]{0,1:T(8,128)(2,1)}, u32[]{:S(2)}, u32[]{:S(2)}) collective-permute-start(bf16[128,512]{0,1:T(8,128)(2,1)} %get-tuple-element.26), channel_id=1, source_target_pairs={{3,0},{4,1},{5,2},{6,3},{7,4},{8,5},{9,6},{10,7},{11,8},{12,9},{13... | collective-permute-start | bytes 393224 | tf_op jit(solution)/shard_map/ppermute | solution.py:22
  134.2 19.6 %collective-permute-start.20 = (bf16[128,512]{0,1:T(8,128)(2,1)}, bf16[128,512]{0,1:T(8,128)(2,1)}, u32[]{:S(2)}, u32[]{:S(2)}) collective-permute-start(bf16[128,512]{0,1:T(8,128)(2,1)} %get-tuple-element.31), channel_id=1, source_target_pairs={{2,0},{3,1},{4,2},{5,3},{6,4},{7,5},{8,6},{9,7},{10,8},{11,9},{12,... | collective-permute-start | bytes 393224 | tf_op jit(solution)/shard_map/ppermute | solution.py:22
  136.2 26.4 %collective-permute-start.21 = (bf16[128,512]{0,1:T(8,128)(2,1)}, bf16[128,512]{0,1:T(8,128)(2,1)}, u32[]{:S(2)}, u32[]{:S(2)}) collective-permute-start(bf16[128,512]{0,1:T(8,128)(2,1)} %get-tuple-element.30), channel_id=1, source_target_pairs={{1,0},{2,1},{3,2},{4,3},{5,4},{6,5},{7,6},{8,7},{9,8},{10,9},{11,1... | collective-permute-start | bytes 393224 | tf_op jit(solution)/shard_map/ppermute | solution.py:22
  138.5 26.1 %collective-permute-start.22 = (bf16[128,512]{0,1:T(8,128)(2,1)}, bf16[128,512]{0,1:T(8,128)(2,1)}, u32[]{:S(2)}, u32[]{:S(2)}) collective-permute-start(bf16[128,512]{0,1:T(8,128)(2,1)} %get-tuple-element.29), channel_id=1, source_target_pairs={{0,1},{1,2},{2,3},{3,4},{4,5},{5,6},{6,7},{7,8},{8,9},{9,10},{10,1... | collective-permute-start | bytes 393224 | tf_op jit(solution)/shard_map/ppermute | solution.py:22
  141.9 25.7 %collective-permute-start.23 = (bf16[128,512]{0,1:T(8,128)(2,1)}, bf16[128,512]{0,1:T(8,128)(2,1)}, u32[]{:S(2)}, u32[]{:S(2)}) collective-permute-start(bf16[128,512]{0,1:T(8,128)(2,1)} %get-tuple-element.28), channel_id=1, source_target_pairs={{0,2},{1,3},{2,4},{3,5},{4,6},{5,7},{6,8},{7,9},{8,10},{9,11},{10,... | collective-permute-start | bytes 393224 | tf_op jit(solution)/shard_map/ppermute | solution.py:22
  146.1 15.2 %copy-start.1 = (f32[1,128,1024]{2,1,0:T(8,128)S(1)}, f32[1,128,1024]{2,1,0:T(8,128)}, u32[]{:S(2)}) copy-start(f32[1,128,1024]{2,1,0:T(8,128)} %copy.56) | copy-start | bytes 1572868
  147.1 14.2 %copy-start.2 = (f32[1,128,1024]{2,1,0:T(8,128)S(1)}, f32[1,128,1024]{2,1,0:T(8,128)}, u32[]{:S(2)}) copy-start(f32[1,128,1024]{2,1,0:T(8,128)} %copy.57) | copy-start | bytes 1572868
  149.1 12.3 %copy-start.3 = (f32[1,128,1024]{2,1,0:T(8,128)S(1)}, f32[1,128,1024]{2,1,0:T(8,128)}, u32[]{:S(2)}) copy-start(f32[1,128,1024]{2,1,0:T(8,128)} %copy.58) | copy-start | bytes 1572868
  149.1 12.3 %copy-start.4 = (f32[1,128,1024]{2,1,0:T(8,128)S(1)}, f32[1,128,1024]{2,1,0:T(8,128)}, u32[]{:S(2)}) copy-start(f32[1,128,1024]{2,1,0:T(8,128)} %copy.59) | copy-start | bytes 1572868
  151.5 18.7 %collective-permute-start.24 = (bf16[128,512]{0,1:T(8,128)(2,1)S(1)}, bf16[128,512]{0,1:T(8,128)(2,1)S(1)}, u32[]{:S(2)}, u32[]{:S(2)}) collective-permute-start(bf16[128,512]{0,1:T(8,128)(2,1)S(1)} %get-tuple-element.27), channel_id=1, source_target_pairs={{0,3},{1,4},{2,5},{3,6},{4,7},{5,8},{6,9},{7,10},{8,11},{9,12},{10... | collective-permute-start | bytes 393224 | tf_op jit(solution)/shard_map/ppermute | solution.py:22
  153.8 19.6 %collective-permute-start.13 = (bf16[128,512]{0,1:T(8,128)(2,1)S(1)}, bf16[128,512]{0,1:T(8,128)(2,1)S(1)}, u32[]{:S(2)}, u32[]{:S(2)}) collective-permute-start(bf16[128,512]{0,1:T(8,128)(2,1)S(1)} %get-tuple-element.32), channel_id=1, source_target_pairs={{3,0},{4,1},{5,2},{6,3},{7,4},{8,5},{9,6},{10,7},{11,8},{12,9},{13... | collective-permute-start | bytes 393224 | tf_op jit(solution)/shard_map/ppermute | solution.py:22
  162.5 15.3 %collective-permute-start.14 = (bf16[128,512]{0,1:T(8,128)(2,1)}, bf16[128,512]{0,1:T(8,128)(2,1)S(1)}, u32[]{:S(2)}, u32[]{:S(2)}) collective-permute-start(bf16[128,512]{0,1:T(8,128)(2,1)} %get-tuple-element.37), channel_id=1, source_target_pairs={{2,0},{3,1},{4,2},{5,3},{6,4},{7,5},{8,6},{9,7},{10,8},{11,9},{12,... | collective-permute-start | bytes 393224 | tf_op jit(solution)/shard_map/ppermute | solution.py:22
  164.6 13.2 %collective-permute-start.15 = (bf16[128,512]{0,1:T(8,128)(2,1)S(1)}, bf16[128,512]{0,1:T(8,128)(2,1)S(1)}, u32[]{:S(2)}, u32[]{:S(2)}) collective-permute-start(bf16[128,512]{0,1:T(8,128)(2,1)S(1)} %get-tuple-element.36), channel_id=1, source_target_pairs={{1,0},{2,1},{3,2},{4,3},{5,4},{6,5},{7,6},{8,7},{9,8},{10,9},{11,1... | collective-permute-start | bytes 393224 | tf_op jit(solution)/shard_map/ppermute | solution.py:22
  167.6 10.2 %collective-permute-start.16 = (bf16[128,512]{0,1:T(8,128)(2,1)S(1)}, bf16[128,512]{0,1:T(8,128)(2,1)S(1)}, u32[]{:S(2)}, u32[]{:S(2)}) collective-permute-start(bf16[128,512]{0,1:T(8,128)(2,1)S(1)} %get-tuple-element.35), channel_id=1, source_target_pairs={{0,1},{1,2},{2,3},{3,4},{4,5},{5,6},{6,7},{7,8},{8,9},{9,10},{10,1... | collective-permute-start | bytes 393224 | tf_op jit(solution)/shard_map/ppermute | solution.py:22
  170.2 11.3 %collective-permute-start.17 = (bf16[128,512]{0,1:T(8,128)(2,1)S(1)}, bf16[128,512]{0,1:T(8,128)(2,1)S(1)}, u32[]{:S(2)}, u32[]{:S(2)}) collective-permute-start(bf16[128,512]{0,1:T(8,128)(2,1)S(1)} %get-tuple-element.34), channel_id=1, source_target_pairs={{0,2},{1,3},{2,4},{3,5},{4,6},{5,7},{6,8},{7,9},{8,10},{9,11},{10,... | collective-permute-start | bytes 393224 | tf_op jit(solution)/shard_map/ppermute | solution.py:22
  173.5 13.6 %collective-permute-start.18 = (bf16[128,512]{0,1:T(8,128)(2,1)S(1)}, bf16[128,512]{0,1:T(8,128)(2,1)S(1)}, u32[]{:S(2)}, u32[]{:S(2)}) collective-permute-start(bf16[128,512]{0,1:T(8,128)(2,1)S(1)} %get-tuple-element.33), channel_id=1, source_target_pairs={{0,3},{1,4},{2,5},{3,6},{4,7},{5,8},{6,9},{7,10},{8,11},{9,12},{10... | collective-permute-start | bytes 393224 | tf_op jit(solution)/shard_map/ppermute | solution.py:22
  (5 other events, 12.2 us)
where the time goes:
time: 190 us; the launch traced here: 189 us
  starting transfers between devices  91.8 us (48%)
  waiting for transfers between devices  32.9 us (17%)
  matrix products  29.3 us (15%)
  local copies, waits for them, and re-layouts  15.9 us (8%)
  other arithmetic  13.8 us (7%)
  between operations  5.26 us (3%)
    ppermute x24, starting transfers between devices, from_behind(): lax.ppermute(value, axis, [(source, source + steps) for source in range(l...  88.8 us
    ppermute x1, waiting for transfers between devices, passed_along(): return lax.ppermute(x, axis, [(i, (i + by) % peers) for i in range(peers)])  21.3 us
    dot_general x4, matrix products, shards(): jnp.einsum('qgd,jkd->gqjk', g_group, v_group, preferred_element_type=jnp....  11.6 us
    ppermute x24, waiting for transfers between devices, from_behind(): lax.ppermute(value, axis, [(source, source + steps) for source in range(l...  11.5 us
    unnamed x40, local copies, waits for them, and re-layouts  8.57 us
    dot_general x4, matrix products, shards(): jnp.einsum('gqjk,qgd->jkd', probs_b.reshape(groups, block_len, window_len...  7.33 us
    convert_element_type x2, other arithmetic, shards(): dscore = (probs * (grad_probs - row_delta)).astype(jnp.bfloat16)  7 us
    dot_general x4, matrix products, shards(): jnp.einsum('gqjk,qgd->jkd', dscore.reshape(groups, block_len, window_len,...  5.93 us
  transfers between devices with their start and end apart: 25, of which 4 were waited for; matrix products, arithmetic and copies ran while one was open for 11% of the time, Pallas kernels for 0%

commit v1 on v0

v1 whole, which is shorter than its diff:
```python
import functools
import math

import jax
import jax.numpy as jnp
from jax import lax
from jax.experimental import pallas as pl
from jax.experimental.pallas import tpu as pltpu
from jax.sharding import PartitionSpec as P

HQ, HK, HD, W = 32, 4, 128, 3
BL = 128
G = HQ // HK
NS = 7
SCALE = 1.0 / math.sqrt(HD)
LOG2E = 1.4426950408889634

NT = (((1,), (1,)), ((), ()))
NN = (((1,), (0,)), ((), ()))


def body(flags, q, g, own_k, own_v, left, right, far, mate, dq, parts, to_mate, to_far, kc, vc, kt, pairs=4):
    lw = G * BL // pairs
    kc[0:128] = own_k[...]
    vc[0:128] = own_v[...]
    for s, ref in ((1, left), (2, right), (3, far)):
        kc[s * BL:(s + 1) * BL] = ref[0]
        vc[s * BL:(s + 1) * BL] = ref[1]
    kc[4 * BL:] = mate[0]
    vc[4 * BL:] = mate[1]
    for s in range(NS):
        kt[:, s * BL:(s + 1) * BL] = kc[s * BL:(s + 1) * BL, :].T
    dk = dv = None
    for t in range(pairs):
        n = lw // HD
        cols = [slice((t * n + i) * HD, (t * n + i + 1) * HD) for i in range(n)]
        qp = jnp.concatenate([q[:, c] for c in cols], axis=0)
        gp = jnp.concatenate([g[:, c] for c in cols], axis=0)
        s = lax.dot_general(kc[...], qp, NT, preferred_element_type=jnp.float32)
        s = jnp.concatenate([jnp.where(flags[i] != 0, s[i * BL:(i + 1) * BL], -jnp.inf) for i in range(NS)], axis=0)
        m = jnp.max(s, axis=0, keepdims=True)
        e = jnp.exp2((s - m) * (SCALE * LOG2E))
        inv = 1.0 / jnp.sum(e, axis=0, keepdims=True)
        p = e * inv
        dp = lax.dot_general(vc[...], gp, NT, preferred_element_type=jnp.float32)
        delta = jnp.sum(p * dp, axis=0, keepdims=True)
        ds = (p * (dp - delta)).astype(jnp.bfloat16)
        pb = p.astype(jnp.bfloat16)
        a = lax.dot_general(pb, gp, NN, preferred_element_type=jnp.float32)
        b = lax.dot_general(ds, qp, NN, preferred_element_type=jnp.float32)
        dv = a if dv is None else dv + a
        dk = b if dk is None else dk + b
        dqt = lax.dot_general(kt[...], ds, NN, preferred_element_type=jnp.float32)
        for i, c in enumerate(cols):
            dq[:, c] = (dqt[:, i * BL:(i + 1) * BL].T * SCALE).astype(jnp.bfloat16)
    dk = dk * SCALE
    parts[0] = dk[:3 * BL]
    parts[1] = dv[:3 * BL]
    to_far[0] = dk[3 * BL:4 * BL].astype(jnp.bfloat16)
    to_far[1] = dv[3 * BL:4 * BL].astype(jnp.bfloat16)
    to_mate[0] = dk[4 * BL:].astype(jnp.bfloat16)
    to_mate[1] = dv[4 * BL:].astype(jnp.bfloat16)


def attn(flags, q, g, k, v, left, right, far, mate, pairs=4):
    b16 = jnp.bfloat16
    col = lambda h: (0, h)
    col3 = lambda h: (0, 0, h)
    return pl.pallas_call(
        functools.partial(body, pairs=pairs),
        grid=(HK,),
        in_specs=[
            pl.BlockSpec(memory_space=pltpu.SMEM),
            pl.BlockSpec((BL, G * HD), col),
            pl.BlockSpec((BL, G * HD), col),
            pl.BlockSpec((BL, HD), col),
            pl.BlockSpec((BL, HD), col),
            pl.BlockSpec((2, BL, HD), col3),
            pl.BlockSpec((2, BL, HD), col3),
            pl.BlockSpec((2, BL, HD), col3),
            pl.BlockSpec((2, 3 * BL, HD), col3),
        ],
        out_specs=[
            pl.BlockSpec((BL, G * HD), col),
            pl.BlockSpec((2, 3 * BL, HD), col3),
            pl.BlockSpec((2, 3 * BL, HD), col3),
            pl.BlockSpec((2, BL, HD), col3),
        ],
        out_shape=[
            jax.ShapeDtypeStruct((BL, HQ * HD), b16),
            jax.ShapeDtypeStruct((2, 3 * BL, HK * HD), jnp.float32),
            jax.ShapeDtypeStruct((2, 3 * BL, HK * HD), b16),
            jax.ShapeDtypeStruct((2, BL, HK * HD), b16),
        ],
        scratch_shapes=[
            pltpu.VMEM((NS * BL, HD), b16),
            pltpu.VMEM((NS * BL, HD), b16),
            pltpu.VMEM((HD, NS * BL), b16),
        ],
        compiler_params=pltpu.CompilerParams(vmem_limit_bytes=40 << 20),
        name="attention_backward",
    )(flags, q, g, k, v, left, right, far, mate)


def shift_pairs(count, by):
    return [(i, i + by) for i in range(count) if 0 <= i + by < count]


def mate_pairs(count):
    return [(i, i ^ 1) for i in range(count)]


def far_pairs(count):
    return [(i, i + (3 if i % 2 else -3)) for i in range(count) if 0 <= i + (3 if i % 2 else -3) < count]


def slot_flags(mask_row, index, count):
    odd = index % 2
    sign = 1 - 2 * odd
    offsets = [0, -2, 2, -3 * sign, sign, sign - 2, sign + 2]
    flags = [jnp.int32(1)]
    for offset in offsets[1:]:
        inside = (index + offset >= 0) & (index + offset < count)
        on = jnp.sum(jnp.where(jnp.arange(2 * W + 1) == offset + W, mask_row, 0)) == 1
        flags.append((inside & on).astype(jnp.int32))
    return jnp.stack(flags)


def shards(query_heads, key_heads, value_heads, section_cotangent, block_mask):
    sections = lax.axis_size("section")
    count = lax.axis_size("seq")
    index = lax.axis_index("seq")
    grad_out = lax.ppermute(
        section_cotangent, "section", [(i, (i - 1) % sections) for i in range(sections)]
    )
    own = jnp.stack([key_heads[0], value_heads[0]])
    left = lax.ppermute(own, "seq", shift_pairs(count, 2))
    right = lax.ppermute(own, "seq", shift_pairs(count, -2))
    far = lax.ppermute(own, "seq", far_pairs(count))
    mate = lax.ppermute(jnp.concatenate([own, left, right], axis=1), "seq", mate_pairs(count))
    flags = slot_flags(block_mask[0], index, count)
    query_grad, parts, to_mate, to_far = attn(
        flags, query_heads[0], grad_out[0], key_heads[0], value_heads[0], left, right, far, mate, pairs=1
    )
    from_mate = lax.ppermute(to_mate, "seq", mate_pairs(count))
    sums = parts + from_mate.astype(jnp.float32)
    back_left = lax.ppermute(sums[:, BL : 2 * BL].astype(jnp.bfloat16), "seq", shift_pairs(count, -2))
    back_right = lax.ppermute(sums[:, 2 * BL :].astype(jnp.bfloat16), "seq", shift_pairs(count, 2))
    back_far = lax.ppermute(to_far, "seq", far_pairs(count))
    total = sums[:, :BL]
    for arrived in (back_left, back_right, back_far):
        total = total + arrived.astype(jnp.float32)
    total = total.astype(jnp.bfloat16)
    return query_grad[None], total[0][None], total[1][None]


def solution(mesh):
    in_specs = (
        P("section", "seq", None),
        P("section", "seq", None),
        P("section", "seq", None),
        P("section", "seq", None),
        P("seq", None),
    )
    out_specs = (P("section", "seq", None), P("section", "seq", None), P("section", "seq", None))
    return jax.shard_map(shards, mesh=mesh, in_specs=in_specs, out_specs=out_specs, check_vma=False)
```

time: 190 us -> 113 us (0.59)
  the two profiles are of different devices: /device:TPU:377 before, /device:TPU:376 now
where the time goes in v1:
time: 113 us; the launch traced here: 112 us
  waiting for transfers between devices  52.4 us (46%)
  starting transfers between devices  30.7 us (27%)
  Pallas kernels  16.3 us (14%)
  local copies, waits for them, and re-layouts  4.99 us (4%)
  between operations  4.54 us (4%)
  other arithmetic  3.07 us (3%)
    ppermute x1, waiting for transfers between devices, shards(): right = lax.ppermute(own, 'seq', shift_pairs(count, -2))  28.7 us
    pallas_call x1, Pallas kernels, attn(): pl.pallas_call(functools.partial(body, pairs=pairs), grid=(HK,), in_specs...  16.3 us
    ppermute x1, starting transfers between devices, shards(): lax.ppermute(sums[:, BL:2 * BL].astype(jnp.bfloat16), 'seq', shift_pairs(...  11.4 us
    ppermute x1, waiting for transfers between devices, shards(): lax.ppermute(sums[:, BL:2 * BL].astype(jnp.bfloat16), 'seq', shift_pairs(...  10 us
    ppermute x1, waiting for transfers between devices, shards(): lax.ppermute(sums[:, 2 * BL:].astype(jnp.bfloat16), 'seq', shift_pairs(co...  7.53 us
    ppermute x1, waiting for transfers between devices, shards(): far = lax.ppermute(own, 'seq', far_pairs(count))  6.08 us
    ppermute x1, starting transfers between devices, shards(): right = lax.ppermute(own, 'seq', shift_pairs(count, -2))  3.73 us
    ppermute x1, starting transfers between devices, shards(): lax.ppermute(section_cotangent, 'section', [(i, (i - 1) % sections) for i...  3.26 us
  transfers between devices with their start and end apart: 9, of which 5 were waited for; matrix products, arithmetic and copies ran while one was open for 3% of the time, Pallas kernels for 0%

profile of v1, /device:TPU:376, one launch (start us, length us, event | category | flops | bytes accessed | tf_op | source)
XLA Modules:
  0.0 112.0 jit_solution(2155337448872486349)
XLA Ops:
  0.6 0.0 copy-start.1
  0.6 0.0 copy-start.3
  0.7 1.7 %constant_dynamic-update-slice_fusion.1 = bf16[2,128,512]{2,1,0:T(8,128)(2,1)} fusion(bf16[1,128,512]{2,1,0:T(8,128)(2,1)} %param.6), kind=kLoop, calls=%fused_computation.7 | loop fusion | bytes 262144
  2.3 1.6 %constant_dynamic-update-slice_fusion = bf16[2,128,512]{2,1,0:T(8,128)(2,1)} fusion(bf16[2,128,512]{2,1,0:T(8,128)(2,1)} %constant_dynamic-update-slice_fusion.1, bf16[1,128,512]{2,1,0:T(8,128)(2,1)} %param.7), kind=kLoop, calls=%fused_computation.6 | loop fusion | bytes 262144 | tf_op jit(solution)/shard_map/stack | solution.py:136
  3.9 3.7 %collective-permute-start.2 = (bf16[2,128,512]{2,1,0:T(8,128)(2,1)}, bf16[2,128,512]{2,1,0:T(8,128)(2,1)S(1)}, u32[]{:S(2)}, u32[]{:S(2)}) collective-permute-start(bf16[2,128,512]{2,1,0:T(8,128)(2,1)} %constant_dynamic-update-slice_fusion), channel_id=1, source_target_pairs={{2,0},{3,1},{4,2},{5,3},{6,4},{7,5},{8,6},{9,7},{10,8},{11,9},{12,... | collective-permute-start | bytes 786440 | tf_op jit(solution)/shard_map/ppermute | solution.py:138
  7.6 2.1 %collective-permute-start.1 = (bf16[2,128,512]{2,1,0:T(8,128)(2,1)}, bf16[2,128,512]{2,1,0:T(8,128)(2,1)S(1)}, u32[]{:S(2)}, u32[]{:S(2)}) collective-permute-start(bf16[2,128,512]{2,1,0:T(8,128)(2,1)} %constant_dynamic-update-slice_fusion), channel_id=1, source_target_pairs={{0,2},{1,3},{2,4},{3,5},{4,6},{5,7},{6,8},{7,9},{8,10},{9,11},{10,... | collective-permute-start | bytes 786440 | tf_op jit(solution)/shard_map/ppermute | solution.py:137
  9.7 3.3 %collective-permute-start = (bf16[1,128,4096]{2,1,0:T(8,128)(2,1)}, bf16[1,128,4096]{2,1,0:T(8,128)(2,1)S(1)}, u32[]{:S(2)}, u32[]{:S(2)}) collective-permute-start(bf16[1,128,4096]{2,1,0:T(8,128)(2,1)} %param.8), channel_id=1, source_target_pairs={{0,480},{32,0},{64,32},{96,64},{128,96},{160,128},{192,160},{224,1... | collective-permute-start | bytes 3145736 | tf_op jit(solution)/shard_map/ppermute | solution.py:133
  13.0 28.7 %collective-permute-done.2.right = bf16[2,128,512]{2,1,0:T(8,128)(2,1)S(1)} collective-permute-done((bf16[2,128,512]{2,1,0:T(8,128)(2,1)}, bf16[2,128,512]{2,1,0:T(8,128)(2,1)S(1)}, u32[]{:S(2)}, u32[]{:S(2)}) %collective-permute-start.2) | collective-permute-done | bytes 262176 | tf_op jit(solution)/shard_map/ppermute | solution.py:138
  41.6 0.0 collective-permute-done.1.left
  41.6 1.9 %pad_maximum_fusion = bf16[2,384,512]{2,1,0:T(8,128)(2,1)} fusion(bf16[2,128,512]{2,1,0:T(8,128)(2,1)S(1)} %collective-permute-done.2.right, bf16[2,128,512]{2,1,0:T(8,128)(2,1)S(1)} %collective-permute-done.1.left, bf16[2,128,512]{2,1,0:T(8,128)(2,1)} %constant_dynamic-update-slice_fusion), kind=kLoop, calls=%fused_computation.1 | loop fusion | flops 2359296 | bytes 1572864 | tf_op jit(solution)/shard_map/concatenate | solution.py:140
  43.5 1.9 %collective-permute-start.4 = (bf16[2,384,512]{2,1,0:T(8,128)(2,1)}, bf16[2,384,512]{2,1,0:T(8,128)(2,1)S(1)}, u32[]{:S(2)}, u32[]{:S(2)}) collective-permute-start(bf16[2,384,512]{2,1,0:T(8,128)(2,1)} %pad_maximum_fusion), channel_id=1, source_target_pairs={{0,1},{1,0},{2,3},{3,2},{4,5},{5,4},{6,7},{7,6},{8,9},{9,8},{10,11... | collective-permute-start | bytes 2359304 | tf_op jit(solution)/shard_map/ppermute | solution.py:140
  45.4 1.9 %collective-permute-start.3 = (bf16[2,128,512]{2,1,0:T(8,128)(2,1)}, bf16[2,128,512]{2,1,0:T(8,128)(2,1)}, u32[]{:S(2)}, u32[]{:S(2)}) collective-permute-start(bf16[2,128,512]{2,1,0:T(8,128)(2,1)} %constant_dynamic-update-slice_fusion), channel_id=1, source_target_pairs={{1,4},{3,6},{4,1},{5,8},{6,3},{7,10},{8,5},{9,12},{10,7},{11,14},{... | collective-permute-start | bytes 786440 | tf_op jit(solution)/shard_map/ppermute | solution.py:139
  47.4 0.0 copy-done.3
  47.4 0.7 fusion.8
  51.9 0.1 stack.38
  52.0 6.1 %collective-permute-done.3.far = bf16[2,128,512]{2,1,0:T(8,128)(2,1)} collective-permute-done((bf16[2,128,512]{2,1,0:T(8,128)(2,1)}, bf16[2,128,512]{2,1,0:T(8,128)(2,1)}, u32[]{:S(2)}, u32[]{:S(2)}) %collective-permute-start.3) | collective-permute-done | bytes 262176 | tf_op jit(solution)/shard_map/ppermute | solution.py:139
  58.1 0.0 collective-permute-done.4.mate
  58.1 0.0 collective-permute-done
  58.1 0.0 copy-start.2
  58.1 0.9 copy-done.2
  59.0 16.3 %attention_backward.1 = (bf16[128,4096]{1,0:T(8,128)(2,1)}, f32[2,384,512]{2,1,0:T(8,128)S(1)}, bf16[2,384,512]{2,1,0:T(8,128)(2,1)S(1)}, bf16[2,128,512]{2,1,0:T(8,128)(2,1)S(1)}) custom-call(s32[7]{0:T(128)S(1)} %stack.39.flags, bf16[128,4096]{1,0:T(8,128)(2,1)S(1)} %bitcast.18, bf16[128,4096]{1,0:T(8,128)(2,1)S(1)} %bitcast.19, ...), custom_call_target="tpu_custom_call" | custom-call | tf_op jit(solution)/shard_map/attention_backward/pallas_call | solution.py:69
  75.3 2.1 %collective-permute-start.5 = (bf16[2,384,512]{2,1,0:T(8,128)(2,1)S(1)}, bf16[2,384,512]{2,1,0:T(8,128)(2,1)S(1)}, u32[]{:S(2)}, u32[]{:S(2)}) collective-permute-start(bf16[2,384,512]{2,1,0:T(8,128)(2,1)S(1)} %get-tuple-element.9), channel_id=1, source_target_pairs={{0,1},{1,0},{2,3},{3,2},{4,5},{5,4},{6,7},{7,6},{8,9},{9,8},{10,11... | collective-permute-start | bytes 2359304 | tf_op jit(solution)/shard_map/ppermute | solution.py:145
  77.4 1.9 %collective-permute-start.8 = (bf16[2,128,512]{2,1,0:T(8,128)(2,1)S(1)}, bf16[2,128,512]{2,1,0:T(8,128)(2,1)S(1)}, u32[]{:S(2)}, u32[]{:S(2)}) collective-permute-start(bf16[2,128,512]{2,1,0:T(8,128)(2,1)S(1)} %get-tuple-element.10), channel_id=1, source_target_pairs={{1,4},{3,6},{4,1},{5,8},{6,3},{7,10},{8,5},{9,12},{10,7},{11,14},{... | collective-permute-start | bytes 786440 | tf_op jit(solution)/shard_map/ppermute | solution.py:149
  79.3 0.1 collective-permute-done.5
  79.4 0.3 fusion.9
  79.8 11.4 %collective-permute-start.6 = (bf16[2,128,512]{2,1,0:T(8,128)(2,1)S(1)}, bf16[2,128,512]{2,1,0:T(8,128)(2,1)S(1)}, u32[]{:S(2)}, u32[]{:S(2)}) collective-permute-start(bf16[2,128,512]{2,1,0:T(8,128)(2,1)S(1)} %get-tuple-element.19), channel_id=1, source_target_pairs={{2,0},{3,1},{4,2},{5,3},{6,4},{7,5},{8,6},{9,7},{10,8},{11,9},{12,... | collective-permute-start | bytes 786440 | tf_op jit(solution)/shard_map/ppermute | solution.py:147
  91.2 2.4 %collective-permute-start.7 = (bf16[2,128,512]{2,1,0:T(8,128)(2,1)S(1)}, bf16[2,128,512]{2,1,0:T(8,128)(2,1)S(1)}, u32[]{:S(2)}, u32[]{:S(2)}) collective-permute-start(bf16[2,128,512]{2,1,0:T(8,128)(2,1)S(1)} %get-tuple-element.20), channel_id=1, source_target_pairs={{0,2},{1,3},{2,4},{3,5},{4,6},{5,7},{6,8},{7,9},{8,10},{9,11},{10,... | collective-permute-start | bytes 786440 | tf_op jit(solution)/shard_map/ppermute | solution.py:148
  93.6 0.0 collective-permute-done.8
  93.6 10.0 %collective-permute-done.6 = bf16[2,128,512]{2,1,0:T(8,128)(2,1)S(1)} collective-permute-done((bf16[2,128,512]{2,1,0:T(8,128)(2,1)S(1)}, bf16[2,128,512]{2,1,0:T(8,128)(2,1)S(1)}, u32[]{:S(2)}, u32[]{:S(2)}) %collective-permute-start.6) | collective-permute-done | bytes 262176 | tf_op jit(solution)/shard_map/ppermute | solution.py:147
  103.6 7.5 %collective-permute-done.7 = bf16[2,128,512]{2,1,0:T(8,128)(2,1)S(1)} collective-permute-done((bf16[2,128,512]{2,1,0:T(8,128)(2,1)S(1)}, bf16[2,128,512]{2,1,0:T(8,128)(2,1)S(1)}, u32[]{:S(2)}, u32[]{:S(2)}) %collective-permute-start.7) | collective-permute-done | bytes 262176 | tf_op jit(solution)/shard_map/ppermute | solution.py:148
  111.1 0.2 fusion.2
  111.3 0.7 fusion.11
  (5 shorter events, 0.0 us)
Async XLA Ops:
  0.6 57.4 %copy-start.1 = (bf16[1,128,512]{2,1,0:T(8,128)(2,1)S(1)}, bf16[1,128,512]{2,1,0:T(8,128)(2,1)}, u32[]{:S(2)}) copy-start(bf16[1,128,512]{2,1,0:T(8,128)(2,1)} %param.6) | copy-start | bytes 393220
  0.6 46.8 %copy-start.3 = (s32[1,7]{1,0:T(1,128)S(1)}, s32[1,7]{1,0:T(1,128)}, u32[]{:S(2)}) copy-start(s32[1,7]{1,0:T(1,128)} %param.9) | copy-start | bytes 88
  0.7 57.4 %copy-start = (bf16[1,128,4096]{2,1,0:T(8,128)(2,1)S(1)}, bf16[1,128,4096]{2,1,0:T(8,128)(2,1)}, u32[]{:S(2)}) copy-start(bf16[1,128,4096]{2,1,0:T(8,128)(2,1)} %param.5) | copy-start | bytes 3145732
  3.9 37.8 %collective-permute-start.2 = (bf16[2,128,512]{2,1,0:T(8,128)(2,1)}, bf16[2,128,512]{2,1,0:T(8,128)(2,1)S(1)}, u32[]{:S(2)}, u32[]{:S(2)}) collective-permute-start(bf16[2,128,512]{2,1,0:T(8,128)(2,1)} %constant_dynamic-update-slice_fusion), channel_id=1, source_target_pairs={{2,0},{3,1},{4,2},{5,3},{6,4},{7,5},{8,6},{9,7},{10,8},{11,9},{12,... | collective-permute-start | bytes 786440 | tf_op jit(solution)/shard_map/ppermute | solution.py:138
  7.6 34.0 %collective-permute-start.1 = (bf16[2,128,512]{2,1,0:T(8,128)(2,1)}, bf16[2,128,512]{2,1,0:T(8,128)(2,1)S(1)}, u32[]{:S(2)}, u32[]{:S(2)}) collective-permute-start(bf16[2,128,512]{2,1,0:T(8,128)(2,1)} %constant_dynamic-update-slice_fusion), channel_id=1, source_target_pairs={{0,2},{1,3},{2,4},{3,5},{4,6},{5,7},{6,8},{7,9},{8,10},{9,11},{10,... | collective-permute-start | bytes 786440 | tf_op jit(solution)/shard_map/ppermute | solution.py:137
  9.7 48.4 %collective-permute-start = (bf16[1,128,4096]{2,1,0:T(8,128)(2,1)}, bf16[1,128,4096]{2,1,0:T(8,128)(2,1)S(1)}, u32[]{:S(2)}, u32[]{:S(2)}) collective-permute-start(bf16[1,128,4096]{2,1,0:T(8,128)(2,1)} %param.8), channel_id=1, source_target_pairs={{0,480},{32,0},{64,32},{96,64},{128,96},{160,128},{192,160},{224,1... | collective-permute-start | bytes 3145736 | tf_op jit(solution)/shard_map/ppermute | solution.py:133
  43.5 14.5 %collective-permute-start.4 = (bf16[2,384,512]{2,1,0:T(8,128)(2,1)}, bf16[2,384,512]{2,1,0:T(8,128)(2,1)S(1)}, u32[]{:S(2)}, u32[]{:S(2)}) collective-permute-start(bf16[2,384,512]{2,1,0:T(8,128)(2,1)} %pad_maximum_fusion), channel_id=1, source_target_pairs={{0,1},{1,0},{2,3},{3,2},{4,5},{5,4},{6,7},{7,6},{8,9},{9,8},{10,11... | collective-permute-start | bytes 2359304 | tf_op jit(solution)/shard_map/ppermute | solution.py:140
  45.4 12.6 %collective-permute-start.3 = (bf16[2,128,512]{2,1,0:T(8,128)(2,1)}, bf16[2,128,512]{2,1,0:T(8,128)(2,1)}, u32[]{:S(2)}, u32[]{:S(2)}) collective-permute-start(bf16[2,128,512]{2,1,0:T(8,128)(2,1)} %constant_dynamic-update-slice_fusion), channel_id=1, source_target_pairs={{1,4},{3,6},{4,1},{5,8},{6,3},{7,10},{8,5},{9,12},{10,7},{11,14},{... | collective-permute-start | bytes 786440 | tf_op jit(solution)/shard_map/ppermute | solution.py:139
  58.1 0.9 copy-start.2
  75.3 4.2 %collective-permute-start.5 = (bf16[2,384,512]{2,1,0:T(8,128)(2,1)S(1)}, bf16[2,384,512]{2,1,0:T(8,128)(2,1)S(1)}, u32[]{:S(2)}, u32[]{:S(2)}) collective-permute-start(bf16[2,384,512]{2,1,0:T(8,128)(2,1)S(1)} %get-tuple-element.9), channel_id=1, source_target_pairs={{0,1},{1,0},{2,3},{3,2},{4,5},{5,4},{6,7},{7,6},{8,9},{9,8},{10,11... | collective-permute-start | bytes 2359304 | tf_op jit(solution)/shard_map/ppermute | solution.py:145
  77.4 16.2 %collective-permute-start.8 = (bf16[2,128,512]{2,1,0:T(8,128)(2,1)S(1)}, bf16[2,128,512]{2,1,0:T(8,128)(2,1)S(1)}, u32[]{:S(2)}, u32[]{:S(2)}) collective-permute-start(bf16[2,128,512]{2,1,0:T(8,128)(2,1)S(1)} %get-tuple-element.10), channel_id=1, source_target_pairs={{1,4},{3,6},{4,1},{5,8},{6,3},{7,10},{8,5},{9,12},{10,7},{11,14},{... | collective-permute-start | bytes 786440 | tf_op jit(solution)/shard_map/ppermute | solution.py:149
  79.8 23.9 %collective-permute-start.6 = (bf16[2,128,512]{2,1,0:T(8,128)(2,1)S(1)}, bf16[2,128,512]{2,1,0:T(8,128)(2,1)S(1)}, u32[]{:S(2)}, u32[]{:S(2)}) collective-permute-start(bf16[2,128,512]{2,1,0:T(8,128)(2,1)S(1)} %get-tuple-element.19), channel_id=1, source_target_pairs={{2,0},{3,1},{4,2},{5,3},{6,4},{7,5},{8,6},{9,7},{10,8},{11,9},{12,... | collective-permute-start | bytes 786440 | tf_op jit(solution)/shard_map/ppermute | solution.py:147
  91.2 20.0 %collective-permute-start.7 = (bf16[2,128,512]{2,1,0:T(8,128)(2,1)S(1)}, bf16[2,128,512]{2,1,0:T(8,128)(2,1)S(1)}, u32[]{:S(2)}, u32[]{:S(2)}) collective-permute-start(bf16[2,128,512]{2,1,0:T(8,128)(2,1)S(1)} %get-tuple-element.20), channel_id=1, source_target_pairs={{0,2},{1,3},{2,4},{3,5},{4,6},{5,7},{6,8},{7,9},{8,10},{9,11},{10,... | collective-permute-start | bytes 786440 | tf_op jit(solution)/shard_map/ppermute | solution.py:148

commit v2 on v1

v2 whole, which is shorter than its diff:
```python
import functools
import math

import jax
import jax.numpy as jnp
from jax import lax
from jax.experimental import pallas as pl
from jax.experimental.pallas import tpu as pltpu
from jax.sharding import PartitionSpec as P

HQ, HK, HD, W = 32, 4, 128, 3
BL = 128
G = HQ // HK
NS = 2 * W + 1
SCALE = 1.0 / math.sqrt(HD)
LOG2E = math.log2(math.e)
NT = (((1,), (1,)), ((), ()))
NN = (((1,), (0,)), ((), ()))
F32, B16 = jnp.float32, jnp.bfloat16


def slot_offsets(odd):
    sign = 1 - 2 * odd
    return [0, -2, 2, -3 * sign, sign, sign - 2, sign + 2]


def backward_body(n_grads, n_kept, *refs):
    mask, q = refs[:2]
    grads = refs[2 : 2 + n_grads]
    own, left, right, far, mate = refs[2 + n_grads : 7 + n_grads]
    dq, parts, to_mate, to_far, kc, vc, kt = refs[7 + n_grads + n_kept :]
    index = lax.axis_index("seq")
    count = lax.axis_size("seq")
    on = [None]
    for offset in slot_offsets(index % 2)[1:]:
        inside = (index + offset >= 0) & (index + offset < count)
        on.append(inside & (mask[0, offset + W] == 1))
    row = 0
    for ref in (own, left, right, far, mate):
        n = ref.shape[1]
        kc[row : row + n] = ref[0]
        vc[row : row + n] = ref[1]
        row += n
    for s in range(NS):
        kt[:, s * BL : (s + 1) * BL] = kc[s * BL : (s + 1) * BL, :].T
    cols = [slice(i * HD, (i + 1) * HD) for i in range(G)]
    qp = jnp.concatenate([q[:, c] for c in cols], axis=0)
    gp = jnp.concatenate([grads[0][:, c] for c in cols], axis=0)
    for more in grads[1:]:
        gp = gp + jnp.concatenate([more[:, c] for c in cols], axis=0)
    s = lax.dot_general(kc[...], qp, NT, preferred_element_type=F32)
    pieces = [s[i * BL : (i + 1) * BL] for i in range(NS)]
    pieces = [p if f is None else jnp.where(f, p, -jnp.inf) for p, f in zip(pieces, on)]
    s = jnp.concatenate(pieces, axis=0)
    m = jnp.max(s, axis=0, keepdims=True)
    e = jnp.exp2((s - m) * (SCALE * LOG2E))
    p = e * (1.0 / jnp.sum(e, axis=0, keepdims=True))
    dp = lax.dot_general(vc[...], gp, NT, preferred_element_type=F32)
    delta = jnp.sum(p * dp, axis=0, keepdims=True)
    ds = (p * (dp - delta)).astype(B16)
    dv = lax.dot_general(p.astype(B16), gp, NN, preferred_element_type=F32)
    dk = lax.dot_general(ds, qp, NN, preferred_element_type=F32) * SCALE
    dqt = lax.dot_general(kt[...], ds, NN, preferred_element_type=F32)
    for i, c in enumerate(cols):
        dq[:, c] = (dqt[:, c].T * SCALE).astype(B16)
    for i, d in enumerate((dk, dv)):
        parts[i] = d[: 3 * BL]
        to_far[i] = d[3 * BL : 4 * BL].astype(B16)
        to_mate[i] = d[4 * BL :].astype(B16)


def attention_backward(mask, q, grads, slots, first, heads, kept):
    at = lambda h: (0, h + first)
    at3 = lambda h: (0, 0, h + first)
    here = lambda h: (0, h)
    width = HK * HD
    shapes = [((BL, HQ * HD), B16), ((2, 3 * BL, width), F32), ((2, 3 * BL, width), B16), ((2, BL, width), B16)]
    n_in = 2 + len(grads) + len(slots)
    return pl.pallas_call(
        functools.partial(backward_body, len(grads), len(kept)),
        grid=(heads,),
        in_specs=[pl.BlockSpec(memory_space=pltpu.SMEM), pl.BlockSpec((BL, G * HD), at)]
        + [pl.BlockSpec((BL, G * HD), here) for _ in grads]
        + [pl.BlockSpec((2, x.shape[1], HD), at3) for x in slots]
        + [pl.BlockSpec(memory_space=pl.ANY) for _ in kept],
        out_specs=[pl.BlockSpec((BL, G * HD), at)] + [pl.BlockSpec((2, s[1], HD), at3) for s, _ in shapes[1:]],
        out_shape=[jax.ShapeDtypeStruct(s, d) for s, d in shapes],
        scratch_shapes=[pltpu.VMEM((NS * BL, HD), B16), pltpu.VMEM((NS * BL, HD), B16), pltpu.VMEM((HD, NS * BL), B16)],
        input_output_aliases={n_in + i: i for i in range(len(kept))},
        compiler_params=pltpu.CompilerParams(vmem_limit_bytes=32 << 20),
        cost_estimate=pl.CostEstimate(flops=heads << 30, bytes_accessed=heads << 20, transcendentals=heads << 20),
        name="attention_backward",
    )(mask, q, *grads, *slots, *kept)


def join_body(k, v, out):
    out[0] = k[...]
    out[1] = v[...]


def join(k, v):
    return pl.pallas_call(
        join_body,
        out_shape=jax.ShapeDtypeStruct((2, *k.shape), k.dtype),
        compiler_params=pltpu.CompilerParams(vmem_limit_bytes=4 << 20),
        name="join",
    )(k, v)


def relay_body(own, left, right, bundle, onward):
    odd = lax.axis_index("seq") % 2 == 1
    for i, ref in enumerate((own, left, right)):
        bundle[:, i * BL : (i + 1) * BL] = ref[...]

    @pl.when(odd)
    def _():
        onward[...] = left[...]

    @pl.when(jnp.logical_not(odd))
    def _():
        onward[...] = right[...]


def relay(own, left, right):
    n, rows, cols = left.shape
    return pl.pallas_call(
        relay_body,
        out_shape=[
            jax.ShapeDtypeStruct((n, 3 * rows, cols), left.dtype),
            jax.ShapeDtypeStruct(left.shape, left.dtype),
        ],
        compiler_params=pltpu.CompilerParams(vmem_limit_bytes=8 << 20),
        name="relay",
    )(own, left, right)


def hold_body(x, out):
    pass


def hold(x):
    return pl.pallas_call(
        hold_body,
        in_specs=[pl.BlockSpec(memory_space=pl.ANY)],
        out_specs=pl.BlockSpec(memory_space=pl.ANY),
        out_shape=jax.ShapeDtypeStruct(x.shape, x.dtype),
        input_output_aliases={0: 0},
        compiler_params=pltpu.CompilerParams(vmem_limit_bytes=1 << 20),
        cost_estimate=pl.CostEstimate(flops=1 << 33, bytes_accessed=0, transcendentals=0),
        name="hold",
    )(x)


def shift_pairs(count, by):
    return [(i, i + by) for i in range(count) if 0 <= i + by < count]


def mate_pairs(count):
    return [(i, i ^ 1) for i in range(count)]


def edge_pairs(count):
    return [(i, j) for i in range(1, count - 1, 2) for j in (i + 1,)] + [(i + 1, i) for i in range(1, count - 1, 2)]


def shards(query_heads, key_heads, value_heads, section_cotangent, block_mask):
    sections = lax.axis_size("section")
    turn = sections // 2
    count = lax.axis_size("seq")
    odd = lax.axis_index("seq") % 2 == 1
    half = HQ * HD // 2
    cot = section_cotangent[0]
    straight = [(i, i - 1) for i in range(sections) if i % turn]
    low, high = cot[:, :half], cot[:, half:]
    grad_low = hold(lax.ppermute(low, "section", [(i, (i - 1) % sections) for i in range(sections)]))
    turned = lax.ppermute(high, "section", [(0, turn), (turn, 0)])
    own = join(key_heads[0], value_heads[0])
    left = lax.ppermute(own, "seq", shift_pairs(count, 2))
    right = lax.ppermute(own, "seq", shift_pairs(count, -2))
    grad_high = lax.ppermute(high, "section", straight)
    bundle, onward = relay(own, left, right)
    far = lax.ppermute(onward, "seq", edge_pairs(count))
    mate = lax.ppermute(bundle, "seq", mate_pairs(count))
    grad_wrap = lax.ppermute(turned, "section", [(0, turn - 1), (turn, sections - 1)])
    slots = (own, left, right, far, mate)
    kept = attention_backward(block_mask, query_heads[0], (grad_low,), slots, 0, 2, ())
    query_grad, parts, to_mate, to_far = attention_backward(
        block_mask, query_heads[0], (grad_high, grad_wrap), slots, 2, 2, kept
    )
    from_far = lax.ppermute(to_far, "seq", edge_pairs(count)).astype(F32)
    from_mate = lax.ppermute(to_mate, "seq", mate_pairs(count)).astype(F32)
    sums = parts + from_mate
    to_left = (sums[:, BL : 2 * BL] + jnp.where(odd, from_far, 0.0)).astype(B16)
    to_right = (sums[:, 2 * BL :] + jnp.where(odd, 0.0, from_far)).astype(B16)
    back_left = lax.ppermute(to_left, "seq", shift_pairs(count, -2))
    back_right = lax.ppermute(to_right, "seq", shift_pairs(count, 2))
    total = (sums[:, :BL] + back_left.astype(F32) + back_right.astype(F32)).astype(B16)
    return query_grad[None], total[0][None], total[1][None]


def solution(mesh):
    in_specs = (
        P("section", "seq", None),
        P("section", "seq", None),
        P("section", "seq", None),
        P("section", "seq", None),
        P("seq", None),
    )
    out_specs = (P("section", "seq", None), P("section", "seq", None), P("section", "seq", None))
    return jax.shard_map(shards, mesh=mesh, in_specs=in_specs, out_specs=out_specs, check_vma=False)
```

time: 113 us -> 104 us (0.920)
  the two profiles are of different devices: /device:TPU:376 before, /device:TPU:377 now
where the time goes in v2:
time: 104 us; the launch traced here: 103 us
  starting transfers between devices  45.6 us (44%)
  waiting for transfers between devices  37 us (36%)
  Pallas kernels  17.1 us (16%)
  local copies, waits for them, and re-layouts  2.08 us (2%)
    pallas_call x2, Pallas kernels, attention_backward(): pl.pallas_call(functools.partial(backward_body, len(grads), len(kept)), g...  17 us
    ppermute x1, waiting for transfers between devices, shards(): back_right = lax.ppermute(to_right, 'seq', shift_pairs(count, 2))  10.5 us
    ppermute x1, starting transfers between devices, shards(): back_left = lax.ppermute(to_left, 'seq', shift_pairs(count, -2))  9.95 us
    ppermute x1, starting transfers between devices, shards(): from_mate = lax.ppermute(to_mate, 'seq', mate_pairs(count)).astype(F32)  9.79 us
    ppermute x1, waiting for transfers between devices, shards(): right = lax.ppermute(own, 'seq', shift_pairs(count, -2))  6.81 us
    ppermute x1, starting transfers between devices, shards(): right = lax.ppermute(own, 'seq', shift_pairs(count, -2))  6.38 us
    ppermute x1, waiting for transfers between devices, shards(): from_far = lax.ppermute(to_far, 'seq', edge_pairs(count)).astype(F32)  5.49 us
    ppermute x1, waiting for transfers between devices, shards(): back_left = lax.ppermute(to_left, 'seq', shift_pairs(count, -2))  5.07 us
  transfers between devices with their start and end apart: 12, of which 6 were waited for; matrix products, arithmetic and copies ran while one was open for 0% of the time, Pallas kernels for 8%

profile of v2, /device:TPU:377, one launch (start us, length us, event | category | flops | bytes accessed | tf_op | source)
XLA Modules:
  0.0 103.1 jit_solution(7946562746292348829)
XLA Ops:
  0.7 1.3 %fusion.6 = (bf16[128,2048]{1,0:T(8,128)(2,1)S(1)}, bf16[128,2048]{1,0:T(8,128)(2,1)S(1)}) fusion(bf16[128,4096]{1,0:T(8,128)(2,1)} %bitcast.9), kind=kLoop, calls=%fused_computation.10 | loop fusion | bytes 2097152 | tf_op jit(solution)/shard_map/slice | solution.py:174
  2.0 0.7 collective-permute-start.1
  2.7 3.0 %collective-permute-start.7 = (bf16[128,2048]{1,0:T(8,128)(2,1)S(1)}, bf16[128,2048]{1,0:T(8,128)(2,1)S(1)}, u32[]{:S(2)}, u32[]{:S(2)}) collective-permute-start(bf16[128,2048]{1,0:T(8,128)(2,1)S(1)} %get-tuple-element.25), channel_id=1, source_target_pairs={{0,480},{32,0},{64,32},{96,64},{128,96},{160,128},{192,160},{224,1... | collective-permute-start | bytes 1572872 | tf_op jit(solution)/shard_map/ppermute | solution.py:175
  5.7 3.1 %collective-permute-start.3 = (bf16[2,128,512]{2,1,0:T(8,128)(2,1)S(1)}, bf16[2,128,512]{2,1,0:T(8,128)(2,1)S(1)}, u32[]{:S(2)}, u32[]{:S(2)}) collective-permute-start(bf16[2,128,512]{2,1,0:T(8,128)(2,1)S(1)} %join.1.own.refs_3_.refs_4_), channel_id=1, source_target_pairs={{0,2},{1,3},{2,4},{3,5},{4,6},{5,7},{6,8},{7,9},{8,10},{9,11},{10,... | collective-permute-start | bytes 786440 | tf_op jit(solution)/shard_map/ppermute | solution.py:178
  8.9 6.4 %collective-permute-start.4 = (bf16[2,128,512]{2,1,0:T(8,128)(2,1)S(1)}, bf16[2,128,512]{2,1,0:T(8,128)(2,1)S(1)}, u32[]{:S(2)}, u32[]{:S(2)}) collective-permute-start(bf16[2,128,512]{2,1,0:T(8,128)(2,1)S(1)} %join.1.own.refs_3_.refs_4_), channel_id=1, source_target_pairs={{2,0},{3,1},{4,2},{5,3},{6,4},{7,5},{8,6},{9,7},{10,8},{11,9},{12,... | collective-permute-start | bytes 786440 | tf_op jit(solution)/shard_map/ppermute | solution.py:179
  15.3 3.0 %collective-permute-start = (bf16[128,2048]{1,0:T(8,128)(2,1)S(1)}, bf16[128,2048]{1,0:T(8,128)(2,1)S(1)}, u32[]{:S(2)}, u32[]{:S(2)}) collective-permute-start(bf16[128,2048]{1,0:T(8,128)(2,1)S(1)} %get-tuple-element.26), channel_id=1, source_target_pairs={{32,0},{64,32},{96,64},{128,96},{160,128},{192,160},{224,192},{288... | collective-permute-start | bytes 1572872 | tf_op jit(solution)/shard_map/ppermute | solution.py:180
  18.3 4.6 %collective-permute-done.3.left.refs_4_.refs_5_ = bf16[2,128,512]{2,1,0:T(8,128)(2,1)S(1)} collective-permute-done((bf16[2,128,512]{2,1,0:T(8,128)(2,1)S(1)}, bf16[2,128,512]{2,1,0:T(8,128)(2,1)S(1)}, u32[]{:S(2)}, u32[]{:S(2)}) %collective-permute-start.3) | collective-permute-done | bytes 262176 | tf_op jit(solution)/shard_map/ppermute | solution.py:178
  22.9 6.8 %collective-permute-done.4.right.refs_5_.refs_6_ = bf16[2,128,512]{2,1,0:T(8,128)(2,1)S(1)} collective-permute-done((bf16[2,128,512]{2,1,0:T(8,128)(2,1)S(1)}, bf16[2,128,512]{2,1,0:T(8,128)(2,1)S(1)}, u32[]{:S(2)}, u32[]{:S(2)}) %collective-permute-start.4) | collective-permute-done | bytes 262176 | tf_op jit(solution)/shard_map/ppermute | solution.py:179
  29.7 0.1 relay.1
  29.8 2.5 %collective-permute-start.6 = (bf16[2,384,512]{2,1,0:T(8,128)(2,1)S(1)}, bf16[2,384,512]{2,1,0:T(8,128)(2,1)S(1)}, u32[]{:S(2)}, u32[]{:S(2)}) collective-permute-start(bf16[2,384,512]{2,1,0:T(8,128)(2,1)S(1)} %get-tuple-element.14), channel_id=1, source_target_pairs={{0,1},{1,0},{2,3},{3,2},{4,5},{5,4},{6,7},{7,6},{8,9},{9,8},{10,11... | collective-permute-start | bytes 2359304 | tf_op jit(solution)/shard_map/ppermute | solution.py:183
  32.3 0.0 copy-start.2
  32.4 0.0 copy-start.3
  32.4 2.1 %collective-permute-start.5 = (bf16[2,128,512]{2,1,0:T(8,128)(2,1)S(1)}, bf16[2,128,512]{2,1,0:T(8,128)(2,1)S(1)}, u32[]{:S(2)}, u32[]{:S(2)}) collective-permute-start(bf16[2,128,512]{2,1,0:T(8,128)(2,1)S(1)} %get-tuple-element.13), channel_id=1, source_target_pairs={{1,2},{3,4},{5,6},{7,8},{9,10},{11,12},{13,14},{15,16},{17,18},{19... | collective-permute-start | bytes 786440 | tf_op jit(solution)/shard_map/ppermute | solution.py:182
  34.4 1.3 %collective-permute-start.2 = (bf16[128,2048]{1,0:T(8,128)(2,1)S(1)}, bf16[128,2048]{1,0:T(8,128)(2,1)S(1)}, u32[]{:S(2)}, u32[]{:S(2)}) collective-permute-start(bf16[128,2048]{1,0:T(8,128)(2,1)S(1)} %collective-permute-done.1), channel_id=1, source_target_pairs={{0,224},{256,480},{1,225},{257,481},{2,226},{258,482},{3,227},{259... | collective-permute-start | bytes 1572872 | tf_op jit(solution)/shard_map/ppermute | solution.py:184
  35.7 0.0 collective-permute-done.7.x
  35.8 4.4 %collective-permute-done.5.refs_6_.refs_7_ = bf16[2,128,512]{2,1,0:T(8,128)(2,1)S(1)} collective-permute-done((bf16[2,128,512]{2,1,0:T(8,128)(2,1)S(1)}, bf16[2,128,512]{2,1,0:T(8,128)(2,1)S(1)}, u32[]{:S(2)}, u32[]{:S(2)}) %collective-permute-start.5) | collective-permute-done | bytes 262176 | tf_op jit(solution)/shard_map/ppermute | solution.py:182
  40.2 8.5 %attention_backward.2 = (bf16[128,4096]{1,0:T(8,128)(2,1)}, f32[2,384,512]{2,1,0:T(8,128)S(1)}, bf16[2,384,512]{2,1,0:T(8,128)(2,1)S(1)}, bf16[2,128,512]{2,1,0:T(8,128)(2,1)S(1)}) custom-call(s32[1,7]{1,0:T(1,128)S(1)} %copy-done.3, bf16[128,4096]{1,0:T(8,128)(2,1)S(1)} %bitcast.7, bf16[128,2048]{1,0:T(8,128)(2,1)S(1)} %hold.1.refs_2_, ...), custom_call_target="tpu_custom_call" | custom-call | flops 2147483648 | bytes 2097152 | tf_op jit(solution)/shard_map/attention_backward/pallas_call | solution.py:79
  48.7 0.0 collective-permute-done.refs_2_
  48.7 0.0 collective-permute-done.2.refs_3_
  48.7 8.5 %attention_backward.3 = (bf16[128,4096]{1,0:T(8,128)(2,1)}, f32[2,384,512]{2,1,0:T(8,128)S(1)}, bf16[2,384,512]{2,1,0:T(8,128)(2,1)S(1)}, bf16[2,128,512]{2,1,0:T(8,128)(2,1)S(1)}) custom-call(s32[1,7]{1,0:T(1,128)S(1)} %copy-done.3, bf16[128,4096]{1,0:T(8,128)(2,1)S(1)} %bitcast.8, ...), custom_call_target="tpu_custom_call", output_to_operand_aliasing={{0}: (9, {}), {1}: (10, {}), {2}: (11, {}), {3}: (12, {})} | custom-call | flops 2147483648 | bytes 2097152 | tf_op jit(solution)/shard_map/attention_backward/pallas_call | solution.py:79
  57.2 9.8 %collective-permute-start.8 = (bf16[2,384,512]{2,1,0:T(8,128)(2,1)S(1)}, bf16[2,384,512]{2,1,0:T(8,128)(2,1)S(1)}, u32[]{:S(2)}, u32[]{:S(2)}) collective-permute-start(bf16[2,384,512]{2,1,0:T(8,128)(2,1)S(1)} %get-tuple-element.21), channel_id=1, source_target_pairs={{0,1},{1,0},{2,3},{3,2},{4,5},{5,4},{6,7},{7,6},{8,9},{9,8},{10,11... | collective-permute-start | bytes 2359304 | tf_op jit(solution)/shard_map/ppermute | solution.py:191
  67.0 1.9 %collective-permute-start.9 = (bf16[2,128,512]{2,1,0:T(8,128)(2,1)S(1)}, bf16[2,128,512]{2,1,0:T(8,128)(2,1)S(1)}, u32[]{:S(2)}, u32[]{:S(2)}) collective-permute-start(bf16[2,128,512]{2,1,0:T(8,128)(2,1)S(1)} %get-tuple-element.22), channel_id=1, source_target_pairs={{1,2},{3,4},{5,6},{7,8},{9,10},{11,12},{13,14},{15,16},{17,18},{19... | collective-permute-start | bytes 786440 | tf_op jit(solution)/shard_map/ppermute | solution.py:190
  68.9 0.0 collective-permute-done.8
  68.9 0.3 convert_add_fusion
  69.2 5.5 %collective-permute-done.9 = bf16[2,128,512]{2,1,0:T(8,128)(2,1)S(1)} collective-permute-done((bf16[2,128,512]{2,1,0:T(8,128)(2,1)S(1)}, bf16[2,128,512]{2,1,0:T(8,128)(2,1)S(1)}, u32[]{:S(2)}, u32[]{:S(2)}) %collective-permute-start.9) | collective-permute-done | bytes 262176 | tf_op jit(solution)/shard_map/ppermute | solution.py:190
  74.7 0.2 fusion.1
  74.9 9.9 %collective-permute-start.10 = (bf16[2,128,512]{2,1,0:T(8,128)(2,1)S(1)}, bf16[2,128,512]{2,1,0:T(8,128)(2,1)S(1)}, u32[]{:S(2)}, u32[]{:S(2)}) collective-permute-start(bf16[2,128,512]{2,1,0:T(8,128)(2,1)S(1)} %get-tuple-element.23), channel_id=1, source_target_pairs={{2,0},{3,1},{4,2},{5,3},{6,4},{7,5},{8,6},{9,7},{10,8},{11,9},{12,... | collective-permute-start | bytes 786440 | tf_op jit(solution)/shard_map/ppermute | solution.py:195
  84.8 1.9 %collective-permute-start.11 = (bf16[2,128,512]{2,1,0:T(8,128)(2,1)S(1)}, bf16[2,128,512]{2,1,0:T(8,128)(2,1)S(1)}, u32[]{:S(2)}, u32[]{:S(2)}) collective-permute-start(bf16[2,128,512]{2,1,0:T(8,128)(2,1)S(1)} %get-tuple-element.24), channel_id=1, source_target_pairs={{0,2},{1,3},{2,4},{3,5},{4,6},{5,7},{6,8},{7,9},{8,10},{9,11},{10,... | collective-permute-start | bytes 786440 | tf_op jit(solution)/shard_map/ppermute | solution.py:196
  86.7 5.1 %collective-permute-done.10 = bf16[2,128,512]{2,1,0:T(8,128)(2,1)S(1)} collective-permute-done((bf16[2,128,512]{2,1,0:T(8,128)(2,1)S(1)}, bf16[2,128,512]{2,1,0:T(8,128)(2,1)S(1)}, u32[]{:S(2)}, u32[]{:S(2)}) %collective-permute-start.10) | collective-permute-done | bytes 262176 | tf_op jit(solution)/shard_map/ppermute | solution.py:195
  91.8 10.5 %collective-permute-done.11 = bf16[2,128,512]{2,1,0:T(8,128)(2,1)S(1)} collective-permute-done((bf16[2,128,512]{2,1,0:T(8,128)(2,1)S(1)}, bf16[2,128,512]{2,1,0:T(8,128)(2,1)S(1)}, u32[]{:S(2)}, u32[]{:S(2)}) %collective-permute-start.11) | collective-permute-done | bytes 262176 | tf_op jit(solution)/shard_map/ppermute | solution.py:196
  102.3 0.1 fusion.5
  102.4 0.7 fusion.7
  (10 shorter events, 0.0 us)
Async XLA Ops:
  0.6 5.1 %copy-start = (bf16[1,128,512]{2,1,0:T(8,128)(2,1)S(1)}, bf16[1,128,512]{2,1,0:T(8,128)(2,1)}, u32[]{:S(2)}) copy-start(bf16[1,128,512]{2,1,0:T(8,128)(2,1)} %param.6) | copy-start | bytes 393220
  0.6 5.1 %copy-start.1 = (bf16[1,128,512]{2,1,0:T(8,128)(2,1)S(1)}, bf16[1,128,512]{2,1,0:T(8,128)(2,1)}, u32[]{:S(2)}) copy-start(bf16[1,128,512]{2,1,0:T(8,128)(2,1)} %param.7) | copy-start | bytes 393220
  2.0 32.4 %collective-permute-start.1 = (bf16[128,2048]{1,0:T(8,128)(2,1)S(1)}, bf16[128,2048]{1,0:T(8,128)(2,1)S(1)}, u32[]{:S(2)}, u32[]{:S(2)}) collective-permute-start(bf16[128,2048]{1,0:T(8,128)(2,1)S(1)} %get-tuple-element.26), channel_id=1, source_target_pairs={{0,256},{256,0},{1,257},{257,1},{2,258},{258,2},{3,259},{259,3},{4... | collective-permute-start | bytes 1572872 | tf_op jit(solution)/shard_map/ppermute | solution.py:176
  2.7 33.0 %collective-permute-start.7 = (bf16[128,2048]{1,0:T(8,128)(2,1)S(1)}, bf16[128,2048]{1,0:T(8,128)(2,1)S(1)}, u32[]{:S(2)}, u32[]{:S(2)}) collective-permute-start(bf16[128,2048]{1,0:T(8,128)(2,1)S(1)} %get-tuple-element.25), channel_id=1, source_target_pairs={{0,480},{32,0},{64,32},{96,64},{128,96},{160,128},{192,160},{224,1... | collective-permute-start | bytes 1572872 | tf_op jit(solution)/shard_map/ppermute | solution.py:175
  5.7 17.2 %collective-permute-start.3 = (bf16[2,128,512]{2,1,0:T(8,128)(2,1)S(1)}, bf16[2,128,512]{2,1,0:T(8,128)(2,1)S(1)}, u32[]{:S(2)}, u32[]{:S(2)}) collective-permute-start(bf16[2,128,512]{2,1,0:T(8,128)(2,1)S(1)} %join.1.own.refs_3_.refs_4_), channel_id=1, source_target_pairs={{0,2},{1,3},{2,4},{3,5},{4,6},{5,7},{6,8},{7,9},{8,10},{9,11},{10,... | collective-permute-start | bytes 786440 | tf_op jit(solution)/shard_map/ppermute | solution.py:178
  8.9 20.9 %collective-permute-start.4 = (bf16[2,128,512]{2,1,0:T(8,128)(2,1)S(1)}, bf16[2,128,512]{2,1,0:T(8,128)(2,1)S(1)}, u32[]{:S(2)}, u32[]{:S(2)}) collective-permute-start(bf16[2,128,512]{2,1,0:T(8,128)(2,1)S(1)} %join.1.own.refs_3_.refs_4_), channel_id=1, source_target_pairs={{2,0},{3,1},{4,2},{5,3},{6,4},{7,5},{8,6},{9,7},{10,8},{11,9},{12,... | collective-permute-start | bytes 786440 | tf_op jit(solution)/shard_map/ppermute | solution.py:179
  15.3 33.4 %collective-permute-start = (bf16[128,2048]{1,0:T(8,128)(2,1)S(1)}, bf16[128,2048]{1,0:T(8,128)(2,1)S(1)}, u32[]{:S(2)}, u32[]{:S(2)}) collective-permute-start(bf16[128,2048]{1,0:T(8,128)(2,1)S(1)} %get-tuple-element.26), channel_id=1, source_target_pairs={{32,0},{64,32},{96,64},{128,96},{160,128},{192,160},{224,192},{288... | collective-permute-start | bytes 1572872 | tf_op jit(solution)/shard_map/ppermute | solution.py:180
  29.8 10.4 %collective-permute-start.6 = (bf16[2,384,512]{2,1,0:T(8,128)(2,1)S(1)}, bf16[2,384,512]{2,1,0:T(8,128)(2,1)S(1)}, u32[]{:S(2)}, u32[]{:S(2)}) collective-permute-start(bf16[2,384,512]{2,1,0:T(8,128)(2,1)S(1)} %get-tuple-element.14), channel_id=1, source_target_pairs={{0,1},{1,0},{2,3},{3,2},{4,5},{5,4},{6,7},{7,6},{8,9},{9,8},{10,11... | collective-permute-start | bytes 2359304 | tf_op jit(solution)/shard_map/ppermute | solution.py:183
  32.3 7.9 %copy-start.2 = (bf16[1,128,4096]{2,1,0:T(8,128)(2,1)S(1)}, bf16[1,128,4096]{2,1,0:T(8,128)(2,1)}, u32[]{:S(2)}) copy-start(bf16[1,128,4096]{2,1,0:T(8,128)(2,1)} %param.5) | copy-start | bytes 3145732
  32.4 7.8 %copy-start.3 = (s32[1,7]{1,0:T(1,128)S(1)}, s32[1,7]{1,0:T(1,128)}, u32[]{:S(2)}) copy-start(s32[1,7]{1,0:T(1,128)} %refs_0_.3) | copy-start | bytes 88
  32.4 7.8 %collective-permute-start.5 = (bf16[2,128,512]{2,1,0:T(8,128)(2,1)S(1)}, bf16[2,128,512]{2,1,0:T(8,128)(2,1)S(1)}, u32[]{:S(2)}, u32[]{:S(2)}) collective-permute-start(bf16[2,128,512]{2,1,0:T(8,128)(2,1)S(1)} %get-tuple-element.13), channel_id=1, source_target_pairs={{1,2},{3,4},{5,6},{7,8},{9,10},{11,12},{13,14},{15,16},{17,18},{19... | collective-permute-start | bytes 786440 | tf_op jit(solution)/shard_map/ppermute | solution.py:182
  34.4 14.3 %collective-permute-start.2 = (bf16[128,2048]{1,0:T(8,128)(2,1)S(1)}, bf16[128,2048]{1,0:T(8,128)(2,1)S(1)}, u32[]{:S(2)}, u32[]{:S(2)}) collective-permute-start(bf16[128,2048]{1,0:T(8,128)(2,1)S(1)} %collective-permute-done.1), channel_id=1, source_target_pairs={{0,224},{256,480},{1,225},{257,481},{2,226},{258,482},{3,227},{259... | collective-permute-start | bytes 1572872 | tf_op jit(solution)/shard_map/ppermute | solution.py:184
  57.2 11.7 %collective-permute-start.8 = (bf16[2,384,512]{2,1,0:T(8,128)(2,1)S(1)}, bf16[2,384,512]{2,1,0:T(8,128)(2,1)S(1)}, u32[]{:S(2)}, u32[]{:S(2)}) collective-permute-start(bf16[2,384,512]{2,1,0:T(8,128)(2,1)S(1)} %get-tuple-element.21), channel_id=1, source_target_pairs={{0,1},{1,0},{2,3},{3,2},{4,5},{5,4},{6,7},{7,6},{8,9},{9,8},{10,11... | collective-permute-start | bytes 2359304 | tf_op jit(solution)/shard_map/ppermute | solution.py:191
  67.0 7.7 %collective-permute-start.9 = (bf16[2,128,512]{2,1,0:T(8,128)(2,1)S(1)}, bf16[2,128,512]{2,1,0:T(8,128)(2,1)S(1)}, u32[]{:S(2)}, u32[]{:S(2)}) collective-permute-start(bf16[2,128,512]{2,1,0:T(8,128)(2,1)S(1)} %get-tuple-element.22), channel_id=1, source_target_pairs={{1,2},{3,4},{5,6},{7,8},{9,10},{11,12},{13,14},{15,16},{17,18},{19... | collective-permute-start | bytes 786440 | tf_op jit(solution)/shard_map/ppermute | solution.py:190
  74.9 16.9 %collective-permute-start.10 = (bf16[2,128,512]{2,1,0:T(8,128)(2,1)S(1)}, bf16[2,128,512]{2,1,0:T(8,128)(2,1)S(1)}, u32[]{:S(2)}, u32[]{:S(2)}) collective-permute-start(bf16[2,128,512]{2,1,0:T(8,128)(2,1)S(1)} %get-tuple-element.23), channel_id=1, source_target_pairs={{2,0},{3,1},{4,2},{5,3},{6,4},{7,5},{8,6},{9,7},{10,8},{11,9},{12,... | collective-permute-start | bytes 786440 | tf_op jit(solution)/shard_map/ppermute | solution.py:195
  84.8 17.5 %collective-permute-start.11 = (bf16[2,128,512]{2,1,0:T(8,128)(2,1)S(1)}, bf16[2,128,512]{2,1,0:T(8,128)(2,1)S(1)}, u32[]{:S(2)}, u32[]{:S(2)}) collective-permute-start(bf16[2,128,512]{2,1,0:T(8,128)(2,1)S(1)} %get-tuple-element.24), channel_id=1, source_target_pairs={{0,2},{1,3},{2,4},{3,5},{4,6},{5,7},{6,8},{7,9},{8,10},{9,11},{10,... | collective-permute-start | bytes 786440 | tf_op jit(solution)/shard_map/ppermute | solution.py:196

commit v3 on v2

--- a/solution.py
+++ b/solution.py
@@ -10,6 +10,7 @@
 
 HQ, HK, HD, W = 32, 4, 128, 3
 BL = 128
+ROW = 8
 G = HQ // HK
 NS = 2 * W + 1
 SCALE = 1.0 / math.sqrt(HD)
@@ -24,23 +25,33 @@
     return [0, -2, 2, -3 * sign, sign, sign - 2, sign + 2]
 
 
+def at_corner(index):
+    place = index % ROW
+    return (place == 0) | (place == ROW - 1)
+
+
 def backward_body(n_grads, n_kept, *refs):
     mask, q = refs[:2]
     grads = refs[2 : 2 + n_grads]
-    own, left, right, far, mate = refs[2 + n_grads : 7 + n_grads]
-    dq, parts, to_mate, to_far, kc, vc, kt = refs[7 + n_grads + n_kept :]
+    own, left, right, far, far_row, mate = refs[2 + n_grads : 8 + n_grads]
+    dq, parts, to_mate, to_far, kc, vc, kt = refs[8 + n_grads + n_kept :]
     index = lax.axis_index("seq")
     count = lax.axis_size("seq")
     on = [None]
     for offset in slot_offsets(index % 2)[1:]:
         inside = (index + offset >= 0) & (index + offset < count)
         on.append(inside & (mask[0, offset + W] == 1))
-    row = 0
-    for ref in (own, left, right, far, mate):
-        n = ref.shape[1]
-        kc[row : row + n] = ref[0]
-        vc[row : row + n] = ref[1]
-        row += n
+    corner = at_corner(index)
+
+    def place(ref, row):
+        kc[row : row + ref.shape[1]] = ref[0]
+        vc[row : row + ref.shape[1]] = ref[1]
+
+    for i, ref in enumerate((own, left, right)):
+        place(ref, i * BL)
+    pl.when(corner)(lambda: place(far_row, 3 * BL))
+    pl.when(jnp.logical_not(corner))(lambda: place(far, 3 * BL))
+    place(mate, 4 * BL)
     for s in range(NS):
         kt[:, s * BL : (s + 1) * BL] = kc[s * BL : (s + 1) * BL, :].T
     cols = [slice(i * HD, (i + 1) * HD) for i in range(G)]
@@ -107,48 +118,37 @@
     )(k, v)
 
 
-def relay_body(own, left, right, bundle, onward):
-    odd = lax.axis_index("seq") % 2 == 1
+def bundle_body(own, left, right, out):
     for i, ref in enumerate((own, left, right)):
-        bundle[:, i * BL : (i + 1) * BL] = ref[...]
-
-    @pl.when(odd)
-    def _():
-        onward[...] = left[...]
-
-    @pl.when(jnp.logical_not(odd))
-    def _():
-        onward[...] = right[...]
-
-
-def relay(own, left, right):
-    n, rows, cols = left.shape
-    return pl.pallas_call(
-        relay_body,
-        out_shape=[
-            jax.ShapeDtypeStruct((n, 3 * rows, cols), left.dtype),
-            jax.ShapeDtypeStruct(left.shape, left.dtype),
-        ],
+        out[:, i * BL : (i + 1) * BL] = ref[...]
+
+
+def bundle(own, left, right):
+    n, rows, cols = own.shape
+    return pl.pallas_call(
+        bundle_body,
+        out_shape=jax.ShapeDtypeStruct((n, 3 * rows, cols), own.dtype),
         compiler_params=pltpu.CompilerParams(vmem_limit_bytes=8 << 20),
-        name="relay",
+        name="bundle",
     )(own, left, right)
 
 
-def hold_body(x, out):
+def hold_body(*refs):
     pass
 
 
-def hold(x):
+def hold(*arrays):
+    anywhere = [pl.BlockSpec(memory_space=pl.ANY) for _ in arrays]
     return pl.pallas_call(
         hold_body,
-        in_specs=[pl.BlockSpec(memory_space=pl.ANY)],
-        out_specs=pl.BlockSpec(memory_space=pl.ANY),
-        out_shape=jax.ShapeDtypeStruct(x.shape, x.dtype),
-        input_output_aliases={0: 0},
+        in_specs=anywhere,
+        out_specs=anywhere,
+        out_shape=[jax.ShapeDtypeStruct(x.shape, x.dtype) for x in arrays],
+        input_output_aliases={i: i for i in range(len(arrays))},
         compiler_params=pltpu.CompilerParams(vmem_limit_bytes=1 << 20),
-        cost_estimate=pl.CostEstimate(flops=1 << 33, bytes_accessed=0, transcendentals=0),
+        cost_estimate=pl.CostEstimate(flops=1 << 34, bytes_accessed=0, transcendentals=0),
         name="hold",
-    )(x)
+    )(*arrays)
 
 
 def shift_pairs(count, by):
@@ -159,42 +159,51 @@
     return [(i, i ^ 1) for i in range(count)]
 
 
-def edge_pairs(count):
-    return [(i, j) for i in range(1, count - 1, 2) for j in (i + 1,)] + [(i + 1, i) for i in range(1, count - 1, 2)]
+def far_hops(count):
+    first, second = [], []
+    for i in range(count):
+        j = i + 3 if i % 2 else i - 3
+        if not 0 <= j < count:
+            continue
+        if j // ROW != i // ROW and j % ROW in (0, ROW - 1):
+            via = j // ROW * ROW + ROW - 1 - j % ROW
+            first.append((i, via))
+            second.append((via, j))
+        else:
+            first.append((i, j))
+    return first, second
 
 
 def shards(query_heads, key_heads, value_heads, section_cotangent, block_mask):
     sections = lax.axis_size("section")
-    turn = sections // 2
     count = lax.axis_size("seq")
-    odd = lax.axis_index("seq") % 2 == 1
+    corner = at_corner(lax.axis_index("seq"))
     half = HQ * HD // 2
     cot = section_cotangent[0]
-    straight = [(i, i - 1) for i in range(sections) if i % turn]
-    low, high = cot[:, :half], cot[:, half:]
-    grad_low = hold(lax.ppermute(low, "section", [(i, (i - 1) % sections) for i in range(sections)]))
-    turned = lax.ppermute(high, "section", [(0, turn), (turn, 0)])
+    before = [(i, (i - 1) % sections) for i in range(sections)]
+    first, second = far_hops(count)
     own = join(key_heads[0], value_heads[0])
     left = lax.ppermute(own, "seq", shift_pairs(count, 2))
     right = lax.ppermute(own, "seq", shift_pairs(count, -2))
-    grad_high = lax.ppermute(high, "section", straight)
-    bundle, onward = relay(own, left, right)
-    far = lax.ppermute(onward, "seq", edge_pairs(count))
-    mate = lax.ppermute(bundle, "seq", mate_pairs(count))
-    grad_wrap = lax.ppermute(turned, "section", [(0, turn - 1), (turn, sections - 1)])
-    slots = (own, left, right, far, mate)
+    far = lax.ppermute(own, "seq", first)
+    (grad_low,) = hold(lax.ppermute(cot[:, :half], "section", before))
+    grad_high = lax.ppermute(cot[:, half:], "section", before)
+    mate = lax.ppermute(bundle(own, left, right), "seq", mate_pairs(count))
+    far_row = lax.ppermute(far, "seq", second)
+    slots = (own, left, right, far, far_row, mate)
     kept = attention_backward(block_mask, query_heads[0], (grad_low,), slots, 0, 2, ())
     query_grad, parts, to_mate, to_far = attention_backward(
-        block_mask, query_heads[0], (grad_high, grad_wrap), slots, 2, 2, kept
+        block_mask, query_heads[0], (grad_high,), slots, 2, 2, kept
     )
-    from_far = lax.ppermute(to_far, "seq", edge_pairs(count)).astype(F32)
-    from_mate = lax.ppermute(to_mate, "seq", mate_pairs(count)).astype(F32)
-    sums = parts + from_mate
-    to_left = (sums[:, BL : 2 * BL] + jnp.where(odd, from_far, 0.0)).astype(B16)
-    to_right = (sums[:, 2 * BL :] + jnp.where(odd, 0.0, from_far)).astype(B16)
-    back_left = lax.ppermute(to_left, "seq", shift_pairs(count, -2))
-    back_right = lax.ppermute(to_right, "seq", shift_pairs(count, 2))
-    total = (sums[:, :BL] + back_left.astype(F32) + back_right.astype(F32)).astype(B16)
+    back_far = lax.ppermute(to_far, "seq", first)
+    sums = parts + lax.ppermute(to_mate, "seq", mate_pairs(count)).astype(F32)
+    back_left, back_right = hold(
+        lax.ppermute(sums[:, BL : 2 * BL].astype(B16), "seq", shift_pairs(count, -2)),
+        lax.ppermute(sums[:, 2 * BL :].astype(B16), "seq", shift_pairs(count, 2)),
+    )
+    back_row = lax.ppermute(back_far, "seq", second)
+    total = sums[:, :BL] + back_left.astype(F32) + back_right.astype(F32)
+    total = (total + jnp.where(corner, back_row, back_far).astype(F32)).astype(B16)
     return query_grad[None], total[0][None], total[1][None]
 
 

time: 104 us -> 105 us (level)
  the two profiles are of different devices: /device:TPU:377 before, /device:TPU:254 now
where the time goes in v3:
time: 105 us
  waiting for transfers between devices  43 us (41%)
  starting transfers between devices  41.1 us (39%)
  Pallas kernels  17.2 us (16%)
  local copies, waits for them, and re-layouts  2.09 us (2%)
    ppermute x1, waiting for transfers between devices, shards(): right = lax.ppermute(own, 'seq', shift_pairs(count, -2))  26 us
    pallas_call x2, Pallas kernels, attention_backward(): pl.pallas_call(functools.partial(backward_body, len(grads), len(kept)), g...  17.1 us
    ppermute x1, waiting for transfers between devices, shards(): lax.ppermute(sums[:, BL:2 * BL].astype(B16), 'seq', shift_pairs(count, -2))  10.9 us
    ppermute x1, starting transfers between devices, shards(): sums = parts + lax.ppermute(to_mate, 'seq', mate_pairs(count)).astype(F32)  9.08 us
    ppermute x1, starting transfers between devices, shards(): lax.ppermute(sums[:, 2 * BL:].astype(B16), 'seq', shift_pairs(count, 2))  7.3 us
    ppermute x1, starting transfers between devices, shards(): left = lax.ppermute(own, 'seq', shift_pairs(count, 2))  6.32 us
    ppermute x1, starting transfers between devices, shards(): grad_low, = hold(lax.ppermute(cot[:, :half], 'section', before))  3.26 us
    ppermute x1, starting transfers between devices, shards(): grad_high = lax.ppermute(cot[:, half:], 'section', before)  3.26 us
  transfers between devices with their start and end apart: 12, of which 5 were waited for; matrix products, arithmetic and copies ran while one was open for 0% of the time, Pallas kernels for 8%

profile of v3, /device:TPU:254, one launch (start us, length us, event | category | flops | bytes accessed | tf_op | source)
XLA Modules:
  0.0 104.8 jit_solution(10951621477818401295)
XLA Ops:
  0.7 1.3 %fusion.4 = (bf16[128,2048]{1,0:T(8,128)(2,1)S(1)}, bf16[128,2048]{1,0:T(8,128)(2,1)S(1)}) fusion(bf16[128,4096]{1,0:T(8,128)(2,1)} %bitcast.9), kind=kLoop, calls=%fused_computation.6 | loop fusion | bytes 2097152 | tf_op jit(solution)/shard_map/slice | solution.py:189
  2.0 3.3 %collective-permute-start.6 = (bf16[128,2048]{1,0:T(8,128)(2,1)S(1)}, bf16[128,2048]{1,0:T(8,128)(2,1)S(1)}, u32[]{:S(2)}, u32[]{:S(2)}) collective-permute-start(bf16[128,2048]{1,0:T(8,128)(2,1)S(1)} %get-tuple-element.25), channel_id=1, source_target_pairs={{0,480},{32,0},{64,32},{96,64},{128,96},{160,128},{192,160},{224,1... | collective-permute-start | bytes 1572872 | tf_op jit(solution)/shard_map/ppermute | solution.py:189
  5.3 6.3 %collective-permute-start.1 = (bf16[2,128,512]{2,1,0:T(8,128)(2,1)S(1)}, bf16[2,128,512]{2,1,0:T(8,128)(2,1)S(1)}, u32[]{:S(2)}, u32[]{:S(2)}) collective-permute-start(bf16[2,128,512]{2,1,0:T(8,128)(2,1)S(1)} %join.1.own.refs_3_), channel_id=1, source_target_pairs={{0,2},{1,3},{2,4},{3,5},{4,6},{5,7},{6,8},{7,9},{8,10},{9,11},{10,... | collective-permute-start | bytes 786440 | tf_op jit(solution)/shard_map/ppermute | solution.py:186
  11.6 1.9 %collective-permute-start.2 = (bf16[2,128,512]{2,1,0:T(8,128)(2,1)S(1)}, bf16[2,128,512]{2,1,0:T(8,128)(2,1)S(1)}, u32[]{:S(2)}, u32[]{:S(2)}) collective-permute-start(bf16[2,128,512]{2,1,0:T(8,128)(2,1)S(1)} %join.1.own.refs_3_), channel_id=1, source_target_pairs={{2,0},{3,1},{4,2},{5,3},{6,4},{7,5},{8,6},{9,7},{10,8},{11,9},{12,... | collective-permute-start | bytes 786440 | tf_op jit(solution)/shard_map/ppermute | solution.py:187
  13.5 1.9 %collective-permute-start.3 = (bf16[2,128,512]{2,1,0:T(8,128)(2,1)S(1)}, bf16[2,128,512]{2,1,0:T(8,128)(2,1)S(1)}, u32[]{:S(2)}, u32[]{:S(2)}) collective-permute-start(bf16[2,128,512]{2,1,0:T(8,128)(2,1)S(1)} %join.1.own.refs_3_), channel_id=1, source_target_pairs={{1,4},{3,6},{4,1},{5,15},{6,3},{7,10},{8,5},{9,12},{10,0},{11,14},... | collective-permute-start | bytes 786440 | tf_op jit(solution)/shard_map/ppermute | solution.py:188
  15.5 3.3 %collective-permute-start = (bf16[128,2048]{1,0:T(8,128)(2,1)S(1)}, bf16[128,2048]{1,0:T(8,128)(2,1)S(1)}, u32[]{:S(2)}, u32[]{:S(2)}) collective-permute-start(bf16[128,2048]{1,0:T(8,128)(2,1)S(1)} %get-tuple-element.26), channel_id=1, source_target_pairs={{0,480},{32,0},{64,32},{96,64},{128,96},{160,128},{192,160},{224,1... | collective-permute-start | bytes 1572872 | tf_op jit(solution)/shard_map/ppermute | solution.py:190
  18.7 3.1 %collective-permute-done.1.left.refs_4_ = bf16[2,128,512]{2,1,0:T(8,128)(2,1)S(1)} collective-permute-done((bf16[2,128,512]{2,1,0:T(8,128)(2,1)S(1)}, bf16[2,128,512]{2,1,0:T(8,128)(2,1)S(1)}, u32[]{:S(2)}, u32[]{:S(2)}) %collective-permute-start.1) | collective-permute-done | bytes 262176 | tf_op jit(solution)/shard_map/ppermute | solution.py:186
  21.8 26.0 %collective-permute-done.2.right.refs_5_ = bf16[2,128,512]{2,1,0:T(8,128)(2,1)S(1)} collective-permute-done((bf16[2,128,512]{2,1,0:T(8,128)(2,1)S(1)}, bf16[2,128,512]{2,1,0:T(8,128)(2,1)S(1)}, u32[]{:S(2)}, u32[]{:S(2)}) %collective-permute-start.2) | collective-permute-done | bytes 262176 | tf_op jit(solution)/shard_map/ppermute | solution.py:187
  47.9 0.1 bundle.1
  47.9 0.0 copy-start.2
  47.9 0.0 copy-start.3
  47.9 2.1 %collective-permute-start.5 = (bf16[2,384,512]{2,1,0:T(8,128)(2,1)S(1)}, bf16[2,384,512]{2,1,0:T(8,128)(2,1)S(1)}, u32[]{:S(2)}, u32[]{:S(2)}) collective-permute-start(bf16[2,384,512]{2,1,0:T(8,128)(2,1)S(1)} %bundle.1), channel_id=1, source_target_pairs={{0,1},{1,0},{2,3},{3,2},{4,5},{5,4},{6,7},{7,6},{8,9},{9,8},{10,11... | collective-permute-start | bytes 2359304 | tf_op jit(solution)/shard_map/ppermute | solution.py:191
  50.0 0.0 collective-permute-done.3.refs_6_
  50.0 0.7 collective-permute-start.4
  50.7 0.0 collective-permute-done.6.refs_0_
  50.7 0.0 collective-permute-done.4.refs_7_
  50.7 1.5 %collective-permute-done.5.refs_8_ = bf16[2,384,512]{2,1,0:T(8,128)(2,1)S(1)} collective-permute-done((bf16[2,384,512]{2,1,0:T(8,128)(2,1)S(1)}, bf16[2,384,512]{2,1,0:T(8,128)(2,1)S(1)}, u32[]{:S(2)}, u32[]{:S(2)}) %collective-permute-start.5) | collective-permute-done | bytes 786464 | tf_op jit(solution)/shard_map/ppermute | solution.py:191
  52.3 8.6 %attention_backward.2 = (bf16[128,4096]{1,0:T(8,128)(2,1)}, f32[2,384,512]{2,1,0:T(8,128)S(1)}, bf16[2,384,512]{2,1,0:T(8,128)(2,1)S(1)}, bf16[2,128,512]{2,1,0:T(8,128)(2,1)S(1)}) custom-call(s32[1,7]{1,0:T(1,128)S(1)} %copy-done.3, bf16[128,4096]{1,0:T(8,128)(2,1)S(1)} %bitcast.7, bf16[128,2048]{1,0:T(8,128)(2,1)S(1)} %hold.2.refs_2_, ...), custom_call_target="tpu_custom_call" | custom-call | flops 2147483648 | bytes 2097152 | tf_op jit(solution)/shard_map/attention_backward/pallas_call | solution.py:90
  60.8 0.0 collective-permute-done.refs_2_
  60.8 8.6 %attention_backward.3 = (bf16[128,4096]{1,0:T(8,128)(2,1)}, f32[2,384,512]{2,1,0:T(8,128)S(1)}, bf16[2,384,512]{2,1,0:T(8,128)(2,1)S(1)}, bf16[2,128,512]{2,1,0:T(8,128)(2,1)S(1)}) custom-call(s32[1,7]{1,0:T(1,128)S(1)} %copy-done.3, bf16[128,4096]{1,0:T(8,128)(2,1)S(1)} %bitcast.8, ...), custom_call_target="tpu_custom_call", output_to_operand_aliasing={{0}: (9, {}), {1}: (10, {}), {2}: (11, {}), {3}: (12, {})} | custom-call | flops 2147483648 | bytes 2097152 | tf_op jit(solution)/shard_map/attention_backward/pallas_call | solution.py:90
  69.4 9.1 %collective-permute-start.7 = (bf16[2,384,512]{2,1,0:T(8,128)(2,1)S(1)}, bf16[2,384,512]{2,1,0:T(8,128)(2,1)S(1)}, u32[]{:S(2)}, u32[]{:S(2)}) collective-permute-start(bf16[2,384,512]{2,1,0:T(8,128)(2,1)S(1)} %get-tuple-element.19), channel_id=1, source_target_pairs={{0,1},{1,0},{2,3},{3,2},{4,5},{5,4},{6,7},{7,6},{8,9},{9,8},{10,11... | collective-permute-start | bytes 2359304 | tf_op jit(solution)/shard_map/ppermute | solution.py:199
  78.5 1.9 %collective-permute-start.10 = (bf16[2,128,512]{2,1,0:T(8,128)(2,1)S(1)}, bf16[2,128,512]{2,1,0:T(8,128)(2,1)S(1)}, u32[]{:S(2)}, u32[]{:S(2)}) collective-permute-start(bf16[2,128,512]{2,1,0:T(8,128)(2,1)S(1)} %get-tuple-element.22), channel_id=1, source_target_pairs={{1,4},{3,6},{4,1},{5,15},{6,3},{7,10},{8,5},{9,12},{10,0},{11,14},... | collective-permute-start | bytes 786440 | tf_op jit(solution)/shard_map/ppermute | solution.py:198
  80.4 0.0 collective-permute-done.7
  80.4 0.3 fusion.3
  80.8 2.8 %collective-permute-start.8 = (bf16[2,128,512]{2,1,0:T(8,128)(2,1)S(1)}, bf16[2,128,512]{2,1,0:T(8,128)(2,1)S(1)}, u32[]{:S(2)}, u32[]{:S(2)}) collective-permute-start(bf16[2,128,512]{2,1,0:T(8,128)(2,1)S(1)} %get-tuple-element.28), channel_id=1, source_target_pairs={{2,0},{3,1},{4,2},{5,3},{6,4},{7,5},{8,6},{9,7},{10,8},{11,9},{12,... | collective-permute-start | bytes 786440 | tf_op jit(solution)/shard_map/ppermute | solution.py:201
  83.5 7.3 %collective-permute-start.9 = (bf16[2,128,512]{2,1,0:T(8,128)(2,1)S(1)}, bf16[2,128,512]{2,1,0:T(8,128)(2,1)S(1)}, u32[]{:S(2)}, u32[]{:S(2)}) collective-permute-start(bf16[2,128,512]{2,1,0:T(8,128)(2,1)S(1)} %get-tuple-element.27), channel_id=1, source_target_pairs={{0,2},{1,3},{2,4},{3,5},{4,6},{5,7},{6,8},{7,9},{8,10},{9,11},{10,... | collective-permute-start | bytes 786440 | tf_op jit(solution)/shard_map/ppermute | solution.py:202
  90.9 1.4 %collective-permute-done.10 = bf16[2,128,512]{2,1,0:T(8,128)(2,1)S(1)} collective-permute-done((bf16[2,128,512]{2,1,0:T(8,128)(2,1)S(1)}, bf16[2,128,512]{2,1,0:T(8,128)(2,1)S(1)}, u32[]{:S(2)}, u32[]{:S(2)}) %collective-permute-start.10) | collective-permute-done | bytes 262176 | tf_op jit(solution)/shard_map/ppermute | solution.py:198
  92.3 0.7 collective-permute-start.11
  92.9 10.9 %collective-permute-done.8.refs_0_ = bf16[2,128,512]{2,1,0:T(8,128)(2,1)S(1)} collective-permute-done((bf16[2,128,512]{2,1,0:T(8,128)(2,1)S(1)}, bf16[2,128,512]{2,1,0:T(8,128)(2,1)S(1)}, u32[]{:S(2)}, u32[]{:S(2)}) %collective-permute-start.8) | collective-permute-done | bytes 262176 | tf_op jit(solution)/shard_map/ppermute | solution.py:201
  103.9 0.0 collective-permute-done.11
  103.9 0.2 fusion.2
  104.1 0.7 fusion.6
  (11 shorter events, 0.1 us)
Async XLA Ops:
  0.6 4.6 %copy-start = (bf16[1,128,512]{2,1,0:T(8,128)(2,1)S(1)}, bf16[1,128,512]{2,1,0:T(8,128)(2,1)}, u32[]{:S(2)}) copy-start(bf16[1,128,512]{2,1,0:T(8,128)(2,1)} %param.6) | copy-start | bytes 393220
  0.6 4.6 %copy-start.1 = (bf16[1,128,512]{2,1,0:T(8,128)(2,1)S(1)}, bf16[1,128,512]{2,1,0:T(8,128)(2,1)}, u32[]{:S(2)}) copy-start(bf16[1,128,512]{2,1,0:T(8,128)(2,1)} %param.7) | copy-start | bytes 393220
  2.0 48.7 %collective-permute-start.6 = (bf16[128,2048]{1,0:T(8,128)(2,1)S(1)}, bf16[128,2048]{1,0:T(8,128)(2,1)S(1)}, u32[]{:S(2)}, u32[]{:S(2)}) collective-permute-start(bf16[128,2048]{1,0:T(8,128)(2,1)S(1)} %get-tuple-element.25), channel_id=1, source_target_pairs={{0,480},{32,0},{64,32},{96,64},{128,96},{160,128},{192,160},{224,1... | collective-permute-start | bytes 1572872 | tf_op jit(solution)/shard_map/ppermute | solution.py:189
  5.3 16.5 %collective-permute-start.1 = (bf16[2,128,512]{2,1,0:T(8,128)(2,1)S(1)}, bf16[2,128,512]{2,1,0:T(8,128)(2,1)S(1)}, u32[]{:S(2)}, u32[]{:S(2)}) collective-permute-start(bf16[2,128,512]{2,1,0:T(8,128)(2,1)S(1)} %join.1.own.refs_3_), channel_id=1, source_target_pairs={{0,2},{1,3},{2,4},{3,5},{4,6},{5,7},{6,8},{7,9},{8,10},{9,11},{10,... | collective-permute-start | bytes 786440 | tf_op jit(solution)/shard_map/ppermute | solution.py:186
  11.6 36.2 %collective-permute-start.2 = (bf16[2,128,512]{2,1,0:T(8,128)(2,1)S(1)}, bf16[2,128,512]{2,1,0:T(8,128)(2,1)S(1)}, u32[]{:S(2)}, u32[]{:S(2)}) collective-permute-start(bf16[2,128,512]{2,1,0:T(8,128)(2,1)S(1)} %join.1.own.refs_3_), channel_id=1, source_target_pairs={{2,0},{3,1},{4,2},{5,3},{6,4},{7,5},{8,6},{9,7},{10,8},{11,9},{12,... | collective-permute-start | bytes 786440 | tf_op jit(solution)/shard_map/ppermute | solution.py:187
  13.5 36.5 %collective-permute-start.3 = (bf16[2,128,512]{2,1,0:T(8,128)(2,1)S(1)}, bf16[2,128,512]{2,1,0:T(8,128)(2,1)S(1)}, u32[]{:S(2)}, u32[]{:S(2)}) collective-permute-start(bf16[2,128,512]{2,1,0:T(8,128)(2,1)S(1)} %join.1.own.refs_3_), channel_id=1, source_target_pairs={{1,4},{3,6},{4,1},{5,15},{6,3},{7,10},{8,5},{9,12},{10,0},{11,14},... | collective-permute-start | bytes 786440 | tf_op jit(solution)/shard_map/ppermute | solution.py:188
  15.5 45.3 %collective-permute-start = (bf16[128,2048]{1,0:T(8,128)(2,1)S(1)}, bf16[128,2048]{1,0:T(8,128)(2,1)S(1)}, u32[]{:S(2)}, u32[]{:S(2)}) collective-permute-start(bf16[128,2048]{1,0:T(8,128)(2,1)S(1)} %get-tuple-element.26), channel_id=1, source_target_pairs={{0,480},{32,0},{64,32},{96,64},{128,96},{160,128},{192,160},{224,1... | collective-permute-start | bytes 1572872 | tf_op jit(solution)/shard_map/ppermute | solution.py:190
  47.9 4.3 %copy-start.2 = (bf16[1,128,4096]{2,1,0:T(8,128)(2,1)S(1)}, bf16[1,128,4096]{2,1,0:T(8,128)(2,1)}, u32[]{:S(2)}) copy-start(bf16[1,128,4096]{2,1,0:T(8,128)(2,1)} %param.5) | copy-start | bytes 3145732
  47.9 4.3 %copy-start.3 = (s32[1,7]{1,0:T(1,128)S(1)}, s32[1,7]{1,0:T(1,128)}, u32[]{:S(2)}) copy-start(s32[1,7]{1,0:T(1,128)} %refs_0_.3) | copy-start | bytes 88
  47.9 4.3 %collective-permute-start.5 = (bf16[2,384,512]{2,1,0:T(8,128)(2,1)S(1)}, bf16[2,384,512]{2,1,0:T(8,128)(2,1)S(1)}, u32[]{:S(2)}, u32[]{:S(2)}) collective-permute-start(bf16[2,384,512]{2,1,0:T(8,128)(2,1)S(1)} %bundle.1), channel_id=1, source_target_pairs={{0,1},{1,0},{2,3},{3,2},{4,5},{5,4},{6,7},{7,6},{8,9},{9,8},{10,11... | collective-permute-start | bytes 2359304 | tf_op jit(solution)/shard_map/ppermute | solution.py:191
  50.0 0.7 collective-permute-start.4
  69.4 11.0 %collective-permute-start.7 = (bf16[2,384,512]{2,1,0:T(8,128)(2,1)S(1)}, bf16[2,384,512]{2,1,0:T(8,128)(2,1)S(1)}, u32[]{:S(2)}, u32[]{:S(2)}) collective-permute-start(bf16[2,384,512]{2,1,0:T(8,128)(2,1)S(1)} %get-tuple-element.19), channel_id=1, source_target_pairs={{0,1},{1,0},{2,3},{3,2},{4,5},{5,4},{6,7},{7,6},{8,9},{9,8},{10,11... | collective-permute-start | bytes 2359304 | tf_op jit(solution)/shard_map/ppermute | solution.py:199
  78.5 13.8 %collective-permute-start.10 = (bf16[2,128,512]{2,1,0:T(8,128)(2,1)S(1)}, bf16[2,128,512]{2,1,0:T(8,128)(2,1)S(1)}, u32[]{:S(2)}, u32[]{:S(2)}) collective-permute-start(bf16[2,128,512]{2,1,0:T(8,128)(2,1)S(1)} %get-tuple-element.22), channel_id=1, source_target_pairs={{1,4},{3,6},{4,1},{5,15},{6,3},{7,10},{8,5},{9,12},{10,0},{11,14},... | collective-permute-start | bytes 786440 | tf_op jit(solution)/shard_map/ppermute | solution.py:198
  80.8 23.1 %collective-permute-start.8 = (bf16[2,128,512]{2,1,0:T(8,128)(2,1)S(1)}, bf16[2,128,512]{2,1,0:T(8,128)(2,1)S(1)}, u32[]{:S(2)}, u32[]{:S(2)}) collective-permute-start(bf16[2,128,512]{2,1,0:T(8,128)(2,1)S(1)} %get-tuple-element.28), channel_id=1, source_target_pairs={{2,0},{3,1},{4,2},{5,3},{6,4},{7,5},{8,6},{9,7},{10,8},{11,9},{12,... | collective-permute-start | bytes 786440 | tf_op jit(solution)/shard_map/ppermute | solution.py:201
  83.5 20.4 %collective-permute-start.9 = (bf16[2,128,512]{2,1,0:T(8,128)(2,1)S(1)}, bf16[2,128,512]{2,1,0:T(8,128)(2,1)S(1)}, u32[]{:S(2)}, u32[]{:S(2)}) collective-permute-start(bf16[2,128,512]{2,1,0:T(8,128)(2,1)S(1)} %get-tuple-element.27), channel_id=1, source_target_pairs={{0,2},{1,3},{2,4},{3,5},{4,6},{5,7},{6,8},{7,9},{8,10},{9,11},{10,... | collective-permute-start | bytes 786440 | tf_op jit(solution)/shard_map/ppermute | solution.py:202
  92.3 11.6 %collective-permute-start.11 = (bf16[2,128,512]{2,1,0:T(8,128)(2,1)S(1)}, bf16[2,128,512]{2,1,0:T(8,128)(2,1)S(1)}, u32[]{:S(2)}, u32[]{:S(2)}) collective-permute-start(bf16[2,128,512]{2,1,0:T(8,128)(2,1)S(1)} %collective-permute-done.10), channel_id=1, source_target_pairs={{15,8},{0,7},{23,16},{8,15},{31,24},{16,23},{47,40},{32,39},{55,48... | collective-permute-start | bytes 786440 | tf_op jit(solution)/shard_map/ppermute | solution.py:204

commit v4 on v3

--- a/solution.py
+++ b/solution.py
@@ -10,7 +10,6 @@
 
 HQ, HK, HD, W = 32, 4, 128, 3
 BL = 128
-ROW = 8
 G = HQ // HK
 NS = 2 * W + 1
 SCALE = 1.0 / math.sqrt(HD)
@@ -25,33 +24,23 @@
     return [0, -2, 2, -3 * sign, sign, sign - 2, sign + 2]
 
 
-def at_corner(index):
-    place = index % ROW
-    return (place == 0) | (place == ROW - 1)
-
-
 def backward_body(n_grads, n_kept, *refs):
     mask, q = refs[:2]
     grads = refs[2 : 2 + n_grads]
-    own, left, right, far, far_row, mate = refs[2 + n_grads : 8 + n_grads]
-    dq, parts, to_mate, to_far, kc, vc, kt = refs[8 + n_grads + n_kept :]
+    own, left, right, far, mate = refs[2 + n_grads : 7 + n_grads]
+    dq, parts, to_mate, to_far, kc, vc, kt = refs[7 + n_grads + n_kept :]
     index = lax.axis_index("seq")
     count = lax.axis_size("seq")
     on = [None]
     for offset in slot_offsets(index % 2)[1:]:
         inside = (index + offset >= 0) & (index + offset < count)
         on.append(inside & (mask[0, offset + W] == 1))
-    corner = at_corner(index)
-
-    def place(ref, row):
-        kc[row : row + ref.shape[1]] = ref[0]
-        vc[row : row + ref.shape[1]] = ref[1]
-
-    for i, ref in enumerate((own, left, right)):
-        place(ref, i * BL)
-    pl.when(corner)(lambda: place(far_row, 3 * BL))
-    pl.when(jnp.logical_not(corner))(lambda: place(far, 3 * BL))
-    place(mate, 4 * BL)
+    row = 0
+    for ref in (own, left, right, far, mate):
+        n = ref.shape[1]
+        kc[row : row + n] = ref[0]
+        vc[row : row + n] = ref[1]
+        row += n
     for s in range(NS):
         kt[:, s * BL : (s + 1) * BL] = kc[s * BL : (s + 1) * BL, :].T
     cols = [slice(i * HD, (i + 1) * HD) for i in range(G)]
@@ -137,7 +126,7 @@
     pass
 
 
-def hold(*arrays):
+def hold(*arrays, flops=1 << 34):
     anywhere = [pl.BlockSpec(memory_space=pl.ANY) for _ in arrays]
     return pl.pallas_call(
         hold_body,
@@ -146,7 +135,7 @@
         out_shape=[jax.ShapeDtypeStruct(x.shape, x.dtype) for x in arrays],
         input_output_aliases={i: i for i in range(len(arrays))},
         compiler_params=pltpu.CompilerParams(vmem_limit_bytes=1 << 20),
-        cost_estimate=pl.CostEstimate(flops=1 << 34, bytes_accessed=0, transcendentals=0),
+        cost_estimate=pl.CostEstimate(flops=flops, bytes_accessed=0, transcendentals=0),
         name="hold",
     )(*arrays)
 
@@ -159,51 +148,44 @@
     return [(i, i ^ 1) for i in range(count)]
 
 
-def far_hops(count):
-    first, second = [], []
-    for i in range(count):
-        j = i + 3 if i % 2 else i - 3
-        if not 0 <= j < count:
-            continue
-        if j // ROW != i // ROW and j % ROW in (0, ROW - 1):
-            via = j // ROW * ROW + ROW - 1 - j % ROW
-            first.append((i, via))
-            second.append((via, j))
-        else:
-            first.append((i, j))
-    return first, second
+def far_pairs(count):
+    ends = [(i, i + 3 if i % 2 else i - 3) for i in range(count)]
+    return [(i, j) for i, j in ends if 0 <= j < count]
 
 
 def shards(query_heads, key_heads, value_heads, section_cotangent, block_mask):
     sections = lax.axis_size("section")
     count = lax.axis_size("seq")
-    corner = at_corner(lax.axis_index("seq"))
     half = HQ * HD // 2
     cot = section_cotangent[0]
     before = [(i, (i - 1) % sections) for i in range(sections)]
-    first, second = far_hops(count)
     own = join(key_heads[0], value_heads[0])
-    left = lax.ppermute(own, "seq", shift_pairs(count, 2))
-    right = lax.ppermute(own, "seq", shift_pairs(count, -2))
-    far = lax.ppermute(own, "seq", first)
-    (grad_low,) = hold(lax.ppermute(cot[:, :half], "section", before))
+    left, right = hold(
+        lax.ppermute(own, "seq", shift_pairs(count, 2)),
+        lax.ppermute(own, "seq", shift_pairs(count, -2)),
+        flops=1 << 32,
+    )
+    far, grad_low = hold(
+        lax.ppermute(own, "seq", far_pairs(count)),
+        lax.ppermute(cot[:, :half], "section", before),
+        flops=1 << 33,
+    )
     grad_high = lax.ppermute(cot[:, half:], "section", before)
     mate = lax.ppermute(bundle(own, left, right), "seq", mate_pairs(count))
-    far_row = lax.ppermute(far, "seq", second)
-    slots = (own, left, right, far, far_row, mate)
+    slots = (own, left, right, far, mate)
     kept = attention_backward(block_mask, query_heads[0], (grad_low,), slots, 0, 2, ())
     query_grad, parts, to_mate, to_far = attention_backward(
         block_mask, query_heads[0], (grad_high,), slots, 2, 2, kept
     )
-    back_far = lax.ppermute(to_far, "seq", first)
+    (back_far,) = hold(lax.ppermute(to_far, "seq", far_pairs(count)), flops=1 << 33)
     sums = parts + lax.ppermute(to_mate, "seq", mate_pairs(count)).astype(F32)
-    back_left, back_right = hold(
+    back_far, back_left, back_right = hold(
+        back_far,
         lax.ppermute(sums[:, BL : 2 * BL].astype(B16), "seq", shift_pairs(count, -2)),
         lax.ppermute(sums[:, 2 * BL :].astype(B16), "seq", shift_pairs(count, 2)),
     )
-    back_row = lax.ppermute(back_far, "seq", second)
-    total = sums[:, :BL] + back_left.astype(F32) + back_right.astype(F32)
-    total = (total + jnp.where(corner, back_row, back_far).astype(F32)).astype(B16)
+    total = sums[:, :BL] + back_left.astype(F32) + back_right.astype(F32) + back_far.astype(F32)
+    total = total.astype(B16)
     return query_grad[None], total[0][None], total[1][None]
 
 

time: 105 us -> 102 us (0.971)
  the two profiles are of different devices: /device:TPU:254 before, /device:TPU:191 now
where the time goes in v4:
time: 102 us; the launch traced here: 101 us
  starting transfers between devices  41 us (40%)
  waiting for transfers between devices  37.9 us (37%)
  Pallas kernels  17 us (17%)
  local copies, waits for them, and re-layouts  3.87 us (4%)
    ppermute x1, waiting for transfers between devices, shards(): lax.ppermute(own, 'seq', shift_pairs(count, 2))  23 us
    pallas_call x2, Pallas kernels, attention_backward(): pl.pallas_call(functools.partial(backward_body, len(grads), len(kept)), g...  17 us
    ppermute x1, starting transfers between devices, shards(): lax.ppermute(own, 'seq', shift_pairs(count, 2))  7.04 us
    ppermute x1, waiting for transfers between devices, shards(): lax.ppermute(sums[:, BL:2 * BL].astype(B16), 'seq', shift_pairs(count, -2))  5.72 us
    ppermute x1, starting transfers between devices, shards(): lax.ppermute(to_far, 'seq', far_pairs(count))  5.52 us
    ppermute x1, starting transfers between devices, shards(): mate = lax.ppermute(bundle(own, left, right), 'seq', mate_pairs(count))  5.51 us
    ppermute x1, starting transfers between devices, shards(): lax.ppermute(own, 'seq', far_pairs(count))  5.04 us
    ppermute x1, starting transfers between devices, shards(): lax.ppermute(sums[:, 2 * BL:].astype(B16), 'seq', shift_pairs(count, 2))  4.74 us
  transfers between devices with their start and end apart: 10, of which 5 were waited for; matrix products, arithmetic and copies ran while one was open for 2% of the time, Pallas kernels for 8%

profile of v4, /device:TPU:191, one launch (start us, length us, event | category | flops | bytes accessed | tf_op | source)
XLA Modules:
  0.0 101.1 jit_solution(4683507531387653941)
XLA Ops:
  0.6 0.9 copy-done
  1.5 0.9 copy-done.1
  2.5 2.5 %collective-permute-start.2 = (bf16[2,128,512]{2,1,0:T(8,128)(2,1)S(1)}, bf16[2,128,512]{2,1,0:T(8,128)(2,1)S(1)}, u32[]{:S(2)}, u32[]{:S(2)}) collective-permute-start(bf16[2,128,512]{2,1,0:T(8,128)(2,1)S(1)} %join.1.own.refs_3_), channel_id=1, source_target_pairs={{2,0},{3,1},{4,2},{5,3},{6,4},{7,5},{8,6},{9,7},{10,8},{11,9},{12,... | collective-permute-start | bytes 786440 | tf_op jit(solution)/shard_map/ppermute | solution.py:165
  4.9 7.0 %collective-permute-start.1 = (bf16[2,128,512]{2,1,0:T(8,128)(2,1)S(1)}, bf16[2,128,512]{2,1,0:T(8,128)(2,1)S(1)}, u32[]{:S(2)}, u32[]{:S(2)}) collective-permute-start(bf16[2,128,512]{2,1,0:T(8,128)(2,1)S(1)} %join.1.own.refs_3_), channel_id=1, source_target_pairs={{0,2},{1,3},{2,4},{3,5},{4,6},{5,7},{6,8},{7,9},{8,10},{9,11},{10,... | collective-permute-start | bytes 786440 | tf_op jit(solution)/shard_map/ppermute | solution.py:164
  12.0 1.3 %fusion.4 = (bf16[128,2048]{1,0:T(8,128)(2,1)S(1)}, bf16[128,2048]{1,0:T(8,128)(2,1)S(1)}) fusion(bf16[128,4096]{1,0:T(8,128)(2,1)} %bitcast.9), kind=kLoop, calls=%fused_computation.6 | loop fusion | bytes 2097152 | tf_op jit(solution)/shard_map/slice | solution.py:170
  13.3 3.0 %collective-permute-start.4 = (bf16[128,2048]{1,0:T(8,128)(2,1)S(1)}, bf16[128,2048]{1,0:T(8,128)(2,1)S(1)}, u32[]{:S(2)}, u32[]{:S(2)}) collective-permute-start(bf16[128,2048]{1,0:T(8,128)(2,1)S(1)} %get-tuple-element.35), channel_id=1, source_target_pairs={{0,480},{32,0},{64,32},{96,64},{128,96},{160,128},{192,160},{224,1... | collective-permute-start | bytes 1572872 | tf_op jit(solution)/shard_map/ppermute | solution.py:170
  16.3 5.0 %collective-permute-start.3 = (bf16[2,128,512]{2,1,0:T(8,128)(2,1)S(1)}, bf16[2,128,512]{2,1,0:T(8,128)(2,1)S(1)}, u32[]{:S(2)}, u32[]{:S(2)}) collective-permute-start(bf16[2,128,512]{2,1,0:T(8,128)(2,1)S(1)} %join.1.own.refs_3_), channel_id=1, source_target_pairs={{1,4},{3,6},{4,1},{5,8},{6,3},{7,10},{8,5},{9,12},{10,7},{11,14},{... | collective-permute-start | bytes 786440 | tf_op jit(solution)/shard_map/ppermute | solution.py:169
  21.3 3.0 %collective-permute-start = (bf16[128,2048]{1,0:T(8,128)(2,1)S(1)}, bf16[128,2048]{1,0:T(8,128)(2,1)S(1)}, u32[]{:S(2)}, u32[]{:S(2)}) collective-permute-start(bf16[128,2048]{1,0:T(8,128)(2,1)S(1)} %get-tuple-element.36), channel_id=1, source_target_pairs={{0,480},{32,0},{64,32},{96,64},{128,96},{160,128},{192,160},{224,1... | collective-permute-start | bytes 1572872 | tf_op jit(solution)/shard_map/ppermute | solution.py:173
  24.3 0.0 collective-permute-done.2.refs_1_
  24.3 23.0 %collective-permute-done.1.refs_0_ = bf16[2,128,512]{2,1,0:T(8,128)(2,1)S(1)} collective-permute-done((bf16[2,128,512]{2,1,0:T(8,128)(2,1)S(1)}, bf16[2,128,512]{2,1,0:T(8,128)(2,1)S(1)}, u32[]{:S(2)}, u32[]{:S(2)}) %collective-permute-start.1) | collective-permute-done | bytes 262176 | tf_op jit(solution)/shard_map/ppermute | solution.py:164
  47.3 0.1 bundle.1
  47.4 0.0 copy-start.2
  47.4 0.0 copy-start.3
  47.4 5.5 %collective-permute-start.5 = (bf16[2,384,512]{2,1,0:T(8,128)(2,1)S(1)}, bf16[2,384,512]{2,1,0:T(8,128)(2,1)S(1)}, u32[]{:S(2)}, u32[]{:S(2)}) collective-permute-start(bf16[2,384,512]{2,1,0:T(8,128)(2,1)S(1)} %bundle.1), channel_id=1, source_target_pairs={{0,1},{1,0},{2,3},{3,2},{4,5},{5,4},{6,7},{7,6},{8,9},{9,8},{10,11... | collective-permute-start | bytes 2359304 | tf_op jit(solution)/shard_map/ppermute | solution.py:174
  52.9 0.0 collective-permute-done.3.refs_0_
  52.9 0.0 collective-permute-done.4.refs_1_
  52.9 1.9 %collective-permute-done.5.refs_7_ = bf16[2,384,512]{2,1,0:T(8,128)(2,1)S(1)} collective-permute-done((bf16[2,384,512]{2,1,0:T(8,128)(2,1)S(1)}, bf16[2,384,512]{2,1,0:T(8,128)(2,1)S(1)}, u32[]{:S(2)}, u32[]{:S(2)}) %collective-permute-start.5) | collective-permute-done | bytes 786464 | tf_op jit(solution)/shard_map/ppermute | solution.py:174
  54.8 0.0 copy-done.2
  54.8 8.5 %attention_backward.2 = (bf16[128,4096]{1,0:T(8,128)(2,1)}, f32[2,384,512]{2,1,0:T(8,128)S(1)}, bf16[2,384,512]{2,1,0:T(8,128)(2,1)S(1)}, bf16[2,128,512]{2,1,0:T(8,128)(2,1)S(1)}) custom-call(s32[1,7]{1,0:T(1,128)S(1)} %copy-done.3, bf16[128,4096]{1,0:T(8,128)(2,1)S(1)} %bitcast.7, bf16[128,2048]{1,0:T(8,128)(2,1)S(1)} %get-tuple-element.21.refs_2_, ...), custom_call_target="tpu_custom_call" | custom-call | flops 2147483648 | bytes 2097152 | tf_op jit(solution)/shard_map/attention_backward/pallas_call | solution.py:79
  63.3 0.0 collective-permute-done.refs_2_
  63.3 8.5 %attention_backward.3 = (bf16[128,4096]{1,0:T(8,128)(2,1)}, f32[2,384,512]{2,1,0:T(8,128)S(1)}, bf16[2,384,512]{2,1,0:T(8,128)(2,1)S(1)}, bf16[2,128,512]{2,1,0:T(8,128)(2,1)S(1)}) custom-call(s32[1,7]{1,0:T(1,128)S(1)} %copy-done.3, bf16[128,4096]{1,0:T(8,128)(2,1)S(1)} %bitcast.8, ...), custom_call_target="tpu_custom_call", output_to_operand_aliasing={{0}: (8, {}), {1}: (9, {}), {2}: (10, {}), {3}: (11, {})} | custom-call | flops 2147483648 | bytes 2097152 | tf_op jit(solution)/shard_map/attention_backward/pallas_call | solution.py:79
  71.8 2.3 %collective-permute-start.6 = (bf16[2,384,512]{2,1,0:T(8,128)(2,1)S(1)}, bf16[2,384,512]{2,1,0:T(8,128)(2,1)S(1)}, u32[]{:S(2)}, u32[]{:S(2)}) collective-permute-start(bf16[2,384,512]{2,1,0:T(8,128)(2,1)S(1)} %get-tuple-element.28), channel_id=1, source_target_pairs={{0,1},{1,0},{2,3},{3,2},{4,5},{5,4},{6,7},{7,6},{8,9},{9,8},{10,11... | collective-permute-start | bytes 2359304 | tf_op jit(solution)/shard_map/ppermute | solution.py:181
  74.0 5.5 %collective-permute-start.7 = (bf16[2,128,512]{2,1,0:T(8,128)(2,1)S(1)}, bf16[2,128,512]{2,1,0:T(8,128)(2,1)S(1)}, u32[]{:S(2)}, u32[]{:S(2)}) collective-permute-start(bf16[2,128,512]{2,1,0:T(8,128)(2,1)S(1)} %get-tuple-element.29), channel_id=1, source_target_pairs={{1,4},{3,6},{4,1},{5,8},{6,3},{7,10},{8,5},{9,12},{10,7},{11,14},{... | collective-permute-start | bytes 786440 | tf_op jit(solution)/shard_map/ppermute | solution.py:180
  79.6 0.0 collective-permute-done.6
  79.6 0.3 fusion.3
  79.9 4.7 %collective-permute-start.9 = (bf16[2,128,512]{2,1,0:T(8,128)(2,1)S(1)}, bf16[2,128,512]{2,1,0:T(8,128)(2,1)S(1)}, u32[]{:S(2)}, u32[]{:S(2)}) collective-permute-start(bf16[2,128,512]{2,1,0:T(8,128)(2,1)S(1)} %get-tuple-element.37), channel_id=1, source_target_pairs={{0,2},{1,3},{2,4},{3,5},{4,6},{5,7},{6,8},{7,9},{8,10},{9,11},{10,... | collective-permute-start | bytes 786440 | tf_op jit(solution)/shard_map/ppermute | solution.py:185
  84.7 2.5 %collective-permute-start.8 = (bf16[2,128,512]{2,1,0:T(8,128)(2,1)S(1)}, bf16[2,128,512]{2,1,0:T(8,128)(2,1)S(1)}, u32[]{:S(2)}, u32[]{:S(2)}) collective-permute-start(bf16[2,128,512]{2,1,0:T(8,128)(2,1)S(1)} %get-tuple-element.38), channel_id=1, source_target_pairs={{2,0},{3,1},{4,2},{5,3},{6,4},{7,5},{8,6},{9,7},{10,8},{11,9},{12,... | collective-permute-start | bytes 786440 | tf_op jit(solution)/shard_map/ppermute | solution.py:184
  87.2 4.5 %collective-permute-done.7.refs_0_ = bf16[2,128,512]{2,1,0:T(8,128)(2,1)S(1)} collective-permute-done((bf16[2,128,512]{2,1,0:T(8,128)(2,1)S(1)}, bf16[2,128,512]{2,1,0:T(8,128)(2,1)S(1)}, u32[]{:S(2)}, u32[]{:S(2)}) %collective-permute-start.7) | collective-permute-done | bytes 262176 | tf_op jit(solution)/shard_map/ppermute | solution.py:180
  91.6 2.9 %collective-permute-done.9.refs_2_ = bf16[2,128,512]{2,1,0:T(8,128)(2,1)S(1)} collective-permute-done((bf16[2,128,512]{2,1,0:T(8,128)(2,1)S(1)}, bf16[2,128,512]{2,1,0:T(8,128)(2,1)S(1)}, u32[]{:S(2)}, u32[]{:S(2)}) %collective-permute-start.9) | collective-permute-done | bytes 262176 | tf_op jit(solution)/shard_map/ppermute | solution.py:185
  94.5 5.7 %collective-permute-done.8.refs_1_ = bf16[2,128,512]{2,1,0:T(8,128)(2,1)S(1)} collective-permute-done((bf16[2,128,512]{2,1,0:T(8,128)(2,1)S(1)}, bf16[2,128,512]{2,1,0:T(8,128)(2,1)S(1)}, u32[]{:S(2)}, u32[]{:S(2)}) %collective-permute-start.8) | collective-permute-done | bytes 262176 | tf_op jit(solution)/shard_map/ppermute | solution.py:184
  100.3 0.2 fusion.2
  100.4 0.7 fusion.6
  (9 shorter events, 0.1 us)
Async XLA Ops:
  0.6 0.9 copy-start
  1.5 0.9 copy-start.1
  2.5 21.8 %collective-permute-start.2 = (bf16[2,128,512]{2,1,0:T(8,128)(2,1)S(1)}, bf16[2,128,512]{2,1,0:T(8,128)(2,1)S(1)}, u32[]{:S(2)}, u32[]{:S(2)}) collective-permute-start(bf16[2,128,512]{2,1,0:T(8,128)(2,1)S(1)} %join.1.own.refs_3_), channel_id=1, source_target_pairs={{2,0},{3,1},{4,2},{5,3},{6,4},{7,5},{8,6},{9,7},{10,8},{11,9},{12,... | collective-permute-start | bytes 786440 | tf_op jit(solution)/shard_map/ppermute | solution.py:165
  4.9 42.4 %collective-permute-start.1 = (bf16[2,128,512]{2,1,0:T(8,128)(2,1)S(1)}, bf16[2,128,512]{2,1,0:T(8,128)(2,1)S(1)}, u32[]{:S(2)}, u32[]{:S(2)}) collective-permute-start(bf16[2,128,512]{2,1,0:T(8,128)(2,1)S(1)} %join.1.own.refs_3_), channel_id=1, source_target_pairs={{0,2},{1,3},{2,4},{3,5},{4,6},{5,7},{6,8},{7,9},{8,10},{9,11},{10,... | collective-permute-start | bytes 786440 | tf_op jit(solution)/shard_map/ppermute | solution.py:164
  13.3 39.6 %collective-permute-start.4 = (bf16[128,2048]{1,0:T(8,128)(2,1)S(1)}, bf16[128,2048]{1,0:T(8,128)(2,1)S(1)}, u32[]{:S(2)}, u32[]{:S(2)}) collective-permute-start(bf16[128,2048]{1,0:T(8,128)(2,1)S(1)} %get-tuple-element.35), channel_id=1, source_target_pairs={{0,480},{32,0},{64,32},{96,64},{128,96},{160,128},{192,160},{224,1... | collective-permute-start | bytes 1572872 | tf_op jit(solution)/shard_map/ppermute | solution.py:170
  16.3 36.6 %collective-permute-start.3 = (bf16[2,128,512]{2,1,0:T(8,128)(2,1)S(1)}, bf16[2,128,512]{2,1,0:T(8,128)(2,1)S(1)}, u32[]{:S(2)}, u32[]{:S(2)}) collective-permute-start(bf16[2,128,512]{2,1,0:T(8,128)(2,1)S(1)} %join.1.own.refs_3_), channel_id=1, source_target_pairs={{1,4},{3,6},{4,1},{5,8},{6,3},{7,10},{8,5},{9,12},{10,7},{11,14},{... | collective-permute-start | bytes 786440 | tf_op jit(solution)/shard_map/ppermute | solution.py:169
  21.3 41.9 %collective-permute-start = (bf16[128,2048]{1,0:T(8,128)(2,1)S(1)}, bf16[128,2048]{1,0:T(8,128)(2,1)S(1)}, u32[]{:S(2)}, u32[]{:S(2)}) collective-permute-start(bf16[128,2048]{1,0:T(8,128)(2,1)S(1)} %get-tuple-element.36), channel_id=1, source_target_pairs={{0,480},{32,0},{64,32},{96,64},{128,96},{160,128},{192,160},{224,1... | collective-permute-start | bytes 1572872 | tf_op jit(solution)/shard_map/ppermute | solution.py:173
  47.4 7.4 %copy-start.2 = (bf16[1,128,4096]{2,1,0:T(8,128)(2,1)S(1)}, bf16[1,128,4096]{2,1,0:T(8,128)(2,1)}, u32[]{:S(2)}) copy-start(bf16[1,128,4096]{2,1,0:T(8,128)(2,1)} %param.5) | copy-start | bytes 3145732
  47.4 7.4 %copy-start.3 = (s32[1,7]{1,0:T(1,128)S(1)}, s32[1,7]{1,0:T(1,128)}, u32[]{:S(2)}) copy-start(s32[1,7]{1,0:T(1,128)} %refs_0_.3) | copy-start | bytes 88
  47.4 7.4 %collective-permute-start.5 = (bf16[2,384,512]{2,1,0:T(8,128)(2,1)S(1)}, bf16[2,384,512]{2,1,0:T(8,128)(2,1)S(1)}, u32[]{:S(2)}, u32[]{:S(2)}) collective-permute-start(bf16[2,384,512]{2,1,0:T(8,128)(2,1)S(1)} %bundle.1), channel_id=1, source_target_pairs={{0,1},{1,0},{2,3},{3,2},{4,5},{5,4},{6,7},{7,6},{8,9},{9,8},{10,11... | collective-permute-start | bytes 2359304 | tf_op jit(solution)/shard_map/ppermute | solution.py:174
  71.8 7.8 %collective-permute-start.6 = (bf16[2,384,512]{2,1,0:T(8,128)(2,1)S(1)}, bf16[2,384,512]{2,1,0:T(8,128)(2,1)S(1)}, u32[]{:S(2)}, u32[]{:S(2)}) collective-permute-start(bf16[2,384,512]{2,1,0:T(8,128)(2,1)S(1)} %get-tuple-element.28), channel_id=1, source_target_pairs={{0,1},{1,0},{2,3},{3,2},{4,5},{5,4},{6,7},{7,6},{8,9},{9,8},{10,11... | collective-permute-start | bytes 2359304 | tf_op jit(solution)/shard_map/ppermute | solution.py:181
  74.0 17.6 %collective-permute-start.7 = (bf16[2,128,512]{2,1,0:T(8,128)(2,1)S(1)}, bf16[2,128,512]{2,1,0:T(8,128)(2,1)S(1)}, u32[]{:S(2)}, u32[]{:S(2)}) collective-permute-start(bf16[2,128,512]{2,1,0:T(8,128)(2,1)S(1)} %get-tuple-element.29), channel_id=1, source_target_pairs={{1,4},{3,6},{4,1},{5,8},{6,3},{7,10},{8,5},{9,12},{10,7},{11,14},{... | collective-permute-start | bytes 786440 | tf_op jit(solution)/shard_map/ppermute | solution.py:180
  79.9 14.6 %collective-permute-start.9 = (bf16[2,128,512]{2,1,0:T(8,128)(2,1)S(1)}, bf16[2,128,512]{2,1,0:T(8,128)(2,1)S(1)}, u32[]{:S(2)}, u32[]{:S(2)}) collective-permute-start(bf16[2,128,512]{2,1,0:T(8,128)(2,1)S(1)} %get-tuple-element.37), channel_id=1, source_target_pairs={{0,2},{1,3},{2,4},{3,5},{4,6},{5,7},{6,8},{7,9},{8,10},{9,11},{10,... | collective-permute-start | bytes 786440 | tf_op jit(solution)/shard_map/ppermute | solution.py:185
  84.7 15.6 %collective-permute-start.8 = (bf16[2,128,512]{2,1,0:T(8,128)(2,1)S(1)}, bf16[2,128,512]{2,1,0:T(8,128)(2,1)S(1)}, u32[]{:S(2)}, u32[]{:S(2)}) collective-permute-start(bf16[2,128,512]{2,1,0:T(8,128)(2,1)S(1)} %get-tuple-element.38), channel_id=1, source_target_pairs={{2,0},{3,1},{4,2},{5,3},{6,4},{7,5},{8,6},{9,7},{10,8},{11,9},{12,... | collective-permute-start | bytes 786440 | tf_op jit(solution)/shard_map/ppermute | solution.py:184

commit v5 on v4

--- a/solution.py
+++ b/solution.py
@@ -157,7 +157,9 @@
     sections = lax.axis_size("section")
     count = lax.axis_size("seq")
     half = HQ * HD // 2
+    turn = sections // 2
     cot = section_cotangent[0]
+    low, high = cot[:, :half], cot[:, half:]
     before = [(i, (i - 1) % sections) for i in range(sections)]
     own = join(key_heads[0], value_heads[0])
     left, right = hold(
@@ -166,16 +168,17 @@
         flops=1 << 32,
     )
     far, grad_low = hold(
-        lax.ppermute(own, "seq", far_pairs(count)),
-        lax.ppermute(cot[:, :half], "section", before),
-        flops=1 << 33,
-    )
-    grad_high = lax.ppermute(cot[:, half:], "section", before)
-    mate = lax.ppermute(bundle(own, left, right), "seq", mate_pairs(count))
+        lax.ppermute(own, "seq", far_pairs(count)), lax.ppermute(low, "section", before), flops=1 << 33
+    )
+    (turned,) = hold(lax.ppermute(high, "section", [(0, turn), (turn, 0)]), flops=1 << 33)
+    joined, high = lax.optimization_barrier((bundle(own, left, right), high))
+    mate = lax.ppermute(joined, "seq", mate_pairs(count))
+    grad_high = lax.ppermute(high, "section", [(i, i - 1) for i in range(sections) if i % turn])
+    grad_wrap = lax.ppermute(turned, "section", [(0, turn - 1), (turn, sections - 1)])
     slots = (own, left, right, far, mate)
     kept = attention_backward(block_mask, query_heads[0], (grad_low,), slots, 0, 2, ())
     query_grad, parts, to_mate, to_far = attention_backward(
-        block_mask, query_heads[0], (grad_high,), slots, 2, 2, kept
+        block_mask, query_heads[0], (grad_high, grad_wrap), slots, 2, 2, kept
     )
     (back_far,) = hold(lax.ppermute(to_far, "seq", far_pairs(count)), flops=1 << 33)
     sums = parts + lax.ppermute(to_mate, "seq", mate_pairs(count)).astype(F32)

time: 102 us -> 93.4 us (0.916)
  the two profiles are of different devices: /device:TPU:191 before, /device:TPU:318 now
where the time goes in v5:
time: 93.4 us; the launch traced here: 92.9 us
  waiting for transfers between devices  38.1 us (41%)
  starting transfers between devices  32.7 us (35%)
  Pallas kernels  17 us (18%)
  local copies, waits for them, and re-layouts  3.87 us (4%)
    pallas_call x2, Pallas kernels, attention_backward(): pl.pallas_call(functools.partial(backward_body, len(grads), len(kept)), g...  17 us
    ppermute x1, waiting for transfers between devices, shards(): lax.ppermute(own, 'seq', shift_pairs(count, 2))  10.7 us
    ppermute x1, waiting for transfers between devices, shards(): lax.ppermute(own, 'seq', shift_pairs(count, -2))  8.37 us
    ppermute x1, starting transfers between devices, shards(): lax.ppermute(sums[:, 2 * BL:].astype(B16), 'seq', shift_pairs(count, 2))  7.54 us
    ppermute x1, waiting for transfers between devices, shards(): lax.ppermute(turned, 'section', [(0, turn - 1), (turn, sections - 1)])  6.87 us
    ppermute x1, starting transfers between devices, shards(): lax.ppermute(own, 'seq', shift_pairs(count, 2))  6.11 us
    ppermute x1, waiting for transfers between devices, shards(): lax.ppermute(sums[:, 2 * BL:].astype(B16), 'seq', shift_pairs(count, 2))  5.44 us
    ppermute x1, waiting for transfers between devices, shards(): lax.ppermute(sums[:, BL:2 * BL].astype(B16), 'seq', shift_pairs(count, -2))  4.84 us
  transfers between devices with their start and end apart: 12, of which 8 were waited for; matrix products, arithmetic and copies ran while one was open for 2% of the time, Pallas kernels for 9%

profile of v5, /device:TPU:318, one launch (start us, length us, event | category | flops | bytes accessed | tf_op | source)
XLA Modules:
  0.0 92.9 jit_solution(1479777913548735008)
XLA Ops:
  0.6 0.9 copy-done
  1.5 0.9 copy-done.1
  2.5 2.7 %collective-permute-start.1 = (bf16[2,128,512]{2,1,0:T(8,128)(2,1)S(1)}, bf16[2,128,512]{2,1,0:T(8,128)(2,1)S(1)}, u32[]{:S(2)}, u32[]{:S(2)}) collective-permute-start(bf16[2,128,512]{2,1,0:T(8,128)(2,1)S(1)} %join.1.own.refs_3_.refs_4_), channel_id=1, source_target_pairs={{2,0},{3,1},{4,2},{5,3},{6,4},{7,5},{8,6},{9,7},{10,8},{11,9},{12,... | collective-permute-start | bytes 786440 | tf_op jit(solution)/shard_map/ppermute | solution.py:167
  5.2 6.1 %collective-permute-start = (bf16[2,128,512]{2,1,0:T(8,128)(2,1)S(1)}, bf16[2,128,512]{2,1,0:T(8,128)(2,1)S(1)}, u32[]{:S(2)}, u32[]{:S(2)}) collective-permute-start(bf16[2,128,512]{2,1,0:T(8,128)(2,1)S(1)} %join.1.own.refs_3_.refs_4_), channel_id=1, source_target_pairs={{0,2},{1,3},{2,4},{3,5},{4,6},{5,7},{6,8},{7,9},{8,10},{9,11},{10,... | collective-permute-start | bytes 786440 | tf_op jit(solution)/shard_map/ppermute | solution.py:166
  11.3 1.3 %fusion.4 = (bf16[128,2048]{1,0:T(8,128)(2,1)S(1)}, bf16[128,2048]{1,0:T(8,128)(2,1)S(1)}) fusion(bf16[128,4096]{1,0:T(8,128)(2,1)} %bitcast.9), kind=kLoop, calls=%fused_computation.6 | loop fusion | bytes 2097152 | tf_op jit(solution)/shard_map/slice | solution.py:162
  12.6 0.7 collective-permute-start.3
  13.3 1.9 %collective-permute-start.5 = (bf16[2,128,512]{2,1,0:T(8,128)(2,1)S(1)}, bf16[2,128,512]{2,1,0:T(8,128)(2,1)S(1)}, u32[]{:S(2)}, u32[]{:S(2)}) collective-permute-start(bf16[2,128,512]{2,1,0:T(8,128)(2,1)S(1)} %join.1.own.refs_3_.refs_4_), channel_id=1, source_target_pairs={{1,4},{3,6},{4,1},{5,8},{6,3},{7,10},{8,5},{9,12},{10,7},{11,14},{... | collective-permute-start | bytes 786440 | tf_op jit(solution)/shard_map/ppermute | solution.py:171
  15.3 3.3 %collective-permute-start.6 = (bf16[128,2048]{1,0:T(8,128)(2,1)S(1)}, bf16[128,2048]{1,0:T(8,128)(2,1)S(1)}, u32[]{:S(2)}, u32[]{:S(2)}) collective-permute-start(bf16[128,2048]{1,0:T(8,128)(2,1)S(1)} %get-tuple-element.39), channel_id=1, source_target_pairs={{0,480},{32,0},{64,32},{96,64},{128,96},{160,128},{192,160},{224,1... | collective-permute-start | bytes 1572872 | tf_op jit(solution)/shard_map/ppermute | solution.py:171
  18.5 8.4 %collective-permute-done.1.refs_1_ = bf16[2,128,512]{2,1,0:T(8,128)(2,1)S(1)} collective-permute-done((bf16[2,128,512]{2,1,0:T(8,128)(2,1)S(1)}, bf16[2,128,512]{2,1,0:T(8,128)(2,1)S(1)}, u32[]{:S(2)}, u32[]{:S(2)}) %collective-permute-start.1) | collective-permute-done | bytes 262176 | tf_op jit(solution)/shard_map/ppermute | solution.py:167
  26.9 10.7 %collective-permute-done.refs_0_ = bf16[2,128,512]{2,1,0:T(8,128)(2,1)S(1)} collective-permute-done((bf16[2,128,512]{2,1,0:T(8,128)(2,1)S(1)}, bf16[2,128,512]{2,1,0:T(8,128)(2,1)S(1)}, u32[]{:S(2)}, u32[]{:S(2)}) %collective-permute-start) | collective-permute-done | bytes 262176 | tf_op jit(solution)/shard_map/ppermute | solution.py:166
  37.6 0.1 bundle.1
  37.6 1.3 %collective-permute-start.2 = (bf16[128,2048]{1,0:T(8,128)(2,1)S(1)}, bf16[128,2048]{1,0:T(8,128)(2,1)S(1)}, u32[]{:S(2)}, u32[]{:S(2)}) collective-permute-start(bf16[128,2048]{1,0:T(8,128)(2,1)S(1)} %get-tuple-element.22), channel_id=1, source_target_pairs={{32,0},{64,32},{96,64},{128,96},{160,128},{192,160},{224,192},{288... | collective-permute-start | bytes 1572872 | tf_op jit(solution)/shard_map/ppermute | solution.py:176
  38.9 1.9 %collective-permute-start.7 = (bf16[2,384,512]{2,1,0:T(8,128)(2,1)S(1)}, bf16[2,384,512]{2,1,0:T(8,128)(2,1)S(1)}, u32[]{:S(2)}, u32[]{:S(2)}) collective-permute-start(bf16[2,384,512]{2,1,0:T(8,128)(2,1)S(1)} %bundle.1), channel_id=1, source_target_pairs={{0,1},{1,0},{2,3},{3,2},{4,5},{5,4},{6,7},{7,6},{8,9},{9,8},{10,11... | collective-permute-start | bytes 2359304 | tf_op jit(solution)/shard_map/ppermute | solution.py:175
  40.9 0.0 collective-permute-done.3.refs_0_
  40.9 0.0 copy-start.2
  40.9 0.0 copy-start.3
  40.9 1.4 %collective-permute-start.4 = (bf16[128,2048]{1,0:T(8,128)(2,1)S(1)}, bf16[128,2048]{1,0:T(8,128)(2,1)S(1)}, u32[]{:S(2)}, u32[]{:S(2)}) collective-permute-start(bf16[128,2048]{1,0:T(8,128)(2,1)S(1)} %hold.6), channel_id=1, source_target_pairs={{0,224},{256,480},{1,225},{257,481},{2,226},{258,482},{3,227},{259... | collective-permute-start | bytes 1572872 | tf_op jit(solution)/shard_map/ppermute | solution.py:177
  42.4 0.7 collective-permute-done.7.refs_7_.refs_8_
  43.1 8.5 %attention_backward.2 = (bf16[128,4096]{1,0:T(8,128)(2,1)}, f32[2,384,512]{2,1,0:T(8,128)S(1)}, bf16[2,384,512]{2,1,0:T(8,128)(2,1)S(1)}, bf16[2,128,512]{2,1,0:T(8,128)(2,1)S(1)}) custom-call(s32[1,7]{1,0:T(1,128)S(1)} %copy-done.3, bf16[128,4096]{1,0:T(8,128)(2,1)S(1)} %bitcast.7, bf16[128,2048]{1,0:T(8,128)(2,1)S(1)} %get-tuple-element.25.refs_2_, ...), custom_call_target="tpu_custom_call" | custom-call | flops 2147483648 | bytes 2097152 | tf_op jit(solution)/shard_map/attention_backward/pallas_call | solution.py:79
  51.6 6.9 %collective-permute-done.4.refs_3_ = bf16[128,2048]{1,0:T(8,128)(2,1)S(1)} collective-permute-done((bf16[128,2048]{1,0:T(8,128)(2,1)S(1)}, bf16[128,2048]{1,0:T(8,128)(2,1)S(1)}, u32[]{:S(2)}, u32[]{:S(2)}) %collective-permute-start.4) | collective-permute-done | bytes 524320 | tf_op jit(solution)/shard_map/ppermute | solution.py:177
  58.5 8.5 %attention_backward.3 = (bf16[128,4096]{1,0:T(8,128)(2,1)}, f32[2,384,512]{2,1,0:T(8,128)S(1)}, bf16[2,384,512]{2,1,0:T(8,128)(2,1)S(1)}, bf16[2,128,512]{2,1,0:T(8,128)(2,1)S(1)}) custom-call(s32[1,7]{1,0:T(1,128)S(1)} %copy-done.3, bf16[128,4096]{1,0:T(8,128)(2,1)S(1)} %bitcast.8, ...), custom_call_target="tpu_custom_call", output_to_operand_aliasing={{0}: (9, {}), {1}: (10, {}), {2}: (11, {}), {3}: (12, {})} | custom-call | flops 2147483648 | bytes 2097152 | tf_op jit(solution)/shard_map/attention_backward/pallas_call | solution.py:79
  67.0 1.9 %collective-permute-start.8 = (bf16[2,384,512]{2,1,0:T(8,128)(2,1)S(1)}, bf16[2,384,512]{2,1,0:T(8,128)(2,1)S(1)}, u32[]{:S(2)}, u32[]{:S(2)}) collective-permute-start(bf16[2,384,512]{2,1,0:T(8,128)(2,1)S(1)} %get-tuple-element.32), channel_id=1, source_target_pairs={{0,1},{1,0},{2,3},{3,2},{4,5},{5,4},{6,7},{7,6},{8,9},{9,8},{10,11... | collective-permute-start | bytes 2359304 | tf_op jit(solution)/shard_map/ppermute | solution.py:184
  68.9 1.9 %collective-permute-start.9 = (bf16[2,128,512]{2,1,0:T(8,128)(2,1)S(1)}, bf16[2,128,512]{2,1,0:T(8,128)(2,1)S(1)}, u32[]{:S(2)}, u32[]{:S(2)}) collective-permute-start(bf16[2,128,512]{2,1,0:T(8,128)(2,1)S(1)} %get-tuple-element.33), channel_id=1, source_target_pairs={{1,4},{3,6},{4,1},{5,8},{6,3},{7,10},{8,5},{9,12},{10,7},{11,14},{... | collective-permute-start | bytes 786440 | tf_op jit(solution)/shard_map/ppermute | solution.py:183
  70.8 0.3 collective-permute-done.8
  71.1 0.3 fusion.3
  71.5 7.5 %collective-permute-start.11 = (bf16[2,128,512]{2,1,0:T(8,128)(2,1)S(1)}, bf16[2,128,512]{2,1,0:T(8,128)(2,1)S(1)}, u32[]{:S(2)}, u32[]{:S(2)}) collective-permute-start(bf16[2,128,512]{2,1,0:T(8,128)(2,1)S(1)} %get-tuple-element.41), channel_id=1, source_target_pairs={{0,2},{1,3},{2,4},{3,5},{4,6},{5,7},{6,8},{7,9},{8,10},{9,11},{10,... | collective-permute-start | bytes 786440 | tf_op jit(solution)/shard_map/ppermute | solution.py:188
  79.0 1.9 %collective-permute-start.10 = (bf16[2,128,512]{2,1,0:T(8,128)(2,1)S(1)}, bf16[2,128,512]{2,1,0:T(8,128)(2,1)S(1)}, u32[]{:S(2)}, u32[]{:S(2)}) collective-permute-start(bf16[2,128,512]{2,1,0:T(8,128)(2,1)S(1)} %get-tuple-element.42), channel_id=1, source_target_pairs={{2,0},{3,1},{4,2},{5,3},{6,4},{7,5},{8,6},{9,7},{10,8},{11,9},{12,... | collective-permute-start | bytes 786440 | tf_op jit(solution)/shard_map/ppermute | solution.py:187
  80.9 0.8 collective-permute-done.9.refs_0_
  81.8 5.4 %collective-permute-done.11.refs_2_ = bf16[2,128,512]{2,1,0:T(8,128)(2,1)S(1)} collective-permute-done((bf16[2,128,512]{2,1,0:T(8,128)(2,1)S(1)}, bf16[2,128,512]{2,1,0:T(8,128)(2,1)S(1)}, u32[]{:S(2)}, u32[]{:S(2)}) %collective-permute-start.11) | collective-permute-done | bytes 262176 | tf_op jit(solution)/shard_map/ppermute | solution.py:188
  87.2 4.8 %collective-permute-done.10.refs_1_ = bf16[2,128,512]{2,1,0:T(8,128)(2,1)S(1)} collective-permute-done((bf16[2,128,512]{2,1,0:T(8,128)(2,1)S(1)}, bf16[2,128,512]{2,1,0:T(8,128)(2,1)S(1)}, u32[]{:S(2)}, u32[]{:S(2)}) %collective-permute-start.10) | collective-permute-done | bytes 262176 | tf_op jit(solution)/shard_map/ppermute | solution.py:187
  92.0 0.2 fusion.2
  92.2 0.7 fusion.6
  (14 shorter events, 0.1 us)
Async XLA Ops:
  0.6 0.9 copy-start
  1.5 0.9 copy-start.1
  2.5 24.4 %collective-permute-start.1 = (bf16[2,128,512]{2,1,0:T(8,128)(2,1)S(1)}, bf16[2,128,512]{2,1,0:T(8,128)(2,1)S(1)}, u32[]{:S(2)}, u32[]{:S(2)}) collective-permute-start(bf16[2,128,512]{2,1,0:T(8,128)(2,1)S(1)} %join.1.own.refs_3_.refs_4_), channel_id=1, source_target_pairs={{2,0},{3,1},{4,2},{5,3},{6,4},{7,5},{8,6},{9,7},{10,8},{11,9},{12,... | collective-permute-start | bytes 786440 | tf_op jit(solution)/shard_map/ppermute | solution.py:167
  5.2 32.3 %collective-permute-start = (bf16[2,128,512]{2,1,0:T(8,128)(2,1)S(1)}, bf16[2,128,512]{2,1,0:T(8,128)(2,1)S(1)}, u32[]{:S(2)}, u32[]{:S(2)}) collective-permute-start(bf16[2,128,512]{2,1,0:T(8,128)(2,1)S(1)} %join.1.own.refs_3_.refs_4_), channel_id=1, source_target_pairs={{0,2},{1,3},{2,4},{3,5},{4,6},{5,7},{6,8},{7,9},{8,10},{9,11},{10,... | collective-permute-start | bytes 786440 | tf_op jit(solution)/shard_map/ppermute | solution.py:166
  12.6 28.2 %collective-permute-start.3 = (bf16[128,2048]{1,0:T(8,128)(2,1)S(1)}, bf16[128,2048]{1,0:T(8,128)(2,1)S(1)}, u32[]{:S(2)}, u32[]{:S(2)}) collective-permute-start(bf16[128,2048]{1,0:T(8,128)(2,1)S(1)} %get-tuple-element.22), channel_id=1, source_target_pairs={{0,256},{256,0},{1,257},{257,1},{2,258},{258,2},{3,259},{259,3},{4... | collective-permute-start | bytes 1572872 | tf_op jit(solution)/shard_map/ppermute | solution.py:173
  13.3 29.0 %collective-permute-start.5 = (bf16[2,128,512]{2,1,0:T(8,128)(2,1)S(1)}, bf16[2,128,512]{2,1,0:T(8,128)(2,1)S(1)}, u32[]{:S(2)}, u32[]{:S(2)}) collective-permute-start(bf16[2,128,512]{2,1,0:T(8,128)(2,1)S(1)} %join.1.own.refs_3_.refs_4_), channel_id=1, source_target_pairs={{1,4},{3,6},{4,1},{5,8},{6,3},{7,10},{8,5},{9,12},{10,7},{11,14},{... | collective-permute-start | bytes 786440 | tf_op jit(solution)/shard_map/ppermute | solution.py:171
  15.3 27.1 %collective-permute-start.6 = (bf16[128,2048]{1,0:T(8,128)(2,1)S(1)}, bf16[128,2048]{1,0:T(8,128)(2,1)S(1)}, u32[]{:S(2)}, u32[]{:S(2)}) collective-permute-start(bf16[128,2048]{1,0:T(8,128)(2,1)S(1)} %get-tuple-element.39), channel_id=1, source_target_pairs={{0,480},{32,0},{64,32},{96,64},{128,96},{160,128},{192,160},{224,1... | collective-permute-start | bytes 1572872 | tf_op jit(solution)/shard_map/ppermute | solution.py:171
  37.6 14.0 %collective-permute-start.2 = (bf16[128,2048]{1,0:T(8,128)(2,1)S(1)}, bf16[128,2048]{1,0:T(8,128)(2,1)S(1)}, u32[]{:S(2)}, u32[]{:S(2)}) collective-permute-start(bf16[128,2048]{1,0:T(8,128)(2,1)S(1)} %get-tuple-element.22), channel_id=1, source_target_pairs={{32,0},{64,32},{96,64},{128,96},{160,128},{192,160},{224,192},{288... | collective-permute-start | bytes 1572872 | tf_op jit(solution)/shard_map/ppermute | solution.py:176
  38.9 4.2 %collective-permute-start.7 = (bf16[2,384,512]{2,1,0:T(8,128)(2,1)S(1)}, bf16[2,384,512]{2,1,0:T(8,128)(2,1)S(1)}, u32[]{:S(2)}, u32[]{:S(2)}) collective-permute-start(bf16[2,384,512]{2,1,0:T(8,128)(2,1)S(1)} %bundle.1), channel_id=1, source_target_pairs={{0,1},{1,0},{2,3},{3,2},{4,5},{5,4},{6,7},{7,6},{8,9},{9,8},{10,11... | collective-permute-start | bytes 2359304 | tf_op jit(solution)/shard_map/ppermute | solution.py:175
  40.9 2.2 %copy-start.2 = (bf16[1,128,4096]{2,1,0:T(8,128)(2,1)S(1)}, bf16[1,128,4096]{2,1,0:T(8,128)(2,1)}, u32[]{:S(2)}) copy-start(bf16[1,128,4096]{2,1,0:T(8,128)(2,1)} %param.5) | copy-start | bytes 3145732
  40.9 2.2 %copy-start.3 = (s32[1,7]{1,0:T(1,128)S(1)}, s32[1,7]{1,0:T(1,128)}, u32[]{:S(2)}) copy-start(s32[1,7]{1,0:T(1,128)} %refs_0_.3) | copy-start | bytes 88
  40.9 17.6 %collective-permute-start.4 = (bf16[128,2048]{1,0:T(8,128)(2,1)S(1)}, bf16[128,2048]{1,0:T(8,128)(2,1)S(1)}, u32[]{:S(2)}, u32[]{:S(2)}) collective-permute-start(bf16[128,2048]{1,0:T(8,128)(2,1)S(1)} %hold.6), channel_id=1, source_target_pairs={{0,224},{256,480},{1,225},{257,481},{2,226},{258,482},{3,227},{259... | collective-permute-start | bytes 1572872 | tf_op jit(solution)/shard_map/ppermute | solution.py:177
  67.0 4.2 %collective-permute-start.8 = (bf16[2,384,512]{2,1,0:T(8,128)(2,1)S(1)}, bf16[2,384,512]{2,1,0:T(8,128)(2,1)S(1)}, u32[]{:S(2)}, u32[]{:S(2)}) collective-permute-start(bf16[2,384,512]{2,1,0:T(8,128)(2,1)S(1)} %get-tuple-element.32), channel_id=1, source_target_pairs={{0,1},{1,0},{2,3},{3,2},{4,5},{5,4},{6,7},{7,6},{8,9},{9,8},{10,11... | collective-permute-start | bytes 2359304 | tf_op jit(solution)/shard_map/ppermute | solution.py:184
  68.9 12.9 %collective-permute-start.9 = (bf16[2,128,512]{2,1,0:T(8,128)(2,1)S(1)}, bf16[2,128,512]{2,1,0:T(8,128)(2,1)S(1)}, u32[]{:S(2)}, u32[]{:S(2)}) collective-permute-start(bf16[2,128,512]{2,1,0:T(8,128)(2,1)S(1)} %get-tuple-element.33), channel_id=1, source_target_pairs={{1,4},{3,6},{4,1},{5,8},{6,3},{7,10},{8,5},{9,12},{10,7},{11,14},{... | collective-permute-start | bytes 786440 | tf_op jit(solution)/shard_map/ppermute | solution.py:183
  71.5 15.7 %collective-permute-start.11 = (bf16[2,128,512]{2,1,0:T(8,128)(2,1)S(1)}, bf16[2,128,512]{2,1,0:T(8,128)(2,1)S(1)}, u32[]{:S(2)}, u32[]{:S(2)}) collective-permute-start(bf16[2,128,512]{2,1,0:T(8,128)(2,1)S(1)} %get-tuple-element.41), channel_id=1, source_target_pairs={{0,2},{1,3},{2,4},{3,5},{4,6},{5,7},{6,8},{7,9},{8,10},{9,11},{10,... | collective-permute-start | bytes 786440 | tf_op jit(solution)/shard_map/ppermute | solution.py:188
  79.0 13.0 %collective-permute-start.10 = (bf16[2,128,512]{2,1,0:T(8,128)(2,1)S(1)}, bf16[2,128,512]{2,1,0:T(8,128)(2,1)S(1)}, u32[]{:S(2)}, u32[]{:S(2)}) collective-permute-start(bf16[2,128,512]{2,1,0:T(8,128)(2,1)S(1)} %get-tuple-element.42), channel_id=1, source_target_pairs={{2,0},{3,1},{4,2},{5,3},{6,4},{7,5},{8,6},{9,7},{10,8},{11,9},{12,... | collective-permute-start | bytes 786440 | tf_op jit(solution)/shard_map/ppermute | solution.py:187

commit v6 on v5

--- a/solution.py
+++ b/solution.py
@@ -10,6 +10,7 @@
 
 HQ, HK, HD, W = 32, 4, 128, 3
 BL = 128
+COLUMNS = 4
 G = HQ // HK
 NS = 2 * W + 1
 SCALE = 1.0 / math.sqrt(HD)
@@ -153,14 +154,30 @@
     return [(i, j) for i, j in ends if 0 <= j < count]
 
 
+def wrap_routes(sections, count):
+    straight, turning, wrapping = [], [], []
+    for i in range(sections):
+        for j in range(count):
+            here, there = i * count + j, (i - 1) % sections * count + j
+            column = j // 2 % COLUMNS
+            if i % (sections // 2) or column not in (0, COLUMNS - 1):
+                straight.append((here, there))
+            else:
+                via = (i + sections // 2) % sections * count + j + (2 if column == 0 else -2)
+                turning.append((here, via))
+                wrapping.append((via, there))
+    return straight, turning, wrapping
+
+
 def shards(query_heads, key_heads, value_heads, section_cotangent, block_mask):
     sections = lax.axis_size("section")
     count = lax.axis_size("seq")
     half = HQ * HD // 2
-    turn = sections // 2
     cot = section_cotangent[0]
     low, high = cot[:, :half], cot[:, half:]
+    straight, turning, wrapping = wrap_routes(sections, count)
     before = [(i, (i - 1) % sections) for i in range(sections)]
+    both = ("section", "seq")
     own = join(key_heads[0], value_heads[0])
     left, right = hold(
         lax.ppermute(own, "seq", shift_pairs(count, 2)),
@@ -168,17 +185,17 @@
         flops=1 << 32,
     )
     far, grad_low = hold(
-        lax.ppermute(own, "seq", far_pairs(count)), lax.ppermute(low, "section", before), flops=1 << 33
-    )
-    (turned,) = hold(lax.ppermute(high, "section", [(0, turn), (turn, 0)]), flops=1 << 33)
+        lax.ppermute(own, "seq", far_pairs(count)), lax.ppermute(low, both, straight), flops=1 << 33
+    )
+    (turned,) = hold(lax.ppermute(low, both, turning), flops=1 << 33)
     joined, high = lax.optimization_barrier((bundle(own, left, right), high))
     mate = lax.ppermute(joined, "seq", mate_pairs(count))
-    grad_high = lax.ppermute(high, "section", [(i, i - 1) for i in range(sections) if i % turn])
-    grad_wrap = lax.ppermute(turned, "section", [(0, turn - 1), (turn, sections - 1)])
+    grad_high = lax.ppermute(high, "section", before)
+    grad_wrap = lax.ppermute(turned, both, wrapping)
     slots = (own, left, right, far, mate)
-    kept = attention_backward(block_mask, query_heads[0], (grad_low,), slots, 0, 2, ())
+    kept = attention_backward(block_mask, query_heads[0], (grad_low, grad_wrap), slots, 0, 2, ())
     query_grad, parts, to_mate, to_far = attention_backward(
-        block_mask, query_heads[0], (grad_high, grad_wrap), slots, 2, 2, kept
+        block_mask, query_heads[0], (grad_high,), slots, 2, 2, kept
     )
     (back_far,) = hold(lax.ppermute(to_far, "seq", far_pairs(count)), flops=1 << 33)
     sums = parts + lax.ppermute(to_mate, "seq", mate_pairs(count)).astype(F32)

time: 93.4 us -> 106 us (1.13)
  the two profiles are of different devices: /device:TPU:318 before, /device:TPU:254 now
where the time goes in v6:
time: 106 us
  waiting for transfers between devices  43.5 us (41%)
  starting transfers between devices  40.1 us (38%)
  Pallas kernels  17.1 us (16%)
  local copies, waits for them, and re-layouts  3.87 us (4%)
    ppermute x1, waiting for transfers between devices, shards(): grad_wrap = lax.ppermute(turned, both, wrapping)  20.2 us
    pallas_call x2, Pallas kernels, attention_backward(): pl.pallas_call(functools.partial(backward_body, len(grads), len(kept)), g...  17 us
    ppermute x1, starting transfers between devices, shards(): lax.ppermute(sums[:, 2 * BL:].astype(B16), 'seq', shift_pairs(count, 2))  11.3 us
    ppermute x1, waiting for transfers between devices, shards(): lax.ppermute(sums[:, BL:2 * BL].astype(B16), 'seq', shift_pairs(count, -2))  11.1 us
    ppermute x1, starting transfers between devices, shards(): lax.ppermute(own, 'seq', shift_pairs(count, 2))  7.32 us
    ppermute x1, waiting for transfers between devices, shards(): lax.ppermute(sums[:, 2 * BL:].astype(B16), 'seq', shift_pairs(count, 2))  6.9 us
    ppermute x1, waiting for transfers between devices, shards(): lax.ppermute(own, 'seq', shift_pairs(count, 2))  5.26 us
    ppermute x1, starting transfers between devices, shards(): lax.ppermute(low, both, straight)  3.29 us
  transfers between devices with their start and end apart: 12, of which 4 were waited for; matrix products, arithmetic and copies ran while one was open for 2% of the time, Pallas kernels for 8%

profile of v6, /device:TPU:254, one launch (start us, length us, event | category | flops | bytes accessed | tf_op | source)
XLA Modules:
  0.0 105.9 jit_solution(14580889994531307297)
XLA Ops:
  0.6 0.9 copy-done
  1.5 0.9 copy-done.1
  2.5 2.7 %collective-permute-start.1 = (bf16[2,128,512]{2,1,0:T(8,128)(2,1)S(1)}, bf16[2,128,512]{2,1,0:T(8,128)(2,1)S(1)}, u32[]{:S(2)}, u32[]{:S(2)}) collective-permute-start(bf16[2,128,512]{2,1,0:T(8,128)(2,1)S(1)} %join.1.own.refs_4_.refs_3_), channel_id=1, source_target_pairs={{2,0},{3,1},{4,2},{5,3},{6,4},{7,5},{8,6},{9,7},{10,8},{11,9},{12,... | collective-permute-start | bytes 786440 | tf_op jit(solution)/shard_map/ppermute | solution.py:184
  5.2 7.3 %collective-permute-start = (bf16[2,128,512]{2,1,0:T(8,128)(2,1)S(1)}, bf16[2,128,512]{2,1,0:T(8,128)(2,1)S(1)}, u32[]{:S(2)}, u32[]{:S(2)}) collective-permute-start(bf16[2,128,512]{2,1,0:T(8,128)(2,1)S(1)} %join.1.own.refs_4_.refs_3_), channel_id=1, source_target_pairs={{0,2},{1,3},{2,4},{3,5},{4,6},{5,7},{6,8},{7,9},{8,10},{9,11},{10,... | collective-permute-start | bytes 786440 | tf_op jit(solution)/shard_map/ppermute | solution.py:183
  12.5 1.3 %fusion.4 = (bf16[128,2048]{1,0:T(8,128)(2,1)S(1)}, bf16[128,2048]{1,0:T(8,128)(2,1)S(1)}) fusion(bf16[128,4096]{1,0:T(8,128)(2,1)} %bitcast.9), kind=kLoop, calls=%fused_computation.6 | loop fusion | bytes 2097152 | tf_op jit(solution)/shard_map/slice | solution.py:177
  13.8 0.7 collective-permute-start.6
  14.5 1.9 %collective-permute-start.3 = (bf16[2,128,512]{2,1,0:T(8,128)(2,1)S(1)}, bf16[2,128,512]{2,1,0:T(8,128)(2,1)S(1)}, u32[]{:S(2)}, u32[]{:S(2)}) collective-permute-start(bf16[2,128,512]{2,1,0:T(8,128)(2,1)S(1)} %join.1.own.refs_4_.refs_3_), channel_id=1, source_target_pairs={{1,4},{3,6},{4,1},{5,8},{6,3},{7,10},{8,5},{9,12},{10,7},{11,14},{... | collective-permute-start | bytes 786440 | tf_op jit(solution)/shard_map/ppermute | solution.py:188
  16.5 3.3 %collective-permute-start.4 = (bf16[128,2048]{1,0:T(8,128)(2,1)S(1)}, bf16[128,2048]{1,0:T(8,128)(2,1)S(1)}, u32[]{:S(2)}, u32[]{:S(2)}) collective-permute-start(bf16[128,2048]{1,0:T(8,128)(2,1)S(1)} %get-tuple-element.39), channel_id=1, source_target_pairs={{2,482},{3,483},{4,484},{5,485},{10,490},{11,491},{12,492},{13,493... | collective-permute-start | bytes 1572872 | tf_op jit(solution)/shard_map/ppermute | solution.py:188
  19.8 0.0 collective-permute-done.1.refs_1_
  19.8 5.3 %collective-permute-done.refs_0_ = bf16[2,128,512]{2,1,0:T(8,128)(2,1)S(1)} collective-permute-done((bf16[2,128,512]{2,1,0:T(8,128)(2,1)S(1)}, bf16[2,128,512]{2,1,0:T(8,128)(2,1)S(1)}, u32[]{:S(2)}, u32[]{:S(2)}) %collective-permute-start) | collective-permute-done | bytes 262176 | tf_op jit(solution)/shard_map/ppermute | solution.py:183
  25.0 0.1 bundle.1
  25.1 3.3 %collective-permute-start.2 = (bf16[128,2048]{1,0:T(8,128)(2,1)S(1)}, bf16[128,2048]{1,0:T(8,128)(2,1)S(1)}, u32[]{:S(2)}, u32[]{:S(2)}) collective-permute-start(bf16[128,2048]{1,0:T(8,128)(2,1)S(1)} %get-tuple-element.22), channel_id=1, source_target_pairs={{0,480},{32,0},{64,32},{96,64},{128,96},{160,128},{192,160},{224,1... | collective-permute-start | bytes 1572872 | tf_op jit(solution)/shard_map/ppermute | solution.py:193
  28.4 1.9 %collective-permute-start.5 = (bf16[2,384,512]{2,1,0:T(8,128)(2,1)S(1)}, bf16[2,384,512]{2,1,0:T(8,128)(2,1)S(1)}, u32[]{:S(2)}, u32[]{:S(2)}) collective-permute-start(bf16[2,384,512]{2,1,0:T(8,128)(2,1)S(1)} %bundle.1), channel_id=1, source_target_pairs={{0,1},{1,0},{2,3},{3,2},{4,5},{5,4},{6,7},{7,6},{8,9},{9,8},{10,11... | collective-permute-start | bytes 2359304 | tf_op jit(solution)/shard_map/ppermute | solution.py:192
  30.3 0.0 copy-start.2
  30.3 0.0 copy-start.3
  30.3 1.4 %collective-permute-start.7 = (bf16[128,2048]{1,0:T(8,128)(2,1)S(1)}, bf16[128,2048]{1,0:T(8,128)(2,1)S(1)}, u32[]{:S(2)}, u32[]{:S(2)}) collective-permute-start(bf16[128,2048]{1,0:T(8,128)(2,1)S(1)} %hold.7), channel_id=1, source_target_pairs={{258,480},{259,481},{260,486},{261,487},{266,488},{267,489},{268,4... | collective-permute-start | bytes 1572872 | tf_op jit(solution)/shard_map/ppermute | solution.py:194
  31.8 0.0 collective-permute-done.3.refs_0_
  31.8 0.0 collective-permute-done.4.refs_1_
  31.8 20.2 %collective-permute-done.7.refs_3_ = bf16[128,2048]{1,0:T(8,128)(2,1)S(1)} collective-permute-done((bf16[128,2048]{1,0:T(8,128)(2,1)S(1)}, bf16[128,2048]{1,0:T(8,128)(2,1)S(1)}, u32[]{:S(2)}, u32[]{:S(2)}) %collective-permute-start.7) | collective-permute-done | bytes 524320 | tf_op jit(solution)/shard_map/ppermute | solution.py:194
  52.0 8.5 %attention_backward.2 = (bf16[128,4096]{1,0:T(8,128)(2,1)}, f32[2,384,512]{2,1,0:T(8,128)S(1)}, bf16[2,384,512]{2,1,0:T(8,128)(2,1)S(1)}, bf16[2,128,512]{2,1,0:T(8,128)(2,1)S(1)}) custom-call(s32[1,7]{1,0:T(1,128)S(1)} %copy-done.3, bf16[128,4096]{1,0:T(8,128)(2,1)S(1)} %bitcast.7, bf16[128,2048]{1,0:T(8,128)(2,1)S(1)} %get-tuple-element.25.refs_2_, ...), custom_call_target="tpu_custom_call" | custom-call | flops 2147483648 | bytes 2097152 | tf_op jit(solution)/shard_map/attention_backward/pallas_call | solution.py:80
  60.5 0.0 collective-permute-done.2.refs_2_
  60.5 8.5 %attention_backward.3 = (bf16[128,4096]{1,0:T(8,128)(2,1)}, f32[2,384,512]{2,1,0:T(8,128)S(1)}, bf16[2,384,512]{2,1,0:T(8,128)(2,1)S(1)}, bf16[2,128,512]{2,1,0:T(8,128)(2,1)S(1)}) custom-call(s32[1,7]{1,0:T(1,128)S(1)} %copy-done.3, bf16[128,4096]{1,0:T(8,128)(2,1)S(1)} %bitcast.8, ...), custom_call_target="tpu_custom_call", output_to_operand_aliasing={{0}: (8, {}), {1}: (9, {}), {2}: (10, {}), {3}: (11, {})} | custom-call | flops 2147483648 | bytes 2097152 | tf_op jit(solution)/shard_map/attention_backward/pallas_call | solution.py:80
  69.0 2.4 %collective-permute-start.8 = (bf16[2,384,512]{2,1,0:T(8,128)(2,1)S(1)}, bf16[2,384,512]{2,1,0:T(8,128)(2,1)S(1)}, u32[]{:S(2)}, u32[]{:S(2)}) collective-permute-start(bf16[2,384,512]{2,1,0:T(8,128)(2,1)S(1)} %get-tuple-element.32), channel_id=1, source_target_pairs={{0,1},{1,0},{2,3},{3,2},{4,5},{5,4},{6,7},{7,6},{8,9},{9,8},{10,11... | collective-permute-start | bytes 2359304 | tf_op jit(solution)/shard_map/ppermute | solution.py:201
  71.4 1.9 %collective-permute-start.9 = (bf16[2,128,512]{2,1,0:T(8,128)(2,1)S(1)}, bf16[2,128,512]{2,1,0:T(8,128)(2,1)S(1)}, u32[]{:S(2)}, u32[]{:S(2)}) collective-permute-start(bf16[2,128,512]{2,1,0:T(8,128)(2,1)S(1)} %get-tuple-element.33), channel_id=1, source_target_pairs={{1,4},{3,6},{4,1},{5,8},{6,3},{7,10},{8,5},{9,12},{10,7},{11,14},{... | collective-permute-start | bytes 786440 | tf_op jit(solution)/shard_map/ppermute | solution.py:200
  73.3 0.0 collective-permute-done.8
  73.3 0.3 fusion.3
  73.7 11.3 %collective-permute-start.11 = (bf16[2,128,512]{2,1,0:T(8,128)(2,1)S(1)}, bf16[2,128,512]{2,1,0:T(8,128)(2,1)S(1)}, u32[]{:S(2)}, u32[]{:S(2)}) collective-permute-start(bf16[2,128,512]{2,1,0:T(8,128)(2,1)S(1)} %get-tuple-element.41), channel_id=1, source_target_pairs={{0,2},{1,3},{2,4},{3,5},{4,6},{5,7},{6,8},{7,9},{8,10},{9,11},{10,... | collective-permute-start | bytes 786440 | tf_op jit(solution)/shard_map/ppermute | solution.py:205
  85.0 1.9 %collective-permute-start.10 = (bf16[2,128,512]{2,1,0:T(8,128)(2,1)S(1)}, bf16[2,128,512]{2,1,0:T(8,128)(2,1)S(1)}, u32[]{:S(2)}, u32[]{:S(2)}) collective-permute-start(bf16[2,128,512]{2,1,0:T(8,128)(2,1)S(1)} %get-tuple-element.42), channel_id=1, source_target_pairs={{2,0},{3,1},{4,2},{5,3},{6,4},{7,5},{8,6},{9,7},{10,8},{11,9},{12,... | collective-permute-start | bytes 786440 | tf_op jit(solution)/shard_map/ppermute | solution.py:204
  87.0 6.9 %collective-permute-done.11.refs_2_ = bf16[2,128,512]{2,1,0:T(8,128)(2,1)S(1)} collective-permute-done((bf16[2,128,512]{2,1,0:T(8,128)(2,1)S(1)}, bf16[2,128,512]{2,1,0:T(8,128)(2,1)S(1)}, u32[]{:S(2)}, u32[]{:S(2)}) %collective-permute-start.11) | collective-permute-done | bytes 262176 | tf_op jit(solution)/shard_map/ppermute | solution.py:205
  93.9 11.1 %collective-permute-done.10.refs_1_ = bf16[2,128,512]{2,1,0:T(8,128)(2,1)S(1)} collective-permute-done((bf16[2,128,512]{2,1,0:T(8,128)(2,1)S(1)}, bf16[2,128,512]{2,1,0:T(8,128)(2,1)S(1)}, u32[]{:S(2)}, u32[]{:S(2)}) %collective-permute-start.10) | collective-permute-done | bytes 262176 | tf_op jit(solution)/shard_map/ppermute | solution.py:204
  105.0 0.2 fusion.2
  105.2 0.7 fusion.6
  (14 shorter events, 0.1 us)
Async XLA Ops:
  0.6 0.9 copy-start
  1.5 0.9 copy-start.1
  2.5 17.3 %collective-permute-start.1 = (bf16[2,128,512]{2,1,0:T(8,128)(2,1)S(1)}, bf16[2,128,512]{2,1,0:T(8,128)(2,1)S(1)}, u32[]{:S(2)}, u32[]{:S(2)}) collective-permute-start(bf16[2,128,512]{2,1,0:T(8,128)(2,1)S(1)} %join.1.own.refs_4_.refs_3_), channel_id=1, source_target_pairs={{2,0},{3,1},{4,2},{5,3},{6,4},{7,5},{8,6},{9,7},{10,8},{11,9},{12,... | collective-permute-start | bytes 786440 | tf_op jit(solution)/shard_map/ppermute | solution.py:184
  5.2 19.8 %collective-permute-start = (bf16[2,128,512]{2,1,0:T(8,128)(2,1)S(1)}, bf16[2,128,512]{2,1,0:T(8,128)(2,1)S(1)}, u32[]{:S(2)}, u32[]{:S(2)}) collective-permute-start(bf16[2,128,512]{2,1,0:T(8,128)(2,1)S(1)} %join.1.own.refs_4_.refs_3_), channel_id=1, source_target_pairs={{0,2},{1,3},{2,4},{3,5},{4,6},{5,7},{6,8},{7,9},{8,10},{9,11},{10,... | collective-permute-start | bytes 786440 | tf_op jit(solution)/shard_map/ppermute | solution.py:183
  13.8 16.4 %collective-permute-start.6 = (bf16[128,2048]{1,0:T(8,128)(2,1)S(1)}, bf16[128,2048]{1,0:T(8,128)(2,1)S(1)}, u32[]{:S(2)}, u32[]{:S(2)}) collective-permute-start(bf16[128,2048]{1,0:T(8,128)(2,1)S(1)} %get-tuple-element.39), channel_id=1, source_target_pairs={{0,258},{1,259},{6,260},{7,261},{8,266},{9,267},{14,268},{15,269},... | collective-permute-start | bytes 1572872 | tf_op jit(solution)/shard_map/ppermute | solution.py:190
  14.5 17.2 %collective-permute-start.3 = (bf16[2,128,512]{2,1,0:T(8,128)(2,1)S(1)}, bf16[2,128,512]{2,1,0:T(8,128)(2,1)S(1)}, u32[]{:S(2)}, u32[]{:S(2)}) collective-permute-start(bf16[2,128,512]{2,1,0:T(8,128)(2,1)S(1)} %join.1.own.refs_4_.refs_3_), channel_id=1, source_target_pairs={{1,4},{3,6},{4,1},{5,8},{6,3},{7,10},{8,5},{9,12},{10,7},{11,14},{... | collective-permute-start | bytes 786440 | tf_op jit(solution)/shard_map/ppermute | solution.py:188
  16.5 15.3 %collective-permute-start.4 = (bf16[128,2048]{1,0:T(8,128)(2,1)S(1)}, bf16[128,2048]{1,0:T(8,128)(2,1)S(1)}, u32[]{:S(2)}, u32[]{:S(2)}) collective-permute-start(bf16[128,2048]{1,0:T(8,128)(2,1)S(1)} %get-tuple-element.39), channel_id=1, source_target_pairs={{2,482},{3,483},{4,484},{5,485},{10,490},{11,491},{12,492},{13,493... | collective-permute-start | bytes 1572872 | tf_op jit(solution)/shard_map/ppermute | solution.py:188
  25.1 35.4 %collective-permute-start.2 = (bf16[128,2048]{1,0:T(8,128)(2,1)S(1)}, bf16[128,2048]{1,0:T(8,128)(2,1)S(1)}, u32[]{:S(2)}, u32[]{:S(2)}) collective-permute-start(bf16[128,2048]{1,0:T(8,128)(2,1)S(1)} %get-tuple-element.22), channel_id=1, source_target_pairs={{0,480},{32,0},{64,32},{96,64},{128,96},{160,128},{192,160},{224,1... | collective-permute-start | bytes 1572872 | tf_op jit(solution)/shard_map/ppermute | solution.py:193
  28.4 23.6 %collective-permute-start.5 = (bf16[2,384,512]{2,1,0:T(8,128)(2,1)S(1)}, bf16[2,384,512]{2,1,0:T(8,128)(2,1)S(1)}, u32[]{:S(2)}, u32[]{:S(2)}) collective-permute-start(bf16[2,384,512]{2,1,0:T(8,128)(2,1)S(1)} %bundle.1), channel_id=1, source_target_pairs={{0,1},{1,0},{2,3},{3,2},{4,5},{5,4},{6,7},{7,6},{8,9},{9,8},{10,11... | collective-permute-start | bytes 2359304 | tf_op jit(solution)/shard_map/ppermute | solution.py:192
  30.3 21.7 %copy-start.2 = (bf16[1,128,4096]{2,1,0:T(8,128)(2,1)S(1)}, bf16[1,128,4096]{2,1,0:T(8,128)(2,1)}, u32[]{:S(2)}) copy-start(bf16[1,128,4096]{2,1,0:T(8,128)(2,1)} %param.5) | copy-start | bytes 3145732
  30.3 21.7 %copy-start.3 = (s32[1,7]{1,0:T(1,128)S(1)}, s32[1,7]{1,0:T(1,128)}, u32[]{:S(2)}) copy-start(s32[1,7]{1,0:T(1,128)} %refs_0_.3) | copy-start | bytes 88
  30.3 21.7 %collective-permute-start.7 = (bf16[128,2048]{1,0:T(8,128)(2,1)S(1)}, bf16[128,2048]{1,0:T(8,128)(2,1)S(1)}, u32[]{:S(2)}, u32[]{:S(2)}) collective-permute-start(bf16[128,2048]{1,0:T(8,128)(2,1)S(1)} %hold.7), channel_id=1, source_target_pairs={{258,480},{259,481},{260,486},{261,487},{266,488},{267,489},{268,4... | collective-permute-start | bytes 1572872 | tf_op jit(solution)/shard_map/ppermute | solution.py:194
  69.0 4.3 %collective-permute-start.8 = (bf16[2,384,512]{2,1,0:T(8,128)(2,1)S(1)}, bf16[2,384,512]{2,1,0:T(8,128)(2,1)S(1)}, u32[]{:S(2)}, u32[]{:S(2)}) collective-permute-start(bf16[2,384,512]{2,1,0:T(8,128)(2,1)S(1)} %get-tuple-element.32), channel_id=1, source_target_pairs={{0,1},{1,0},{2,3},{3,2},{4,5},{5,4},{6,7},{7,6},{8,9},{9,8},{10,11... | collective-permute-start | bytes 2359304 | tf_op jit(solution)/shard_map/ppermute | solution.py:201
  71.4 15.6 %collective-permute-start.9 = (bf16[2,128,512]{2,1,0:T(8,128)(2,1)S(1)}, bf16[2,128,512]{2,1,0:T(8,128)(2,1)S(1)}, u32[]{:S(2)}, u32[]{:S(2)}) collective-permute-start(bf16[2,128,512]{2,1,0:T(8,128)(2,1)S(1)} %get-tuple-element.33), channel_id=1, source_target_pairs={{1,4},{3,6},{4,1},{5,8},{6,3},{7,10},{8,5},{9,12},{10,7},{11,14},{... | collective-permute-start | bytes 786440 | tf_op jit(solution)/shard_map/ppermute | solution.py:200
  73.7 20.2 %collective-permute-start.11 = (bf16[2,128,512]{2,1,0:T(8,128)(2,1)S(1)}, bf16[2,128,512]{2,1,0:T(8,128)(2,1)S(1)}, u32[]{:S(2)}, u32[]{:S(2)}) collective-permute-start(bf16[2,128,512]{2,1,0:T(8,128)(2,1)S(1)} %get-tuple-element.41), channel_id=1, source_target_pairs={{0,2},{1,3},{2,4},{3,5},{4,6},{5,7},{6,8},{7,9},{8,10},{9,11},{10,... | collective-permute-start | bytes 786440 | tf_op jit(solution)/shard_map/ppermute | solution.py:205
  85.0 20.0 %collective-permute-start.10 = (bf16[2,128,512]{2,1,0:T(8,128)(2,1)S(1)}, bf16[2,128,512]{2,1,0:T(8,128)(2,1)S(1)}, u32[]{:S(2)}, u32[]{:S(2)}) collective-permute-start(bf16[2,128,512]{2,1,0:T(8,128)(2,1)S(1)} %get-tuple-element.42), channel_id=1, source_target_pairs={{2,0},{3,1},{4,2},{5,3},{6,4},{7,5},{8,6},{9,7},{10,8},{11,9},{12,... | collective-permute-start | bytes 786440 | tf_op jit(solution)/shard_map/ppermute | solution.py:204

commit v7 on v6

--- a/solution.py
+++ b/solution.py
@@ -185,17 +185,17 @@
         flops=1 << 32,
     )
     far, grad_low = hold(
-        lax.ppermute(own, "seq", far_pairs(count)), lax.ppermute(low, both, straight), flops=1 << 33
-    )
-    (turned,) = hold(lax.ppermute(low, both, turning), flops=1 << 33)
-    joined, high = lax.optimization_barrier((bundle(own, left, right), high))
+        lax.ppermute(own, "seq", far_pairs(count)), lax.ppermute(low, "section", before), flops=1 << 33
+    )
+    (turned,) = hold(lax.ppermute(high, both, turning), flops=1 << 33)
+    joined, late = lax.optimization_barrier((bundle(own, left, right), high))
     mate = lax.ppermute(joined, "seq", mate_pairs(count))
-    grad_high = lax.ppermute(high, "section", before)
+    grad_high = lax.ppermute(late, both, straight)
     grad_wrap = lax.ppermute(turned, both, wrapping)
     slots = (own, left, right, far, mate)
-    kept = attention_backward(block_mask, query_heads[0], (grad_low, grad_wrap), slots, 0, 2, ())
+    kept = attention_backward(block_mask, query_heads[0], (grad_low,), slots, 0, 2, ())
     query_grad, parts, to_mate, to_far = attention_backward(
-        block_mask, query_heads[0], (grad_high,), slots, 2, 2, kept
+        block_mask, query_heads[0], (grad_high, grad_wrap), slots, 2, 2, kept
     )
     (back_far,) = hold(lax.ppermute(to_far, "seq", far_pairs(count)), flops=1 << 33)
     sums = parts + lax.ppermute(to_mate, "seq", mate_pairs(count)).astype(F32)

time: 106 us -> 100 us (0.943)
  waiting for transfers between devices: 43.5 us -> 35.6 us
  starting transfers between devices: 40.1 us -> 41.8 us
    ppermute x1, waiting for transfers between devices: 20.2 us -> 4.33 us  [shards(): grad_wrap = lax.ppermute(turned, both, wrapping)]
    ppermute x1, starting transfers between devices: 11.3 us -> 2.75 us  [shards(): lax.ppermute(sums[:, 2 * BL:].astype(B16), 'seq', shift_pairs(count, 2))]
    ppermute x1, starting transfers between devices: 2.39 us -> 10.9 us  [shards(): sums = parts + lax.ppermute(to_mate, 'seq', mate_pairs(count)).astype(F32)]
    ppermute x3, waiting for transfers between devices: 0.02 us -> 7.34 us  [the longest x1 7.33 us: shards(): lax.ppermute(low, 'section', before)]
    ppermute x1, waiting for transfers between devices: 6.9 us -> 3.02 us  [shards(): lax.ppermute(sums[:, 2 * BL:].astype(B16), 'seq', shift_pairs(count, 2))]
    ppermute x1, waiting for transfers between devices: 0.01 us -> 2.72 us  [shards(): lax.ppermute(to_far, 'seq', far_pairs(count))]
    ppermute x1, waiting for transfers between devices: 11.1 us -> 13.4 us  [shards(): lax.ppermute(sums[:, BL:2 * BL].astype(B16), 'seq', shift_pairs(count, -2))]
    ppermute x1, starting transfers between devices: 1.92 us -> 3.1 us  [shards(): lax.ppermute(sums[:, BL:2 * BL].astype(B16), 'seq', shift_pairs(count, -2))]
  transfers between devices with their start and end apart: 12 -> 12, of which waited for: 4 -> 6; matrix products, arithmetic and copies ran while one was open for 2% -> 2% of each run, Pallas kernels for 8% -> 9%
where the time goes in v7:
time: 100 us; the launch traced here: 99.6 us
  starting transfers between devices  41.8 us (42%)
  waiting for transfers between devices  35.6 us (36%)
  Pallas kernels  17.1 us (17%)
  local copies, waits for them, and re-layouts  3.87 us (4%)
    pallas_call x2, Pallas kernels, attention_backward(): pl.pallas_call(functools.partial(backward_body, len(grads), len(kept)), g...  17 us
    ppermute x1, waiting for transfers between devices, shards(): lax.ppermute(sums[:, BL:2 * BL].astype(B16), 'seq', shift_pairs(count, -2))  13.4 us
    ppermute x1, starting transfers between devices, shards(): sums = parts + lax.ppermute(to_mate, 'seq', mate_pairs(count)).astype(F32)  10.9 us
    ppermute x1, waiting for transfers between devices, shards(): lax.ppermute(low, 'section', before)  7.33 us
    ppermute x1, starting transfers between devices, shards(): lax.ppermute(own, 'seq', shift_pairs(count, 2))  7.32 us
    ppermute x1, waiting for transfers between devices, shards(): lax.ppermute(own, 'seq', shift_pairs(count, 2))  4.74 us
    ppermute x1, waiting for transfers between devices, shards(): grad_wrap = lax.ppermute(turned, both, wrapping)  4.33 us
    ppermute x1, starting transfers between devices, shards(): grad_high = lax.ppermute(late, both, straight)  3.83 us
  transfers between devices with their start and end apart: 12, of which 6 were waited for; matrix products, arithmetic and copies ran while one was open for 2% of the time, Pallas kernels for 9%

profile of v7, /device:TPU:254, one launch (start us, length us, event | category | flops | bytes accessed | tf_op | source)
XLA Modules:
  0.0 99.6 jit_solution(7452184715734311268)
XLA Ops:
  0.6 0.9 copy-done
  1.5 0.9 copy-done.1
  2.5 2.7 %collective-permute-start.1 = (bf16[2,128,512]{2,1,0:T(8,128)(2,1)S(1)}, bf16[2,128,512]{2,1,0:T(8,128)(2,1)S(1)}, u32[]{:S(2)}, u32[]{:S(2)}) collective-permute-start(bf16[2,128,512]{2,1,0:T(8,128)(2,1)S(1)} %join.1.own.refs_3_.refs_4_), channel_id=1, source_target_pairs={{2,0},{3,1},{4,2},{5,3},{6,4},{7,5},{8,6},{9,7},{10,8},{11,9},{12,... | collective-permute-start | bytes 786440 | tf_op jit(solution)/shard_map/ppermute | solution.py:184
  5.2 7.3 %collective-permute-start = (bf16[2,128,512]{2,1,0:T(8,128)(2,1)S(1)}, bf16[2,128,512]{2,1,0:T(8,128)(2,1)S(1)}, u32[]{:S(2)}, u32[]{:S(2)}) collective-permute-start(bf16[2,128,512]{2,1,0:T(8,128)(2,1)S(1)} %join.1.own.refs_3_.refs_4_), channel_id=1, source_target_pairs={{0,2},{1,3},{2,4},{3,5},{4,6},{5,7},{6,8},{7,9},{8,10},{9,11},{10,... | collective-permute-start | bytes 786440 | tf_op jit(solution)/shard_map/ppermute | solution.py:183
  12.5 1.3 %fusion.4 = (bf16[128,2048]{1,0:T(8,128)(2,1)S(1)}, bf16[128,2048]{1,0:T(8,128)(2,1)S(1)}) fusion(bf16[128,4096]{1,0:T(8,128)(2,1)} %bitcast.9), kind=kLoop, calls=%fused_computation.6 | loop fusion | bytes 2097152 | tf_op jit(solution)/shard_map/slice | solution.py:177
  13.8 0.7 collective-permute-start.3
  14.5 1.9 %collective-permute-start.5 = (bf16[2,128,512]{2,1,0:T(8,128)(2,1)S(1)}, bf16[2,128,512]{2,1,0:T(8,128)(2,1)S(1)}, u32[]{:S(2)}, u32[]{:S(2)}) collective-permute-start(bf16[2,128,512]{2,1,0:T(8,128)(2,1)S(1)} %join.1.own.refs_3_.refs_4_), channel_id=1, source_target_pairs={{1,4},{3,6},{4,1},{5,8},{6,3},{7,10},{8,5},{9,12},{10,7},{11,14},{... | collective-permute-start | bytes 786440 | tf_op jit(solution)/shard_map/ppermute | solution.py:188
  16.5 3.3 %collective-permute-start.6 = (bf16[128,2048]{1,0:T(8,128)(2,1)S(1)}, bf16[128,2048]{1,0:T(8,128)(2,1)S(1)}, u32[]{:S(2)}, u32[]{:S(2)}) collective-permute-start(bf16[128,2048]{1,0:T(8,128)(2,1)S(1)} %get-tuple-element.39), channel_id=1, source_target_pairs={{0,480},{32,0},{64,32},{96,64},{128,96},{160,128},{192,160},{224,1... | collective-permute-start | bytes 1572872 | tf_op jit(solution)/shard_map/ppermute | solution.py:188
  19.7 0.0 collective-permute-done.1.refs_1_
  19.8 4.7 %collective-permute-done.refs_0_ = bf16[2,128,512]{2,1,0:T(8,128)(2,1)S(1)} collective-permute-done((bf16[2,128,512]{2,1,0:T(8,128)(2,1)S(1)}, bf16[2,128,512]{2,1,0:T(8,128)(2,1)S(1)}, u32[]{:S(2)}, u32[]{:S(2)}) %collective-permute-start) | collective-permute-done | bytes 262176 | tf_op jit(solution)/shard_map/ppermute | solution.py:183
  24.5 0.1 bundle.1
  24.5 3.8 %collective-permute-start.2 = (bf16[128,2048]{1,0:T(8,128)(2,1)S(1)}, bf16[128,2048]{1,0:T(8,128)(2,1)S(1)}, u32[]{:S(2)}, u32[]{:S(2)}) collective-permute-start(bf16[128,2048]{1,0:T(8,128)(2,1)S(1)} %get-tuple-element.22), channel_id=1, source_target_pairs={{2,482},{3,483},{4,484},{5,485},{10,490},{11,491},{12,492},{13,493... | collective-permute-start | bytes 1572872 | tf_op jit(solution)/shard_map/ppermute | solution.py:193
  28.4 1.9 %collective-permute-start.7 = (bf16[2,384,512]{2,1,0:T(8,128)(2,1)S(1)}, bf16[2,384,512]{2,1,0:T(8,128)(2,1)S(1)}, u32[]{:S(2)}, u32[]{:S(2)}) collective-permute-start(bf16[2,384,512]{2,1,0:T(8,128)(2,1)S(1)} %bundle.1), channel_id=1, source_target_pairs={{0,1},{1,0},{2,3},{3,2},{4,5},{5,4},{6,7},{7,6},{8,9},{9,8},{10,11... | collective-permute-start | bytes 2359304 | tf_op jit(solution)/shard_map/ppermute | solution.py:192
  30.3 0.0 copy-start.2
  30.3 0.0 copy-start.3
  30.4 1.4 %collective-permute-start.4 = (bf16[128,2048]{1,0:T(8,128)(2,1)S(1)}, bf16[128,2048]{1,0:T(8,128)(2,1)S(1)}, u32[]{:S(2)}, u32[]{:S(2)}) collective-permute-start(bf16[128,2048]{1,0:T(8,128)(2,1)S(1)} %hold.6), channel_id=1, source_target_pairs={{258,480},{259,481},{260,486},{261,487},{266,488},{267,489},{268,4... | collective-permute-start | bytes 1572872 | tf_op jit(solution)/shard_map/ppermute | solution.py:194
  31.8 0.0 collective-permute-done.5.refs_0_
  31.8 7.3 %collective-permute-done.6.refs_1_ = bf16[128,2048]{1,0:T(8,128)(2,1)S(1)} collective-permute-done((bf16[128,2048]{1,0:T(8,128)(2,1)S(1)}, bf16[128,2048]{1,0:T(8,128)(2,1)S(1)}, u32[]{:S(2)}, u32[]{:S(2)}) %collective-permute-start.6) | collective-permute-done | bytes 524320 | tf_op jit(solution)/shard_map/ppermute | solution.py:188
  39.1 0.0 collective-permute-done.7.refs_7_.refs_8_
  39.1 8.5 %attention_backward.2 = (bf16[128,4096]{1,0:T(8,128)(2,1)}, f32[2,384,512]{2,1,0:T(8,128)S(1)}, bf16[2,384,512]{2,1,0:T(8,128)(2,1)S(1)}, bf16[2,128,512]{2,1,0:T(8,128)(2,1)S(1)}) custom-call(s32[1,7]{1,0:T(1,128)S(1)} %copy-done.3, bf16[128,4096]{1,0:T(8,128)(2,1)S(1)} %bitcast.7, bf16[128,2048]{1,0:T(8,128)(2,1)S(1)} %get-tuple-element.25.refs_2_, ...), custom_call_target="tpu_custom_call" | custom-call | flops 2147483648 | bytes 2097152 | tf_op jit(solution)/shard_map/attention_backward/pallas_call | solution.py:80
  47.7 4.3 %collective-permute-done.4.refs_3_ = bf16[128,2048]{1,0:T(8,128)(2,1)S(1)} collective-permute-done((bf16[128,2048]{1,0:T(8,128)(2,1)S(1)}, bf16[128,2048]{1,0:T(8,128)(2,1)S(1)}, u32[]{:S(2)}, u32[]{:S(2)}) %collective-permute-start.4) | collective-permute-done | bytes 524320 | tf_op jit(solution)/shard_map/ppermute | solution.py:194
  52.0 8.5 %attention_backward.3 = (bf16[128,4096]{1,0:T(8,128)(2,1)}, f32[2,384,512]{2,1,0:T(8,128)S(1)}, bf16[2,384,512]{2,1,0:T(8,128)(2,1)S(1)}, bf16[2,128,512]{2,1,0:T(8,128)(2,1)S(1)}) custom-call(s32[1,7]{1,0:T(1,128)S(1)} %copy-done.3, bf16[128,4096]{1,0:T(8,128)(2,1)S(1)} %bitcast.8, ...), custom_call_target="tpu_custom_call", output_to_operand_aliasing={{0}: (9, {}), {1}: (10, {}), {2}: (11, {}), {3}: (12, {})} | custom-call | flops 2147483648 | bytes 2097152 | tf_op jit(solution)/shard_map/attention_backward/pallas_call | solution.py:80
  60.5 10.9 %collective-permute-start.8 = (bf16[2,384,512]{2,1,0:T(8,128)(2,1)S(1)}, bf16[2,384,512]{2,1,0:T(8,128)(2,1)S(1)}, u32[]{:S(2)}, u32[]{:S(2)}) collective-permute-start(bf16[2,384,512]{2,1,0:T(8,128)(2,1)S(1)} %get-tuple-element.32), channel_id=1, source_target_pairs={{0,1},{1,0},{2,3},{3,2},{4,5},{5,4},{6,7},{7,6},{8,9},{9,8},{10,11... | collective-permute-start | bytes 2359304 | tf_op jit(solution)/shard_map/ppermute | solution.py:201
  71.4 1.9 %collective-permute-start.9 = (bf16[2,128,512]{2,1,0:T(8,128)(2,1)S(1)}, bf16[2,128,512]{2,1,0:T(8,128)(2,1)S(1)}, u32[]{:S(2)}, u32[]{:S(2)}) collective-permute-start(bf16[2,128,512]{2,1,0:T(8,128)(2,1)S(1)} %get-tuple-element.33), channel_id=1, source_target_pairs={{1,4},{3,6},{4,1},{5,8},{6,3},{7,10},{8,5},{9,12},{10,7},{11,14},{... | collective-permute-start | bytes 786440 | tf_op jit(solution)/shard_map/ppermute | solution.py:200
  73.4 0.3 fusion.3
  73.7 2.7 %collective-permute-start.11 = (bf16[2,128,512]{2,1,0:T(8,128)(2,1)S(1)}, bf16[2,128,512]{2,1,0:T(8,128)(2,1)S(1)}, u32[]{:S(2)}, u32[]{:S(2)}) collective-permute-start(bf16[2,128,512]{2,1,0:T(8,128)(2,1)S(1)} %get-tuple-element.41), channel_id=1, source_target_pairs={{0,2},{1,3},{2,4},{3,5},{4,6},{5,7},{6,8},{7,9},{8,10},{9,11},{10,... | collective-permute-start | bytes 786440 | tf_op jit(solution)/shard_map/ppermute | solution.py:205
  76.5 3.1 %collective-permute-start.10 = (bf16[2,128,512]{2,1,0:T(8,128)(2,1)S(1)}, bf16[2,128,512]{2,1,0:T(8,128)(2,1)S(1)}, u32[]{:S(2)}, u32[]{:S(2)}) collective-permute-start(bf16[2,128,512]{2,1,0:T(8,128)(2,1)S(1)} %get-tuple-element.42), channel_id=1, source_target_pairs={{2,0},{3,1},{4,2},{5,3},{6,4},{7,5},{8,6},{9,7},{10,8},{11,9},{12,... | collective-permute-start | bytes 786440 | tf_op jit(solution)/shard_map/ppermute | solution.py:204
  79.6 2.7 %collective-permute-done.9.refs_0_ = bf16[2,128,512]{2,1,0:T(8,128)(2,1)S(1)} collective-permute-done((bf16[2,128,512]{2,1,0:T(8,128)(2,1)S(1)}, bf16[2,128,512]{2,1,0:T(8,128)(2,1)S(1)}, u32[]{:S(2)}, u32[]{:S(2)}) %collective-permute-start.9) | collective-permute-done | bytes 262176 | tf_op jit(solution)/shard_map/ppermute | solution.py:200
  82.3 3.0 %collective-permute-done.11.refs_2_ = bf16[2,128,512]{2,1,0:T(8,128)(2,1)S(1)} collective-permute-done((bf16[2,128,512]{2,1,0:T(8,128)(2,1)S(1)}, bf16[2,128,512]{2,1,0:T(8,128)(2,1)S(1)}, u32[]{:S(2)}, u32[]{:S(2)}) %collective-permute-start.11) | collective-permute-done | bytes 262176 | tf_op jit(solution)/shard_map/ppermute | solution.py:205
  85.3 13.4 %collective-permute-done.10.refs_1_ = bf16[2,128,512]{2,1,0:T(8,128)(2,1)S(1)} collective-permute-done((bf16[2,128,512]{2,1,0:T(8,128)(2,1)S(1)}, bf16[2,128,512]{2,1,0:T(8,128)(2,1)S(1)}, u32[]{:S(2)}, u32[]{:S(2)}) %collective-permute-start.10) | collective-permute-done | bytes 262176 | tf_op jit(solution)/shard_map/ppermute | solution.py:204
  98.8 0.2 fusion.2
  98.9 0.7 fusion.6
  (14 shorter events, 0.1 us)
Async XLA Ops:
  0.6 0.9 copy-start
  1.5 0.9 copy-start.1
  2.5 17.3 %collective-permute-start.1 = (bf16[2,128,512]{2,1,0:T(8,128)(2,1)S(1)}, bf16[2,128,512]{2,1,0:T(8,128)(2,1)S(1)}, u32[]{:S(2)}, u32[]{:S(2)}) collective-permute-start(bf16[2,128,512]{2,1,0:T(8,128)(2,1)S(1)} %join.1.own.refs_3_.refs_4_), channel_id=1, source_target_pairs={{2,0},{3,1},{4,2},{5,3},{6,4},{7,5},{8,6},{9,7},{10,8},{11,9},{12,... | collective-permute-start | bytes 786440 | tf_op jit(solution)/shard_map/ppermute | solution.py:184
  5.2 19.3 %collective-permute-start = (bf16[2,128,512]{2,1,0:T(8,128)(2,1)S(1)}, bf16[2,128,512]{2,1,0:T(8,128)(2,1)S(1)}, u32[]{:S(2)}, u32[]{:S(2)}) collective-permute-start(bf16[2,128,512]{2,1,0:T(8,128)(2,1)S(1)} %join.1.own.refs_3_.refs_4_), channel_id=1, source_target_pairs={{0,2},{1,3},{2,4},{3,5},{4,6},{5,7},{6,8},{7,9},{8,10},{9,11},{10,... | collective-permute-start | bytes 786440 | tf_op jit(solution)/shard_map/ppermute | solution.py:183
  13.8 16.5 %collective-permute-start.3 = (bf16[128,2048]{1,0:T(8,128)(2,1)S(1)}, bf16[128,2048]{1,0:T(8,128)(2,1)S(1)}, u32[]{:S(2)}, u32[]{:S(2)}) collective-permute-start(bf16[128,2048]{1,0:T(8,128)(2,1)S(1)} %get-tuple-element.22), channel_id=1, source_target_pairs={{0,258},{1,259},{6,260},{7,261},{8,266},{9,267},{14,268},{15,269},... | collective-permute-start | bytes 1572872 | tf_op jit(solution)/shard_map/ppermute | solution.py:190
  14.5 17.2 %collective-permute-start.5 = (bf16[2,128,512]{2,1,0:T(8,128)(2,1)S(1)}, bf16[2,128,512]{2,1,0:T(8,128)(2,1)S(1)}, u32[]{:S(2)}, u32[]{:S(2)}) collective-permute-start(bf16[2,128,512]{2,1,0:T(8,128)(2,1)S(1)} %join.1.own.refs_3_.refs_4_), channel_id=1, source_target_pairs={{1,4},{3,6},{4,1},{5,8},{6,3},{7,10},{8,5},{9,12},{10,7},{11,14},{... | collective-permute-start | bytes 786440 | tf_op jit(solution)/shard_map/ppermute | solution.py:188
  16.5 22.7 %collective-permute-start.6 = (bf16[128,2048]{1,0:T(8,128)(2,1)S(1)}, bf16[128,2048]{1,0:T(8,128)(2,1)S(1)}, u32[]{:S(2)}, u32[]{:S(2)}) collective-permute-start(bf16[128,2048]{1,0:T(8,128)(2,1)S(1)} %get-tuple-element.39), channel_id=1, source_target_pairs={{0,480},{32,0},{64,32},{96,64},{128,96},{160,128},{192,160},{224,1... | collective-permute-start | bytes 1572872 | tf_op jit(solution)/shard_map/ppermute | solution.py:188
  24.5 23.1 %collective-permute-start.2 = (bf16[128,2048]{1,0:T(8,128)(2,1)S(1)}, bf16[128,2048]{1,0:T(8,128)(2,1)S(1)}, u32[]{:S(2)}, u32[]{:S(2)}) collective-permute-start(bf16[128,2048]{1,0:T(8,128)(2,1)S(1)} %get-tuple-element.22), channel_id=1, source_target_pairs={{2,482},{3,483},{4,484},{5,485},{10,490},{11,491},{12,492},{13,493... | collective-permute-start | bytes 1572872 | tf_op jit(solution)/shard_map/ppermute | solution.py:193
  28.4 10.8 %collective-permute-start.7 = (bf16[2,384,512]{2,1,0:T(8,128)(2,1)S(1)}, bf16[2,384,512]{2,1,0:T(8,128)(2,1)S(1)}, u32[]{:S(2)}, u32[]{:S(2)}) collective-permute-start(bf16[2,384,512]{2,1,0:T(8,128)(2,1)S(1)} %bundle.1), channel_id=1, source_target_pairs={{0,1},{1,0},{2,3},{3,2},{4,5},{5,4},{6,7},{7,6},{8,9},{9,8},{10,11... | collective-permute-start | bytes 2359304 | tf_op jit(solution)/shard_map/ppermute | solution.py:192
  30.3 8.8 %copy-start.2 = (bf16[1,128,4096]{2,1,0:T(8,128)(2,1)S(1)}, bf16[1,128,4096]{2,1,0:T(8,128)(2,1)}, u32[]{:S(2)}) copy-start(bf16[1,128,4096]{2,1,0:T(8,128)(2,1)} %param.5) | copy-start | bytes 3145732
  30.3 8.8 %copy-start.3 = (s32[1,7]{1,0:T(1,128)S(1)}, s32[1,7]{1,0:T(1,128)}, u32[]{:S(2)}) copy-start(s32[1,7]{1,0:T(1,128)} %refs_0_.3) | copy-start | bytes 88
  30.4 21.6 %collective-permute-start.4 = (bf16[128,2048]{1,0:T(8,128)(2,1)S(1)}, bf16[128,2048]{1,0:T(8,128)(2,1)S(1)}, u32[]{:S(2)}, u32[]{:S(2)}) collective-permute-start(bf16[128,2048]{1,0:T(8,128)(2,1)S(1)} %hold.6), channel_id=1, source_target_pairs={{258,480},{259,481},{260,486},{261,487},{266,488},{267,489},{268,4... | collective-permute-start | bytes 1572872 | tf_op jit(solution)/shard_map/ppermute | solution.py:194
  60.5 12.9 %collective-permute-start.8 = (bf16[2,384,512]{2,1,0:T(8,128)(2,1)S(1)}, bf16[2,384,512]{2,1,0:T(8,128)(2,1)S(1)}, u32[]{:S(2)}, u32[]{:S(2)}) collective-permute-start(bf16[2,384,512]{2,1,0:T(8,128)(2,1)S(1)} %get-tuple-element.32), channel_id=1, source_target_pairs={{0,1},{1,0},{2,3},{3,2},{4,5},{5,4},{6,7},{7,6},{8,9},{9,8},{10,11... | collective-permute-start | bytes 2359304 | tf_op jit(solution)/shard_map/ppermute | solution.py:201
  71.4 10.9 %collective-permute-start.9 = (bf16[2,128,512]{2,1,0:T(8,128)(2,1)S(1)}, bf16[2,128,512]{2,1,0:T(8,128)(2,1)S(1)}, u32[]{:S(2)}, u32[]{:S(2)}) collective-permute-start(bf16[2,128,512]{2,1,0:T(8,128)(2,1)S(1)} %get-tuple-element.33), channel_id=1, source_target_pairs={{1,4},{3,6},{4,1},{5,8},{6,3},{7,10},{8,5},{9,12},{10,7},{11,14},{... | collective-permute-start | bytes 786440 | tf_op jit(solution)/shard_map/ppermute | solution.py:200
  73.7 11.6 %collective-permute-start.11 = (bf16[2,128,512]{2,1,0:T(8,128)(2,1)S(1)}, bf16[2,128,512]{2,1,0:T(8,128)(2,1)S(1)}, u32[]{:S(2)}, u32[]{:S(2)}) collective-permute-start(bf16[2,128,512]{2,1,0:T(8,128)(2,1)S(1)} %get-tuple-element.41), channel_id=1, source_target_pairs={{0,2},{1,3},{2,4},{3,5},{4,6},{5,7},{6,8},{7,9},{8,10},{9,11},{10,... | collective-permute-start | bytes 786440 | tf_op jit(solution)/shard_map/ppermute | solution.py:205
  76.5 22.3 %collective-permute-start.10 = (bf16[2,128,512]{2,1,0:T(8,128)(2,1)S(1)}, bf16[2,128,512]{2,1,0:T(8,128)(2,1)S(1)}, u32[]{:S(2)}, u32[]{:S(2)}) collective-permute-start(bf16[2,128,512]{2,1,0:T(8,128)(2,1)S(1)} %get-tuple-element.42), channel_id=1, source_target_pairs={{2,0},{3,1},{4,2},{5,3},{6,4},{7,5},{8,6},{9,7},{10,8},{11,9},{12,... | collective-permute-start | bytes 786440 | tf_op jit(solution)/shard_map/ppermute | solution.py:204

commit v8 on v5

--- a/solution.py
+++ b/solution.py
@@ -171,12 +171,15 @@
         lax.ppermute(own, "seq", far_pairs(count)), lax.ppermute(low, "section", before), flops=1 << 33
     )
     (turned,) = hold(lax.ppermute(high, "section", [(0, turn), (turn, 0)]), flops=1 << 33)
-    joined, high = lax.optimization_barrier((bundle(own, left, right), high))
-    mate = lax.ppermute(joined, "seq", mate_pairs(count))
-    grad_high = lax.ppermute(high, "section", [(i, i - 1) for i in range(sections) if i % turn])
+    left, right, late = lax.optimization_barrier((left, right, high))
+    left, right, turned = lax.optimization_barrier((left, right, turned))
+    mate = lax.ppermute(bundle(own, left, right), "seq", mate_pairs(count))
+    grad_high = lax.ppermute(late, "section", [(i, i - 1) for i in range(sections) if i % turn])
     grad_wrap = lax.ppermute(turned, "section", [(0, turn - 1), (turn, sections - 1)])
     slots = (own, left, right, far, mate)
     kept = attention_backward(block_mask, query_heads[0], (grad_low,), slots, 0, 2, ())
+    grad_wrap, last = hold(grad_wrap, kept[3], flops=1 << 31)
+    kept = [*kept[:3], last]
     query_grad, parts, to_mate, to_far = attention_backward(
         block_mask, query_heads[0], (grad_high, grad_wrap), slots, 2, 2, kept
     )

time: 93.4 us -> 92 us (0.985)
  the two profiles are of different devices: /device:TPU:318 before, /device:TPU:262 now
where the time goes in v8:
time: 92 us; the launch traced here: 91.5 us
  starting transfers between devices  41 us (45%)
  waiting for transfers between devices  28.3 us (31%)
  Pallas kernels  17.1 us (19%)
  local copies, waits for them, and re-layouts  3.87 us (4%)
    pallas_call x2, Pallas kernels, attention_backward(): pl.pallas_call(functools.partial(backward_body, len(grads), len(kept)), g...  17 us
    ppermute x1, waiting for transfers between devices, shards(): lax.ppermute(high, 'section', [(0, turn), (turn, 0)])  9.95 us
    ppermute x1, starting transfers between devices, shards(): lax.ppermute(sums[:, 2 * BL:].astype(B16), 'seq', shift_pairs(count, 2))  7.89 us
    ppermute x1, starting transfers between devices, shards(): lax.ppermute(turned, 'section', [(0, turn - 1), (turn, sections - 1)])  6.19 us
    ppermute x1, starting transfers between devices, shards(): lax.ppermute(own, 'seq', shift_pairs(count, 2))  6.11 us
    ppermute x1, waiting for transfers between devices, shards(): lax.ppermute(sums[:, BL:2 * BL].astype(B16), 'seq', shift_pairs(count, -2))  5.12 us
    ppermute x1, waiting for transfers between devices, shards(): lax.ppermute(own, 'seq', shift_pairs(count, 2))  4.81 us
    ppermute x1, waiting for transfers between devices, shards(): lax.ppermute(sums[:, 2 * BL:].astype(B16), 'seq', shift_pairs(count, 2))  4.78 us
  transfers between devices with their start and end apart: 12, of which 7 were waited for; matrix products, arithmetic and copies ran while one was open for 2% of the time, Pallas kernels for 9%

profile of v8, /device:TPU:262, one launch (start us, length us, event | category | flops | bytes accessed | tf_op | source)
XLA Modules:
  0.0 91.5 jit_solution(15993346101106777810)
XLA Ops:
  0.6 0.9 copy-done
  1.5 0.9 copy-done.1
  2.5 2.7 %collective-permute-start.1 = (bf16[2,128,512]{2,1,0:T(8,128)(2,1)S(1)}, bf16[2,128,512]{2,1,0:T(8,128)(2,1)S(1)}, u32[]{:S(2)}, u32[]{:S(2)}) collective-permute-start(bf16[2,128,512]{2,1,0:T(8,128)(2,1)S(1)} %join.1.own.refs_3_.refs_4_), channel_id=1, source_target_pairs={{2,0},{3,1},{4,2},{5,3},{6,4},{7,5},{8,6},{9,7},{10,8},{11,9},{12,... | collective-permute-start | bytes 786440 | tf_op jit(solution)/shard_map/ppermute | solution.py:167
  5.2 6.1 %collective-permute-start = (bf16[2,128,512]{2,1,0:T(8,128)(2,1)S(1)}, bf16[2,128,512]{2,1,0:T(8,128)(2,1)S(1)}, u32[]{:S(2)}, u32[]{:S(2)}) collective-permute-start(bf16[2,128,512]{2,1,0:T(8,128)(2,1)S(1)} %join.1.own.refs_3_.refs_4_), channel_id=1, source_target_pairs={{0,2},{1,3},{2,4},{3,5},{4,6},{5,7},{6,8},{7,9},{8,10},{9,11},{10,... | collective-permute-start | bytes 786440 | tf_op jit(solution)/shard_map/ppermute | solution.py:166
  11.3 1.3 %fusion.4 = (bf16[128,2048]{1,0:T(8,128)(2,1)S(1)}, bf16[128,2048]{1,0:T(8,128)(2,1)S(1)}) fusion(bf16[128,4096]{1,0:T(8,128)(2,1)} %bitcast.9), kind=kLoop, calls=%fused_computation.6 | loop fusion | bytes 2097152 | tf_op jit(solution)/shard_map/slice | solution.py:162
  12.6 3.4 %collective-permute-start.3 = (bf16[128,2048]{1,0:T(8,128)(2,1)S(1)}, bf16[128,2048]{1,0:T(8,128)(2,1)S(1)}, u32[]{:S(2)}, u32[]{:S(2)}) collective-permute-start(bf16[128,2048]{1,0:T(8,128)(2,1)S(1)} %get-tuple-element.28), channel_id=1, source_target_pairs={{0,256},{256,0},{1,257},{257,1},{2,258},{258,2},{3,259},{259,3},{4... | collective-permute-start | bytes 1572872 | tf_op jit(solution)/shard_map/ppermute | solution.py:173
  16.0 1.9 %collective-permute-start.5 = (bf16[2,128,512]{2,1,0:T(8,128)(2,1)S(1)}, bf16[2,128,512]{2,1,0:T(8,128)(2,1)S(1)}, u32[]{:S(2)}, u32[]{:S(2)}) collective-permute-start(bf16[2,128,512]{2,1,0:T(8,128)(2,1)S(1)} %join.1.own.refs_3_.refs_4_), channel_id=1, source_target_pairs={{1,4},{3,6},{4,1},{5,8},{6,3},{7,10},{8,5},{9,12},{10,7},{11,14},{... | collective-permute-start | bytes 786440 | tf_op jit(solution)/shard_map/ppermute | solution.py:171
  18.0 3.6 %collective-permute-start.6 = (bf16[128,2048]{1,0:T(8,128)(2,1)S(1)}, bf16[128,2048]{1,0:T(8,128)(2,1)S(1)}, u32[]{:S(2)}, u32[]{:S(2)}) collective-permute-start(bf16[128,2048]{1,0:T(8,128)(2,1)S(1)} %get-tuple-element.51), channel_id=1, source_target_pairs={{0,480},{32,0},{64,32},{96,64},{128,96},{160,128},{192,160},{224,1... | collective-permute-start | bytes 1572872 | tf_op jit(solution)/shard_map/ppermute | solution.py:171
  21.6 0.0 collective-permute-done.1.refs_1_
  21.6 4.8 %collective-permute-done.refs_0_ = bf16[2,128,512]{2,1,0:T(8,128)(2,1)S(1)} collective-permute-done((bf16[2,128,512]{2,1,0:T(8,128)(2,1)S(1)}, bf16[2,128,512]{2,1,0:T(8,128)(2,1)S(1)}, u32[]{:S(2)}, u32[]{:S(2)}) %collective-permute-start) | collective-permute-done | bytes 262176 | tf_op jit(solution)/shard_map/ppermute | solution.py:166
  26.4 1.3 %collective-permute-start.2 = (bf16[128,2048]{1,0:T(8,128)(2,1)S(1)}, bf16[128,2048]{1,0:T(8,128)(2,1)S(1)}, u32[]{:S(2)}, u32[]{:S(2)}) collective-permute-start(bf16[128,2048]{1,0:T(8,128)(2,1)S(1)} %get-tuple-element.28), channel_id=1, source_target_pairs={{32,0},{64,32},{96,64},{128,96},{160,128},{192,160},{224,192},{288... | collective-permute-start | bytes 1572872 | tf_op jit(solution)/shard_map/ppermute | solution.py:177
  27.7 9.9 %collective-permute-done.3.refs_0_ = bf16[128,2048]{1,0:T(8,128)(2,1)S(1)} collective-permute-done((bf16[128,2048]{1,0:T(8,128)(2,1)S(1)}, bf16[128,2048]{1,0:T(8,128)(2,1)S(1)}, u32[]{:S(2)}, u32[]{:S(2)}) %collective-permute-start.3) | collective-permute-done | bytes 524320 | tf_op jit(solution)/shard_map/ppermute | solution.py:173
  37.6 6.2 %collective-permute-start.4 = (bf16[128,2048]{1,0:T(8,128)(2,1)S(1)}, bf16[128,2048]{1,0:T(8,128)(2,1)S(1)}, u32[]{:S(2)}, u32[]{:S(2)}) collective-permute-start(bf16[128,2048]{1,0:T(8,128)(2,1)S(1)} %hold.7), channel_id=1, source_target_pairs={{0,224},{256,480},{1,225},{257,481},{2,226},{258,482},{3,227},{259... | collective-permute-start | bytes 1572872 | tf_op jit(solution)/shard_map/ppermute | solution.py:178
  43.8 0.1 bundle.1
  43.9 0.0 copy-start.2
  43.9 0.0 copy-start.3
  43.9 2.1 %collective-permute-start.7 = (bf16[2,384,512]{2,1,0:T(8,128)(2,1)S(1)}, bf16[2,384,512]{2,1,0:T(8,128)(2,1)S(1)}, u32[]{:S(2)}, u32[]{:S(2)}) collective-permute-start(bf16[2,384,512]{2,1,0:T(8,128)(2,1)S(1)} %bundle.1), channel_id=1, source_target_pairs={{0,1},{1,0},{2,3},{3,2},{4,5},{5,4},{6,7},{7,6},{8,9},{9,8},{10,11... | collective-permute-start | bytes 2359304 | tf_op jit(solution)/shard_map/ppermute | solution.py:176
  46.0 0.0 collective-permute-done.5.refs_0_
  46.0 2.2 %collective-permute-done.7.refs_7_.refs_8_ = bf16[2,384,512]{2,1,0:T(8,128)(2,1)S(1)} collective-permute-done((bf16[2,384,512]{2,1,0:T(8,128)(2,1)S(1)}, bf16[2,384,512]{2,1,0:T(8,128)(2,1)S(1)}, u32[]{:S(2)}, u32[]{:S(2)}) %collective-permute-start.7) | collective-permute-done | bytes 786464 | tf_op jit(solution)/shard_map/ppermute | solution.py:176
  48.2 8.5 %attention_backward.2 = (bf16[128,4096]{1,0:T(8,128)(2,1)}, f32[2,384,512]{2,1,0:T(8,128)S(1)}, bf16[2,384,512]{2,1,0:T(8,128)(2,1)S(1)}, bf16[2,128,512]{2,1,0:T(8,128)(2,1)S(1)}) custom-call(s32[1,7]{1,0:T(1,128)S(1)} %copy-done.3, bf16[128,4096]{1,0:T(8,128)(2,1)S(1)} %bitcast.7, bf16[128,2048]{1,0:T(8,128)(2,1)S(1)} %get-tuple-element.32.refs_2_, ...), custom_call_target="tpu_custom_call" | custom-call | flops 2147483648 | bytes 2097152 | tf_op jit(solution)/shard_map/attention_backward/pallas_call | solution.py:79
  56.7 8.5 %attention_backward.3 = (bf16[128,4096]{1,0:T(8,128)(2,1)}, f32[2,384,512]{2,1,0:T(8,128)S(1)}, bf16[2,384,512]{2,1,0:T(8,128)(2,1)S(1)}, bf16[2,128,512]{2,1,0:T(8,128)(2,1)S(1)}) custom-call(s32[1,7]{1,0:T(1,128)S(1)} %copy-done.3, bf16[128,4096]{1,0:T(8,128)(2,1)S(1)} %bitcast.8, ...), custom_call_target="tpu_custom_call", output_to_operand_aliasing={{0}: (9, {}), {1}: (10, {}), {2}: (11, {}), {3}: (12, {})} | custom-call | flops 2147483648 | bytes 2097152 | tf_op jit(solution)/shard_map/attention_backward/pallas_call | solution.py:79
  65.2 2.0 %collective-permute-start.8 = (bf16[2,384,512]{2,1,0:T(8,128)(2,1)S(1)}, bf16[2,384,512]{2,1,0:T(8,128)(2,1)S(1)}, u32[]{:S(2)}, u32[]{:S(2)}) collective-permute-start(bf16[2,384,512]{2,1,0:T(8,128)(2,1)S(1)} %get-tuple-element.44), channel_id=1, source_target_pairs={{0,1},{1,0},{2,3},{3,2},{4,5},{5,4},{6,7},{7,6},{8,9},{9,8},{10,11... | collective-permute-start | bytes 2359304 | tf_op jit(solution)/shard_map/ppermute | solution.py:187
  67.3 1.9 %collective-permute-start.9 = (bf16[2,128,512]{2,1,0:T(8,128)(2,1)S(1)}, bf16[2,128,512]{2,1,0:T(8,128)(2,1)S(1)}, u32[]{:S(2)}, u32[]{:S(2)}) collective-permute-start(bf16[2,128,512]{2,1,0:T(8,128)(2,1)S(1)} %get-tuple-element.45), channel_id=1, source_target_pairs={{1,4},{3,6},{4,1},{5,8},{6,3},{7,10},{8,5},{9,12},{10,7},{11,14},{... | collective-permute-start | bytes 786440 | tf_op jit(solution)/shard_map/ppermute | solution.py:186
  69.2 0.2 collective-permute-done.8
  69.4 0.3 fusion.3
  69.7 7.9 %collective-permute-start.11 = (bf16[2,128,512]{2,1,0:T(8,128)(2,1)S(1)}, bf16[2,128,512]{2,1,0:T(8,128)(2,1)S(1)}, u32[]{:S(2)}, u32[]{:S(2)}) collective-permute-start(bf16[2,128,512]{2,1,0:T(8,128)(2,1)S(1)} %get-tuple-element.53), channel_id=1, source_target_pairs={{0,2},{1,3},{2,4},{3,5},{4,6},{5,7},{6,8},{7,9},{8,10},{9,11},{10,... | collective-permute-start | bytes 786440 | tf_op jit(solution)/shard_map/ppermute | solution.py:191
  77.6 1.9 %collective-permute-start.10 = (bf16[2,128,512]{2,1,0:T(8,128)(2,1)S(1)}, bf16[2,128,512]{2,1,0:T(8,128)(2,1)S(1)}, u32[]{:S(2)}, u32[]{:S(2)}) collective-permute-start(bf16[2,128,512]{2,1,0:T(8,128)(2,1)S(1)} %get-tuple-element.54), channel_id=1, source_target_pairs={{2,0},{3,1},{4,2},{5,3},{6,4},{7,5},{8,6},{9,7},{10,8},{11,9},{12,... | collective-permute-start | bytes 786440 | tf_op jit(solution)/shard_map/ppermute | solution.py:190
  79.6 1.2 %collective-permute-done.9.refs_0_ = bf16[2,128,512]{2,1,0:T(8,128)(2,1)S(1)} collective-permute-done((bf16[2,128,512]{2,1,0:T(8,128)(2,1)S(1)}, bf16[2,128,512]{2,1,0:T(8,128)(2,1)S(1)}, u32[]{:S(2)}, u32[]{:S(2)}) %collective-permute-start.9) | collective-permute-done | bytes 262176 | tf_op jit(solution)/shard_map/ppermute | solution.py:186
  80.8 4.8 %collective-permute-done.11.refs_2_ = bf16[2,128,512]{2,1,0:T(8,128)(2,1)S(1)} collective-permute-done((bf16[2,128,512]{2,1,0:T(8,128)(2,1)S(1)}, bf16[2,128,512]{2,1,0:T(8,128)(2,1)S(1)}, u32[]{:S(2)}, u32[]{:S(2)}) %collective-permute-start.11) | collective-permute-done | bytes 262176 | tf_op jit(solution)/shard_map/ppermute | solution.py:191
  85.5 5.1 %collective-permute-done.10.refs_1_ = bf16[2,128,512]{2,1,0:T(8,128)(2,1)S(1)} collective-permute-done((bf16[2,128,512]{2,1,0:T(8,128)(2,1)S(1)}, bf16[2,128,512]{2,1,0:T(8,128)(2,1)S(1)}, u32[]{:S(2)}, u32[]{:S(2)}) %collective-permute-start.10) | collective-permute-done | bytes 262176 | tf_op jit(solution)/shard_map/ppermute | solution.py:190
  90.7 0.2 fusion.2
  90.8 0.7 fusion.6
  (15 shorter events, 0.1 us)
Async XLA Ops:
  0.6 0.9 copy-start
  1.5 0.9 copy-start.1
  2.5 19.1 %collective-permute-start.1 = (bf16[2,128,512]{2,1,0:T(8,128)(2,1)S(1)}, bf16[2,128,512]{2,1,0:T(8,128)(2,1)S(1)}, u32[]{:S(2)}, u32[]{:S(2)}) collective-permute-start(bf16[2,128,512]{2,1,0:T(8,128)(2,1)S(1)} %join.1.own.refs_3_.refs_4_), channel_id=1, source_target_pairs={{2,0},{3,1},{4,2},{5,3},{6,4},{7,5},{8,6},{9,7},{10,8},{11,9},{12,... | collective-permute-start | bytes 786440 | tf_op jit(solution)/shard_map/ppermute | solution.py:167
  5.2 21.2 %collective-permute-start = (bf16[2,128,512]{2,1,0:T(8,128)(2,1)S(1)}, bf16[2,128,512]{2,1,0:T(8,128)(2,1)S(1)}, u32[]{:S(2)}, u32[]{:S(2)}) collective-permute-start(bf16[2,128,512]{2,1,0:T(8,128)(2,1)S(1)} %join.1.own.refs_3_.refs_4_), channel_id=1, source_target_pairs={{0,2},{1,3},{2,4},{3,5},{4,6},{5,7},{6,8},{7,9},{8,10},{9,11},{10,... | collective-permute-start | bytes 786440 | tf_op jit(solution)/shard_map/ppermute | solution.py:166
  12.6 25.0 %collective-permute-start.3 = (bf16[128,2048]{1,0:T(8,128)(2,1)S(1)}, bf16[128,2048]{1,0:T(8,128)(2,1)S(1)}, u32[]{:S(2)}, u32[]{:S(2)}) collective-permute-start(bf16[128,2048]{1,0:T(8,128)(2,1)S(1)} %get-tuple-element.28), channel_id=1, source_target_pairs={{0,256},{256,0},{1,257},{257,1},{2,258},{258,2},{3,259},{259,3},{4... | collective-permute-start | bytes 1572872 | tf_op jit(solution)/shard_map/ppermute | solution.py:173
  16.0 29.9 %collective-permute-start.5 = (bf16[2,128,512]{2,1,0:T(8,128)(2,1)S(1)}, bf16[2,128,512]{2,1,0:T(8,128)(2,1)S(1)}, u32[]{:S(2)}, u32[]{:S(2)}) collective-permute-start(bf16[2,128,512]{2,1,0:T(8,128)(2,1)S(1)} %join.1.own.refs_3_.refs_4_), channel_id=1, source_target_pairs={{1,4},{3,6},{4,1},{5,8},{6,3},{7,10},{8,5},{9,12},{10,7},{11,14},{... | collective-permute-start | bytes 786440 | tf_op jit(solution)/shard_map/ppermute | solution.py:171
  18.0 28.0 %collective-permute-start.6 = (bf16[128,2048]{1,0:T(8,128)(2,1)S(1)}, bf16[128,2048]{1,0:T(8,128)(2,1)S(1)}, u32[]{:S(2)}, u32[]{:S(2)}) collective-permute-start(bf16[128,2048]{1,0:T(8,128)(2,1)S(1)} %get-tuple-element.51), channel_id=1, source_target_pairs={{0,480},{32,0},{64,32},{96,64},{128,96},{160,128},{192,160},{224,1... | collective-permute-start | bytes 1572872 | tf_op jit(solution)/shard_map/ppermute | solution.py:171
  26.4 30.3 %collective-permute-start.2 = (bf16[128,2048]{1,0:T(8,128)(2,1)S(1)}, bf16[128,2048]{1,0:T(8,128)(2,1)S(1)}, u32[]{:S(2)}, u32[]{:S(2)}) collective-permute-start(bf16[128,2048]{1,0:T(8,128)(2,1)S(1)} %get-tuple-element.28), channel_id=1, source_target_pairs={{32,0},{64,32},{96,64},{128,96},{160,128},{192,160},{224,192},{288... | collective-permute-start | bytes 1572872 | tf_op jit(solution)/shard_map/ppermute | solution.py:177
  37.6 19.1 %collective-permute-start.4 = (bf16[128,2048]{1,0:T(8,128)(2,1)S(1)}, bf16[128,2048]{1,0:T(8,128)(2,1)S(1)}, u32[]{:S(2)}, u32[]{:S(2)}) collective-permute-start(bf16[128,2048]{1,0:T(8,128)(2,1)S(1)} %hold.7), channel_id=1, source_target_pairs={{0,224},{256,480},{1,225},{257,481},{2,226},{258,482},{3,227},{259... | collective-permute-start | bytes 1572872 | tf_op jit(solution)/shard_map/ppermute | solution.py:178
  43.9 4.3 %copy-start.2 = (bf16[1,128,4096]{2,1,0:T(8,128)(2,1)S(1)}, bf16[1,128,4096]{2,1,0:T(8,128)(2,1)}, u32[]{:S(2)}) copy-start(bf16[1,128,4096]{2,1,0:T(8,128)(2,1)} %param.5) | copy-start | bytes 3145732
  43.9 4.3 %copy-start.3 = (s32[1,7]{1,0:T(1,128)S(1)}, s32[1,7]{1,0:T(1,128)}, u32[]{:S(2)}) copy-start(s32[1,7]{1,0:T(1,128)} %refs_0_.3) | copy-start | bytes 88
  43.9 4.3 %collective-permute-start.7 = (bf16[2,384,512]{2,1,0:T(8,128)(2,1)S(1)}, bf16[2,384,512]{2,1,0:T(8,128)(2,1)S(1)}, u32[]{:S(2)}, u32[]{:S(2)}) collective-permute-start(bf16[2,384,512]{2,1,0:T(8,128)(2,1)S(1)} %bundle.1), channel_id=1, source_target_pairs={{0,1},{1,0},{2,3},{3,2},{4,5},{5,4},{6,7},{7,6},{8,9},{9,8},{10,11... | collective-permute-start | bytes 2359304 | tf_op jit(solution)/shard_map/ppermute | solution.py:176
  65.2 4.2 %collective-permute-start.8 = (bf16[2,384,512]{2,1,0:T(8,128)(2,1)S(1)}, bf16[2,384,512]{2,1,0:T(8,128)(2,1)S(1)}, u32[]{:S(2)}, u32[]{:S(2)}) collective-permute-start(bf16[2,384,512]{2,1,0:T(8,128)(2,1)S(1)} %get-tuple-element.44), channel_id=1, source_target_pairs={{0,1},{1,0},{2,3},{3,2},{4,5},{5,4},{6,7},{7,6},{8,9},{9,8},{10,11... | collective-permute-start | bytes 2359304 | tf_op jit(solution)/shard_map/ppermute | solution.py:187
  67.3 13.5 %collective-permute-start.9 = (bf16[2,128,512]{2,1,0:T(8,128)(2,1)S(1)}, bf16[2,128,512]{2,1,0:T(8,128)(2,1)S(1)}, u32[]{:S(2)}, u32[]{:S(2)}) collective-permute-start(bf16[2,128,512]{2,1,0:T(8,128)(2,1)S(1)} %get-tuple-element.45), channel_id=1, source_target_pairs={{1,4},{3,6},{4,1},{5,8},{6,3},{7,10},{8,5},{9,12},{10,7},{11,14},{... | collective-permute-start | bytes 786440 | tf_op jit(solution)/shard_map/ppermute | solution.py:186
  69.7 15.8 %collective-permute-start.11 = (bf16[2,128,512]{2,1,0:T(8,128)(2,1)S(1)}, bf16[2,128,512]{2,1,0:T(8,128)(2,1)S(1)}, u32[]{:S(2)}, u32[]{:S(2)}) collective-permute-start(bf16[2,128,512]{2,1,0:T(8,128)(2,1)S(1)} %get-tuple-element.53), channel_id=1, source_target_pairs={{0,2},{1,3},{2,4},{3,5},{4,6},{5,7},{6,8},{7,9},{8,10},{9,11},{10,... | collective-permute-start | bytes 786440 | tf_op jit(solution)/shard_map/ppermute | solution.py:191
  77.6 13.0 %collective-permute-start.10 = (bf16[2,128,512]{2,1,0:T(8,128)(2,1)S(1)}, bf16[2,128,512]{2,1,0:T(8,128)(2,1)S(1)}, u32[]{:S(2)}, u32[]{:S(2)}) collective-permute-start(bf16[2,128,512]{2,1,0:T(8,128)(2,1)S(1)} %get-tuple-element.54), channel_id=1, source_target_pairs={{2,0},{3,1},{4,2},{5,3},{6,4},{7,5},{8,6},{9,7},{10,8},{11,9},{12,... | collective-permute-start | bytes 786440 | tf_op jit(solution)/shard_map/ppermute | solution.py:190

commit v9 on v8

--- a/solution.py
+++ b/solution.py
@@ -162,17 +162,13 @@
     low, high = cot[:, :half], cot[:, half:]
     before = [(i, (i - 1) % sections) for i in range(sections)]
     own = join(key_heads[0], value_heads[0])
-    left, right = hold(
-        lax.ppermute(own, "seq", shift_pairs(count, 2)),
-        lax.ppermute(own, "seq", shift_pairs(count, -2)),
-        flops=1 << 32,
-    )
+    left = lax.ppermute(own, "seq", shift_pairs(count, 2))
+    right = lax.ppermute(own, "seq", shift_pairs(count, -2))
     far, grad_low = hold(
         lax.ppermute(own, "seq", far_pairs(count)), lax.ppermute(low, "section", before), flops=1 << 33
     )
     (turned,) = hold(lax.ppermute(high, "section", [(0, turn), (turn, 0)]), flops=1 << 33)
-    left, right, late = lax.optimization_barrier((left, right, high))
-    left, right, turned = lax.optimization_barrier((left, right, turned))
+    left, right, late, _ = lax.optimization_barrier((left, right, high, turned))
     mate = lax.ppermute(bundle(own, left, right), "seq", mate_pairs(count))
     grad_high = lax.ppermute(late, "section", [(i, i - 1) for i in range(sections) if i % turn])
     grad_wrap = lax.ppermute(turned, "section", [(0, turn - 1), (turn, sections - 1)])

time: 92 us -> 92.3 us (level)
  the two profiles are of different devices: /device:TPU:262 before, /device:TPU:254 now
where the time goes in v9:
time: 92.3 us; the launch traced here: 91.8 us
  starting transfers between devices  48.1 us (52%)
  waiting for transfers between devices  23.3 us (25%)
  Pallas kernels  17.1 us (19%)
  local copies, waits for them, and re-layouts  2.11 us (2%)
    pallas_call x2, Pallas kernels, attention_backward(): pl.pallas_call(functools.partial(backward_body, len(grads), len(kept)), g...  17 us
    ppermute x1, starting transfers between devices, shards(): mate = lax.ppermute(bundle(own, left, right), 'seq', mate_pairs(count))  16.7 us
    ppermute x1, waiting for transfers between devices, shards(): lax.ppermute(sums[:, BL:2 * BL].astype(B16), 'seq', shift_pairs(count, -2))  13.6 us
    ppermute x1, starting transfers between devices, shards(): left = lax.ppermute(own, 'seq', shift_pairs(count, 2))  8.14 us
    ppermute x1, starting transfers between devices, shards(): lax.ppermute(sums[:, BL:2 * BL].astype(B16), 'seq', shift_pairs(count, -2))  3.92 us
    ppermute x1, waiting for transfers between devices, shards(): lax.ppermute(sums[:, 2 * BL:].astype(B16), 'seq', shift_pairs(count, 2))  3.52 us
    ppermute x1, waiting for transfers between devices, shards(): left = lax.ppermute(own, 'seq', shift_pairs(count, 2))  3.29 us
    ppermute x1, starting transfers between devices, shards(): lax.ppermute(late, 'section', [(i, i - 1) for i in range(sections) if i %...  3.27 us
  transfers between devices with their start and end apart: 12, of which 5 were waited for; matrix products, arithmetic and copies ran while one was open for 0% of the time, Pallas kernels for 9%

profile of v9, /device:TPU:254, one launch (start us, length us, event | category | flops | bytes accessed | tf_op | source)
XLA Modules:
  0.0 91.8 jit_solution(15172762016543521071)
XLA Ops:
  0.7 1.3 %fusion.4 = (bf16[128,2048]{1,0:T(8,128)(2,1)S(1)}, bf16[128,2048]{1,0:T(8,128)(2,1)S(1)}) fusion(bf16[128,4096]{1,0:T(8,128)(2,1)} %bitcast.9), kind=kLoop, calls=%fused_computation.6 | loop fusion | bytes 2097152 | tf_op jit(solution)/shard_map/slice | solution.py:162
  2.0 0.7 collective-permute-start.2
  2.7 2.8 %collective-permute-start.5 = (bf16[2,128,512]{2,1,0:T(8,128)(2,1)S(1)}, bf16[2,128,512]{2,1,0:T(8,128)(2,1)S(1)}, u32[]{:S(2)}, u32[]{:S(2)}) collective-permute-start(bf16[2,128,512]{2,1,0:T(8,128)(2,1)S(1)} %join.1.own.refs_3_.refs_4_), channel_id=1, source_target_pairs={{1,4},{3,6},{4,1},{5,8},{6,3},{7,10},{8,5},{9,12},{10,7},{11,14},{... | collective-permute-start | bytes 786440 | tf_op jit(solution)/shard_map/ppermute | solution.py:168
  5.5 1.9 %collective-permute-start.1 = (bf16[2,128,512]{2,1,0:T(8,128)(2,1)S(1)}, bf16[2,128,512]{2,1,0:T(8,128)(2,1)S(1)}, u32[]{:S(2)}, u32[]{:S(2)}) collective-permute-start(bf16[2,128,512]{2,1,0:T(8,128)(2,1)S(1)} %join.1.own.refs_3_.refs_4_), channel_id=1, source_target_pairs={{2,0},{3,1},{4,2},{5,3},{6,4},{7,5},{8,6},{9,7},{10,8},{11,9},{12,... | collective-permute-start | bytes 786440 | tf_op jit(solution)/shard_map/ppermute | solution.py:166
  7.4 8.1 %collective-permute-start = (bf16[2,128,512]{2,1,0:T(8,128)(2,1)S(1)}, bf16[2,128,512]{2,1,0:T(8,128)(2,1)S(1)}, u32[]{:S(2)}, u32[]{:S(2)}) collective-permute-start(bf16[2,128,512]{2,1,0:T(8,128)(2,1)S(1)} %join.1.own.refs_3_.refs_4_), channel_id=1, source_target_pairs={{0,2},{1,3},{2,4},{3,5},{4,6},{5,7},{6,8},{7,9},{8,10},{9,11},{10,... | collective-permute-start | bytes 786440 | tf_op jit(solution)/shard_map/ppermute | solution.py:165
  15.6 3.3 %collective-permute-start.6 = (bf16[128,2048]{1,0:T(8,128)(2,1)S(1)}, bf16[128,2048]{1,0:T(8,128)(2,1)S(1)}, u32[]{:S(2)}, u32[]{:S(2)}) collective-permute-start(bf16[128,2048]{1,0:T(8,128)(2,1)S(1)} %get-tuple-element.41), channel_id=1, source_target_pairs={{0,480},{32,0},{64,32},{96,64},{128,96},{160,128},{192,160},{224,1... | collective-permute-start | bytes 1572872 | tf_op jit(solution)/shard_map/ppermute | solution.py:168
  18.9 0.0 collective-permute-done.2.refs_0_
  18.9 1.3 %collective-permute-start.4 = (bf16[128,2048]{1,0:T(8,128)(2,1)S(1)}, bf16[128,2048]{1,0:T(8,128)(2,1)S(1)}, u32[]{:S(2)}, u32[]{:S(2)}) collective-permute-start(bf16[128,2048]{1,0:T(8,128)(2,1)S(1)} %hold.5), channel_id=1, source_target_pairs={{0,224},{256,480},{1,225},{257,481},{2,226},{258,482},{3,227},{259... | collective-permute-start | bytes 1572872 | tf_op jit(solution)/shard_map/ppermute | solution.py:174
  20.2 0.0 collective-permute-done.1.right.refs_5_.refs_6_
  20.2 3.3 %collective-permute-done.left.refs_4_.refs_5_ = bf16[2,128,512]{2,1,0:T(8,128)(2,1)S(1)} collective-permute-done((bf16[2,128,512]{2,1,0:T(8,128)(2,1)S(1)}, bf16[2,128,512]{2,1,0:T(8,128)(2,1)S(1)}, u32[]{:S(2)}, u32[]{:S(2)}) %collective-permute-start) | collective-permute-done | bytes 262176 | tf_op jit(solution)/shard_map/ppermute | solution.py:165
  23.5 3.3 %collective-permute-start.3 = (bf16[128,2048]{1,0:T(8,128)(2,1)S(1)}, bf16[128,2048]{1,0:T(8,128)(2,1)S(1)}, u32[]{:S(2)}, u32[]{:S(2)}) collective-permute-start(bf16[128,2048]{1,0:T(8,128)(2,1)S(1)} %get-tuple-element.21), channel_id=1, source_target_pairs={{32,0},{64,32},{96,64},{128,96},{160,128},{192,160},{224,192},{288... | collective-permute-start | bytes 1572872 | tf_op jit(solution)/shard_map/ppermute | solution.py:173
  26.8 0.1 bundle.1
  26.8 0.0 copy-start.2
  26.8 0.0 copy-start.3
  26.8 16.7 %collective-permute-start.7 = (bf16[2,384,512]{2,1,0:T(8,128)(2,1)S(1)}, bf16[2,384,512]{2,1,0:T(8,128)(2,1)S(1)}, u32[]{:S(2)}, u32[]{:S(2)}) collective-permute-start(bf16[2,384,512]{2,1,0:T(8,128)(2,1)S(1)} %bundle.1), channel_id=1, source_target_pairs={{0,1},{1,0},{2,3},{3,2},{4,5},{5,4},{6,7},{7,6},{8,9},{9,8},{10,11... | collective-permute-start | bytes 2359304 | tf_op jit(solution)/shard_map/ppermute | solution.py:172
  43.5 0.0 collective-permute-done.5.refs_0_
  43.6 0.0 collective-permute-done.6.refs_1_
  43.6 1.9 %collective-permute-done.7.refs_7_.refs_8_ = bf16[2,384,512]{2,1,0:T(8,128)(2,1)S(1)} collective-permute-done((bf16[2,384,512]{2,1,0:T(8,128)(2,1)S(1)}, bf16[2,384,512]{2,1,0:T(8,128)(2,1)S(1)}, u32[]{:S(2)}, u32[]{:S(2)}) %collective-permute-start.7) | collective-permute-done | bytes 786464 | tf_op jit(solution)/shard_map/ppermute | solution.py:172
  45.4 8.5 %attention_backward.2 = (bf16[128,4096]{1,0:T(8,128)(2,1)}, f32[2,384,512]{2,1,0:T(8,128)S(1)}, bf16[2,384,512]{2,1,0:T(8,128)(2,1)S(1)}, bf16[2,128,512]{2,1,0:T(8,128)(2,1)S(1)}) custom-call(s32[1,7]{1,0:T(1,128)S(1)} %copy-done.3, bf16[128,4096]{1,0:T(8,128)(2,1)S(1)} %bitcast.7, bf16[128,2048]{1,0:T(8,128)(2,1)S(1)} %get-tuple-element.22.refs_2_, ...), custom_call_target="tpu_custom_call" | custom-call | flops 2147483648 | bytes 2097152 | tf_op jit(solution)/shard_map/attention_backward/pallas_call | solution.py:79
  53.9 0.0 collective-permute-done.4.refs_0_
  53.9 0.0 collective-permute-done.3.refs_2_
  53.9 8.5 %attention_backward.3 = (bf16[128,4096]{1,0:T(8,128)(2,1)}, f32[2,384,512]{2,1,0:T(8,128)S(1)}, bf16[2,384,512]{2,1,0:T(8,128)(2,1)S(1)}, bf16[2,128,512]{2,1,0:T(8,128)(2,1)S(1)}) custom-call(s32[1,7]{1,0:T(1,128)S(1)} %copy-done.3, bf16[128,4096]{1,0:T(8,128)(2,1)S(1)} %bitcast.8, ...), custom_call_target="tpu_custom_call", output_to_operand_aliasing={{0}: (9, {}), {1}: (10, {}), {2}: (11, {}), {3}: (12, {})} | custom-call | flops 2147483648 | bytes 2097152 | tf_op jit(solution)/shard_map/attention_backward/pallas_call | solution.py:79
  62.4 2.3 %collective-permute-start.8 = (bf16[2,384,512]{2,1,0:T(8,128)(2,1)S(1)}, bf16[2,384,512]{2,1,0:T(8,128)(2,1)S(1)}, u32[]{:S(2)}, u32[]{:S(2)}) collective-permute-start(bf16[2,384,512]{2,1,0:T(8,128)(2,1)S(1)} %get-tuple-element.34), channel_id=1, source_target_pairs={{0,1},{1,0},{2,3},{3,2},{4,5},{5,4},{6,7},{7,6},{8,9},{9,8},{10,11... | collective-permute-start | bytes 2359304 | tf_op jit(solution)/shard_map/ppermute | solution.py:183
  64.7 1.9 %collective-permute-start.9 = (bf16[2,128,512]{2,1,0:T(8,128)(2,1)S(1)}, bf16[2,128,512]{2,1,0:T(8,128)(2,1)S(1)}, u32[]{:S(2)}, u32[]{:S(2)}) collective-permute-start(bf16[2,128,512]{2,1,0:T(8,128)(2,1)S(1)} %get-tuple-element.35), channel_id=1, source_target_pairs={{1,4},{3,6},{4,1},{5,8},{6,3},{7,10},{8,5},{9,12},{10,7},{11,14},{... | collective-permute-start | bytes 786440 | tf_op jit(solution)/shard_map/ppermute | solution.py:182
  66.6 0.3 fusion.3
  67.0 1.9 %collective-permute-start.11 = (bf16[2,128,512]{2,1,0:T(8,128)(2,1)S(1)}, bf16[2,128,512]{2,1,0:T(8,128)(2,1)S(1)}, u32[]{:S(2)}, u32[]{:S(2)}) collective-permute-start(bf16[2,128,512]{2,1,0:T(8,128)(2,1)S(1)} %get-tuple-element.43), channel_id=1, source_target_pairs={{0,2},{1,3},{2,4},{3,5},{4,6},{5,7},{6,8},{7,9},{8,10},{9,11},{10,... | collective-permute-start | bytes 786440 | tf_op jit(solution)/shard_map/ppermute | solution.py:187
  68.9 3.9 %collective-permute-start.10 = (bf16[2,128,512]{2,1,0:T(8,128)(2,1)S(1)}, bf16[2,128,512]{2,1,0:T(8,128)(2,1)S(1)}, u32[]{:S(2)}, u32[]{:S(2)}) collective-permute-start(bf16[2,128,512]{2,1,0:T(8,128)(2,1)S(1)} %get-tuple-element.44), channel_id=1, source_target_pairs={{2,0},{3,1},{4,2},{5,3},{6,4},{7,5},{8,6},{9,7},{10,8},{11,9},{12,... | collective-permute-start | bytes 786440 | tf_op jit(solution)/shard_map/ppermute | solution.py:186
  72.9 1.0 %collective-permute-done.9.refs_0_ = bf16[2,128,512]{2,1,0:T(8,128)(2,1)S(1)} collective-permute-done((bf16[2,128,512]{2,1,0:T(8,128)(2,1)S(1)}, bf16[2,128,512]{2,1,0:T(8,128)(2,1)S(1)}, u32[]{:S(2)}, u32[]{:S(2)}) %collective-permute-start.9) | collective-permute-done | bytes 262176 | tf_op jit(solution)/shard_map/ppermute | solution.py:182
  73.9 3.5 %collective-permute-done.11.refs_2_ = bf16[2,128,512]{2,1,0:T(8,128)(2,1)S(1)} collective-permute-done((bf16[2,128,512]{2,1,0:T(8,128)(2,1)S(1)}, bf16[2,128,512]{2,1,0:T(8,128)(2,1)S(1)}, u32[]{:S(2)}, u32[]{:S(2)}) %collective-permute-start.11) | collective-permute-done | bytes 262176 | tf_op jit(solution)/shard_map/ppermute | solution.py:187
  77.4 13.6 %collective-permute-done.10.refs_1_ = bf16[2,128,512]{2,1,0:T(8,128)(2,1)S(1)} collective-permute-done((bf16[2,128,512]{2,1,0:T(8,128)(2,1)S(1)}, bf16[2,128,512]{2,1,0:T(8,128)(2,1)S(1)}, u32[]{:S(2)}, u32[]{:S(2)}) %collective-permute-start.10) | collective-permute-done | bytes 262176 | tf_op jit(solution)/shard_map/ppermute | solution.py:186
  91.0 0.2 fusion.2
  91.1 0.7 fusion.6
  (14 shorter events, 0.1 us)
Async XLA Ops:
  0.6 2.1 %copy-start.1 = (bf16[1,128,512]{2,1,0:T(8,128)(2,1)S(1)}, bf16[1,128,512]{2,1,0:T(8,128)(2,1)}, u32[]{:S(2)}) copy-start(bf16[1,128,512]{2,1,0:T(8,128)(2,1)} %param.7) | copy-start | bytes 393220
  0.6 2.1 %copy-start = (bf16[1,128,512]{2,1,0:T(8,128)(2,1)S(1)}, bf16[1,128,512]{2,1,0:T(8,128)(2,1)}, u32[]{:S(2)}) copy-start(bf16[1,128,512]{2,1,0:T(8,128)(2,1)} %param.6) | copy-start | bytes 393220
  2.0 16.9 %collective-permute-start.2 = (bf16[128,2048]{1,0:T(8,128)(2,1)S(1)}, bf16[128,2048]{1,0:T(8,128)(2,1)S(1)}, u32[]{:S(2)}, u32[]{:S(2)}) collective-permute-start(bf16[128,2048]{1,0:T(8,128)(2,1)S(1)} %get-tuple-element.21), channel_id=1, source_target_pairs={{0,256},{256,0},{1,257},{257,1},{2,258},{258,2},{3,259},{259,3},{4... | collective-permute-start | bytes 1572872 | tf_op jit(solution)/shard_map/ppermute | solution.py:170
  2.7 40.8 %collective-permute-start.5 = (bf16[2,128,512]{2,1,0:T(8,128)(2,1)S(1)}, bf16[2,128,512]{2,1,0:T(8,128)(2,1)S(1)}, u32[]{:S(2)}, u32[]{:S(2)}) collective-permute-start(bf16[2,128,512]{2,1,0:T(8,128)(2,1)S(1)} %join.1.own.refs_3_.refs_4_), channel_id=1, source_target_pairs={{1,4},{3,6},{4,1},{5,8},{6,3},{7,10},{8,5},{9,12},{10,7},{11,14},{... | collective-permute-start | bytes 786440 | tf_op jit(solution)/shard_map/ppermute | solution.py:168
  5.5 14.7 %collective-permute-start.1 = (bf16[2,128,512]{2,1,0:T(8,128)(2,1)S(1)}, bf16[2,128,512]{2,1,0:T(8,128)(2,1)S(1)}, u32[]{:S(2)}, u32[]{:S(2)}) collective-permute-start(bf16[2,128,512]{2,1,0:T(8,128)(2,1)S(1)} %join.1.own.refs_3_.refs_4_), channel_id=1, source_target_pairs={{2,0},{3,1},{4,2},{5,3},{6,4},{7,5},{8,6},{9,7},{10,8},{11,9},{12,... | collective-permute-start | bytes 786440 | tf_op jit(solution)/shard_map/ppermute | solution.py:166
  7.4 16.0 %collective-permute-start = (bf16[2,128,512]{2,1,0:T(8,128)(2,1)S(1)}, bf16[2,128,512]{2,1,0:T(8,128)(2,1)S(1)}, u32[]{:S(2)}, u32[]{:S(2)}) collective-permute-start(bf16[2,128,512]{2,1,0:T(8,128)(2,1)S(1)} %join.1.own.refs_3_.refs_4_), channel_id=1, source_target_pairs={{0,2},{1,3},{2,4},{3,5},{4,6},{5,7},{6,8},{7,9},{8,10},{9,11},{10,... | collective-permute-start | bytes 786440 | tf_op jit(solution)/shard_map/ppermute | solution.py:165
  15.6 28.0 %collective-permute-start.6 = (bf16[128,2048]{1,0:T(8,128)(2,1)S(1)}, bf16[128,2048]{1,0:T(8,128)(2,1)S(1)}, u32[]{:S(2)}, u32[]{:S(2)}) collective-permute-start(bf16[128,2048]{1,0:T(8,128)(2,1)S(1)} %get-tuple-element.41), channel_id=1, source_target_pairs={{0,480},{32,0},{64,32},{96,64},{128,96},{160,128},{192,160},{224,1... | collective-permute-start | bytes 1572872 | tf_op jit(solution)/shard_map/ppermute | solution.py:168
  18.9 35.0 %collective-permute-start.4 = (bf16[128,2048]{1,0:T(8,128)(2,1)S(1)}, bf16[128,2048]{1,0:T(8,128)(2,1)S(1)}, u32[]{:S(2)}, u32[]{:S(2)}) collective-permute-start(bf16[128,2048]{1,0:T(8,128)(2,1)S(1)} %hold.5), channel_id=1, source_target_pairs={{0,224},{256,480},{1,225},{257,481},{2,226},{258,482},{3,227},{259... | collective-permute-start | bytes 1572872 | tf_op jit(solution)/shard_map/ppermute | solution.py:174
  23.5 30.5 %collective-permute-start.3 = (bf16[128,2048]{1,0:T(8,128)(2,1)S(1)}, bf16[128,2048]{1,0:T(8,128)(2,1)S(1)}, u32[]{:S(2)}, u32[]{:S(2)}) collective-permute-start(bf16[128,2048]{1,0:T(8,128)(2,1)S(1)} %get-tuple-element.21), channel_id=1, source_target_pairs={{32,0},{64,32},{96,64},{128,96},{160,128},{192,160},{224,192},{288... | collective-permute-start | bytes 1572872 | tf_op jit(solution)/shard_map/ppermute | solution.py:173
  26.8 18.6 %copy-start.2 = (bf16[1,128,4096]{2,1,0:T(8,128)(2,1)S(1)}, bf16[1,128,4096]{2,1,0:T(8,128)(2,1)}, u32[]{:S(2)}) copy-start(bf16[1,128,4096]{2,1,0:T(8,128)(2,1)} %param.5) | copy-start | bytes 3145732
  26.8 18.6 %copy-start.3 = (s32[1,7]{1,0:T(1,128)S(1)}, s32[1,7]{1,0:T(1,128)}, u32[]{:S(2)}) copy-start(s32[1,7]{1,0:T(1,128)} %refs_0_.3) | copy-start | bytes 88
  26.8 18.6 %collective-permute-start.7 = (bf16[2,384,512]{2,1,0:T(8,128)(2,1)S(1)}, bf16[2,384,512]{2,1,0:T(8,128)(2,1)S(1)}, u32[]{:S(2)}, u32[]{:S(2)}) collective-permute-start(bf16[2,384,512]{2,1,0:T(8,128)(2,1)S(1)} %bundle.1), channel_id=1, source_target_pairs={{0,1},{1,0},{2,3},{3,2},{4,5},{5,4},{6,7},{7,6},{8,9},{9,8},{10,11... | collective-permute-start | bytes 2359304 | tf_op jit(solution)/shard_map/ppermute | solution.py:172
  62.4 4.2 %collective-permute-start.8 = (bf16[2,384,512]{2,1,0:T(8,128)(2,1)S(1)}, bf16[2,384,512]{2,1,0:T(8,128)(2,1)S(1)}, u32[]{:S(2)}, u32[]{:S(2)}) collective-permute-start(bf16[2,384,512]{2,1,0:T(8,128)(2,1)S(1)} %get-tuple-element.34), channel_id=1, source_target_pairs={{0,1},{1,0},{2,3},{3,2},{4,5},{5,4},{6,7},{7,6},{8,9},{9,8},{10,11... | collective-permute-start | bytes 2359304 | tf_op jit(solution)/shard_map/ppermute | solution.py:183
  64.7 9.2 %collective-permute-start.9 = (bf16[2,128,512]{2,1,0:T(8,128)(2,1)S(1)}, bf16[2,128,512]{2,1,0:T(8,128)(2,1)S(1)}, u32[]{:S(2)}, u32[]{:S(2)}) collective-permute-start(bf16[2,128,512]{2,1,0:T(8,128)(2,1)S(1)} %get-tuple-element.35), channel_id=1, source_target_pairs={{1,4},{3,6},{4,1},{5,8},{6,3},{7,10},{8,5},{9,12},{10,7},{11,14},{... | collective-permute-start | bytes 786440 | tf_op jit(solution)/shard_map/ppermute | solution.py:182
  67.0 10.4 %collective-permute-start.11 = (bf16[2,128,512]{2,1,0:T(8,128)(2,1)S(1)}, bf16[2,128,512]{2,1,0:T(8,128)(2,1)S(1)}, u32[]{:S(2)}, u32[]{:S(2)}) collective-permute-start(bf16[2,128,512]{2,1,0:T(8,128)(2,1)S(1)} %get-tuple-element.43), channel_id=1, source_target_pairs={{0,2},{1,3},{2,4},{3,5},{4,6},{5,7},{6,8},{7,9},{8,10},{9,11},{10,... | collective-permute-start | bytes 786440 | tf_op jit(solution)/shard_map/ppermute | solution.py:187
  68.9 22.1 %collective-permute-start.10 = (bf16[2,128,512]{2,1,0:T(8,128)(2,1)S(1)}, bf16[2,128,512]{2,1,0:T(8,128)(2,1)S(1)}, u32[]{:S(2)}, u32[]{:S(2)}) collective-permute-start(bf16[2,128,512]{2,1,0:T(8,128)(2,1)S(1)} %get-tuple-element.44), channel_id=1, source_target_pairs={{2,0},{3,1},{4,2},{5,3},{6,4},{7,5},{8,6},{9,7},{10,8},{11,9},{12,... | collective-permute-start | bytes 786440 | tf_op jit(solution)/shard_map/ppermute | solution.py:186

commit v10 on v9

--- a/solution.py
+++ b/solution.py
@@ -165,19 +165,17 @@
     left = lax.ppermute(own, "seq", shift_pairs(count, 2))
     right = lax.ppermute(own, "seq", shift_pairs(count, -2))
     far, grad_low = hold(
-        lax.ppermute(own, "seq", far_pairs(count)), lax.ppermute(low, "section", before), flops=1 << 33
-    )
-    (turned,) = hold(lax.ppermute(high, "section", [(0, turn), (turn, 0)]), flops=1 << 33)
+        lax.ppermute(own, "seq", far_pairs(count)), lax.ppermute(low, "section", [(i, i - 1) for i in range(sections) if i % turn]), flops=1 << 33
+    )
+    (turned,) = hold(lax.ppermute(low, "section", [(0, turn), (turn, 0)]), flops=1 << 33)
     left, right, late, _ = lax.optimization_barrier((left, right, high, turned))
     mate = lax.ppermute(bundle(own, left, right), "seq", mate_pairs(count))
-    grad_high = lax.ppermute(late, "section", [(i, i - 1) for i in range(sections) if i % turn])
-    grad_wrap = lax.ppermute(turned, "section", [(0, turn - 1), (turn, sections - 1)])
+    grad_high = lax.ppermute(late, "section", before)
+    (grad_wrap,) = hold(lax.ppermute(turned, "section", [(0, turn - 1), (turn, sections - 1)]), flops=1 << 33)
     slots = (own, left, right, far, mate)
-    kept = attention_backward(block_mask, query_heads[0], (grad_low,), slots, 0, 2, ())
-    grad_wrap, last = hold(grad_wrap, kept[3], flops=1 << 31)
-    kept = [*kept[:3], last]
+    kept = attention_backward(block_mask, query_heads[0], (grad_low, grad_wrap), slots, 0, 2, ())
     query_grad, parts, to_mate, to_far = attention_backward(
-        block_mask, query_heads[0], (grad_high, grad_wrap), slots, 2, 2, kept
+        block_mask, query_heads[0], (grad_high,), slots, 2, 2, kept
     )
     (back_far,) = hold(lax.ppermute(to_far, "seq", far_pairs(count)), flops=1 << 33)
     sums = parts + lax.ppermute(to_mate, "seq", mate_pairs(count)).astype(F32)

time: 92.3 us -> 91.1 us (0.987)
  the two profiles are of different devices: /device:TPU:254 before, /device:TPU:206 now
where the time goes in v10:
time: 91.1 us; the launch traced here: 90.6 us
  starting transfers between devices  45.7 us (50%)
  waiting for transfers between devices  24.4 us (27%)
  Pallas kernels  17 us (19%)
  local copies, waits for them, and re-layouts  2.11 us (2%)
    pallas_call x2, Pallas kernels, attention_backward(): pl.pallas_call(functools.partial(backward_body, len(grads), len(kept)), g...  17 us
    ppermute x1, starting transfers between devices, shards(): grad_high = lax.ppermute(late, 'section', before)  16.2 us
    ppermute x1, waiting for transfers between devices, shards(): lax.ppermute(sums[:, BL:2 * BL].astype(B16), 'seq', shift_pairs(count, -2))  14.1 us
    ppermute x1, starting transfers between devices, shards(): left = lax.ppermute(own, 'seq', shift_pairs(count, 2))  8.14 us
    ppermute x1, starting transfers between devices, shards(): lax.ppermute(sums[:, BL:2 * BL].astype(B16), 'seq', shift_pairs(count, -2))  3.92 us
    ppermute x1, starting transfers between devices, shards(): lax.ppermute(low, 'section', [(i, i - 1) for i in range(sections) if i %...  3.58 us
    ppermute x1, waiting for transfers between devices, shards(): left = lax.ppermute(own, 'seq', shift_pairs(count, 2))  3.56 us
    ppermute x1, waiting for transfers between devices, shards(): lax.ppermute(sums[:, 2 * BL:].astype(B16), 'seq', shift_pairs(count, 2))  3.55 us
  transfers between devices with their start and end apart: 12, of which 6 were waited for; matrix products, arithmetic and copies ran while one was open for 0% of the time, Pallas kernels for 9%

profile of v10, /device:TPU:206, one launch (start us, length us, event | category | flops | bytes accessed | tf_op | source)
XLA Modules:
  0.0 90.6 jit_solution(12561396876419810821)
XLA Ops:
  0.7 1.3 %fusion.4 = (bf16[128,2048]{1,0:T(8,128)(2,1)S(1)}, bf16[128,2048]{1,0:T(8,128)(2,1)S(1)}) fusion(bf16[128,4096]{1,0:T(8,128)(2,1)} %bitcast.9), kind=kLoop, calls=%fused_computation.6 | loop fusion | bytes 2097152 | tf_op jit(solution)/shard_map/slice | solution.py:162
  2.0 0.7 collective-permute-start.2
  2.7 2.8 %collective-permute-start.4 = (bf16[2,128,512]{2,1,0:T(8,128)(2,1)S(1)}, bf16[2,128,512]{2,1,0:T(8,128)(2,1)S(1)}, u32[]{:S(2)}, u32[]{:S(2)}) collective-permute-start(bf16[2,128,512]{2,1,0:T(8,128)(2,1)S(1)} %join.1.own.refs_4_.refs_3_), channel_id=1, source_target_pairs={{1,4},{3,6},{4,1},{5,8},{6,3},{7,10},{8,5},{9,12},{10,7},{11,14},{... | collective-permute-start | bytes 786440 | tf_op jit(solution)/shard_map/ppermute | solution.py:168
  5.5 1.9 %collective-permute-start.1 = (bf16[2,128,512]{2,1,0:T(8,128)(2,1)S(1)}, bf16[2,128,512]{2,1,0:T(8,128)(2,1)S(1)}, u32[]{:S(2)}, u32[]{:S(2)}) collective-permute-start(bf16[2,128,512]{2,1,0:T(8,128)(2,1)S(1)} %join.1.own.refs_4_.refs_3_), channel_id=1, source_target_pairs={{2,0},{3,1},{4,2},{5,3},{6,4},{7,5},{8,6},{9,7},{10,8},{11,9},{12,... | collective-permute-start | bytes 786440 | tf_op jit(solution)/shard_map/ppermute | solution.py:166
  7.4 8.1 %collective-permute-start = (bf16[2,128,512]{2,1,0:T(8,128)(2,1)S(1)}, bf16[2,128,512]{2,1,0:T(8,128)(2,1)S(1)}, u32[]{:S(2)}, u32[]{:S(2)}) collective-permute-start(bf16[2,128,512]{2,1,0:T(8,128)(2,1)S(1)} %join.1.own.refs_4_.refs_3_), channel_id=1, source_target_pairs={{0,2},{1,3},{2,4},{3,5},{4,6},{5,7},{6,8},{7,9},{8,10},{9,11},{10,... | collective-permute-start | bytes 786440 | tf_op jit(solution)/shard_map/ppermute | solution.py:165
  15.6 3.6 %collective-permute-start.5 = (bf16[128,2048]{1,0:T(8,128)(2,1)S(1)}, bf16[128,2048]{1,0:T(8,128)(2,1)S(1)}, u32[]{:S(2)}, u32[]{:S(2)}) collective-permute-start(bf16[128,2048]{1,0:T(8,128)(2,1)S(1)} %get-tuple-element.37), channel_id=1, source_target_pairs={{32,0},{64,32},{96,64},{128,96},{160,128},{192,160},{224,192},{288... | collective-permute-start | bytes 1572872 | tf_op jit(solution)/shard_map/ppermute | solution.py:168
  19.2 0.0 collective-permute-done.2.refs_0_
  19.2 0.7 collective-permute-start.7
  19.9 0.0 collective-permute-done.1.right.refs_6_.refs_5_
  19.9 3.6 %collective-permute-done.left.refs_5_.refs_4_ = bf16[2,128,512]{2,1,0:T(8,128)(2,1)S(1)} collective-permute-done((bf16[2,128,512]{2,1,0:T(8,128)(2,1)S(1)}, bf16[2,128,512]{2,1,0:T(8,128)(2,1)S(1)}, u32[]{:S(2)}, u32[]{:S(2)}) %collective-permute-start) | collective-permute-done | bytes 262176 | tf_op jit(solution)/shard_map/ppermute | solution.py:165
  23.5 16.2 %collective-permute-start.3 = (bf16[128,2048]{1,0:T(8,128)(2,1)S(1)}, bf16[128,2048]{1,0:T(8,128)(2,1)S(1)}, u32[]{:S(2)}, u32[]{:S(2)}) collective-permute-start(bf16[128,2048]{1,0:T(8,128)(2,1)S(1)} %get-tuple-element.19), channel_id=1, source_target_pairs={{0,480},{32,0},{64,32},{96,64},{128,96},{160,128},{192,160},{224,1... | collective-permute-start | bytes 1572872 | tf_op jit(solution)/shard_map/ppermute | solution.py:173
  39.7 0.1 bundle.1
  39.8 1.9 %collective-permute-start.6 = (bf16[2,384,512]{2,1,0:T(8,128)(2,1)S(1)}, bf16[2,384,512]{2,1,0:T(8,128)(2,1)S(1)}, u32[]{:S(2)}, u32[]{:S(2)}) collective-permute-start(bf16[2,384,512]{2,1,0:T(8,128)(2,1)S(1)} %bundle.1), channel_id=1, source_target_pairs={{0,1},{1,0},{2,3},{3,2},{4,5},{5,4},{6,7},{7,6},{8,9},{9,8},{10,11... | collective-permute-start | bytes 2359304 | tf_op jit(solution)/shard_map/ppermute | solution.py:172
  41.7 0.0 collective-permute-done.4.refs_0_
  41.7 0.0 collective-permute-done.5.refs_1_
  41.7 0.0 copy-start.2
  41.7 0.0 copy-start.3
  41.7 0.0 collective-permute-done.7.refs_0_
  41.8 2.2 %collective-permute-done.6.refs_8_.refs_7_ = bf16[2,384,512]{2,1,0:T(8,128)(2,1)S(1)} collective-permute-done((bf16[2,384,512]{2,1,0:T(8,128)(2,1)S(1)}, bf16[2,384,512]{2,1,0:T(8,128)(2,1)S(1)}, u32[]{:S(2)}, u32[]{:S(2)}) %collective-permute-start.6) | collective-permute-done | bytes 786464 | tf_op jit(solution)/shard_map/ppermute | solution.py:172
  43.9 8.5 %attention_backward.2 = (bf16[128,4096]{1,0:T(8,128)(2,1)}, f32[2,384,512]{2,1,0:T(8,128)S(1)}, bf16[2,384,512]{2,1,0:T(8,128)(2,1)S(1)}, bf16[2,128,512]{2,1,0:T(8,128)(2,1)S(1)}) custom-call(s32[1,7]{1,0:T(1,128)S(1)} %copy-done.3, bf16[128,4096]{1,0:T(8,128)(2,1)S(1)} %bitcast.7, bf16[128,2048]{1,0:T(8,128)(2,1)S(1)} %get-tuple-element.23.refs_2_, ...), custom_call_target="tpu_custom_call" | custom-call | flops 2147483648 | bytes 2097152 | tf_op jit(solution)/shard_map/attention_backward/pallas_call | solution.py:79
  52.4 8.5 %attention_backward.3 = (bf16[128,4096]{1,0:T(8,128)(2,1)}, f32[2,384,512]{2,1,0:T(8,128)S(1)}, bf16[2,384,512]{2,1,0:T(8,128)(2,1)S(1)}, bf16[2,128,512]{2,1,0:T(8,128)(2,1)S(1)}) custom-call(s32[1,7]{1,0:T(1,128)S(1)} %copy-done.3, bf16[128,4096]{1,0:T(8,128)(2,1)S(1)} %bitcast.8, ...), custom_call_target="tpu_custom_call", output_to_operand_aliasing={{0}: (8, {}), {1}: (9, {}), {2}: (10, {}), {3}: (11, {})} | custom-call | flops 2147483648 | bytes 2097152 | tf_op jit(solution)/shard_map/attention_backward/pallas_call | solution.py:79
  60.9 2.0 %collective-permute-start.8 = (bf16[2,384,512]{2,1,0:T(8,128)(2,1)S(1)}, bf16[2,384,512]{2,1,0:T(8,128)(2,1)S(1)}, u32[]{:S(2)}, u32[]{:S(2)}) collective-permute-start(bf16[2,384,512]{2,1,0:T(8,128)(2,1)S(1)} %get-tuple-element.30), channel_id=1, source_target_pairs={{0,1},{1,0},{2,3},{3,2},{4,5},{5,4},{6,7},{7,6},{8,9},{9,8},{10,11... | collective-permute-start | bytes 2359304 | tf_op jit(solution)/shard_map/ppermute | solution.py:181
  63.0 1.9 %collective-permute-start.9 = (bf16[2,128,512]{2,1,0:T(8,128)(2,1)S(1)}, bf16[2,128,512]{2,1,0:T(8,128)(2,1)S(1)}, u32[]{:S(2)}, u32[]{:S(2)}) collective-permute-start(bf16[2,128,512]{2,1,0:T(8,128)(2,1)S(1)} %get-tuple-element.31), channel_id=1, source_target_pairs={{1,4},{3,6},{4,1},{5,8},{6,3},{7,10},{8,5},{9,12},{10,7},{11,14},{... | collective-permute-start | bytes 786440 | tf_op jit(solution)/shard_map/ppermute | solution.py:180
  64.9 0.2 collective-permute-done.8
  65.1 0.3 fusion.3
  65.4 1.9 %collective-permute-start.11 = (bf16[2,128,512]{2,1,0:T(8,128)(2,1)S(1)}, bf16[2,128,512]{2,1,0:T(8,128)(2,1)S(1)}, u32[]{:S(2)}, u32[]{:S(2)}) collective-permute-start(bf16[2,128,512]{2,1,0:T(8,128)(2,1)S(1)} %get-tuple-element.39), channel_id=1, source_target_pairs={{0,2},{1,3},{2,4},{3,5},{4,6},{5,7},{6,8},{7,9},{8,10},{9,11},{10,... | collective-permute-start | bytes 786440 | tf_op jit(solution)/shard_map/ppermute | solution.py:185
  67.3 3.9 %collective-permute-start.10 = (bf16[2,128,512]{2,1,0:T(8,128)(2,1)S(1)}, bf16[2,128,512]{2,1,0:T(8,128)(2,1)S(1)}, u32[]{:S(2)}, u32[]{:S(2)}) collective-permute-start(bf16[2,128,512]{2,1,0:T(8,128)(2,1)S(1)} %get-tuple-element.40), channel_id=1, source_target_pairs={{2,0},{3,1},{4,2},{5,3},{6,4},{7,5},{8,6},{9,7},{10,8},{11,9},{12,... | collective-permute-start | bytes 786440 | tf_op jit(solution)/shard_map/ppermute | solution.py:184
  71.3 0.9 collective-permute-done.9.refs_0_
  72.2 3.6 %collective-permute-done.11.refs_2_ = bf16[2,128,512]{2,1,0:T(8,128)(2,1)S(1)} collective-permute-done((bf16[2,128,512]{2,1,0:T(8,128)(2,1)S(1)}, bf16[2,128,512]{2,1,0:T(8,128)(2,1)S(1)}, u32[]{:S(2)}, u32[]{:S(2)}) %collective-permute-start.11) | collective-permute-done | bytes 262176 | tf_op jit(solution)/shard_map/ppermute | solution.py:185
  75.7 14.1 %collective-permute-done.10.refs_1_ = bf16[2,128,512]{2,1,0:T(8,128)(2,1)S(1)} collective-permute-done((bf16[2,128,512]{2,1,0:T(8,128)(2,1)S(1)}, bf16[2,128,512]{2,1,0:T(8,128)(2,1)S(1)}, u32[]{:S(2)}, u32[]{:S(2)}) %collective-permute-start.10) | collective-permute-done | bytes 262176 | tf_op jit(solution)/shard_map/ppermute | solution.py:184
  89.8 0.2 fusion.2
  89.9 0.7 fusion.6
  (14 shorter events, 0.1 us)
Async XLA Ops:
  0.6 2.1 %copy-start.1 = (bf16[1,128,512]{2,1,0:T(8,128)(2,1)S(1)}, bf16[1,128,512]{2,1,0:T(8,128)(2,1)}, u32[]{:S(2)}) copy-start(bf16[1,128,512]{2,1,0:T(8,128)(2,1)} %param.7) | copy-start | bytes 393220
  0.6 2.1 %copy-start = (bf16[1,128,512]{2,1,0:T(8,128)(2,1)S(1)}, bf16[1,128,512]{2,1,0:T(8,128)(2,1)}, u32[]{:S(2)}) copy-start(bf16[1,128,512]{2,1,0:T(8,128)(2,1)} %param.6) | copy-start | bytes 393220
  2.0 17.2 %collective-permute-start.2 = (bf16[128,2048]{1,0:T(8,128)(2,1)S(1)}, bf16[128,2048]{1,0:T(8,128)(2,1)S(1)}, u32[]{:S(2)}, u32[]{:S(2)}) collective-permute-start(bf16[128,2048]{1,0:T(8,128)(2,1)S(1)} %get-tuple-element.37), channel_id=1, source_target_pairs={{0,256},{256,0},{1,257},{257,1},{2,258},{258,2},{3,259},{259,3},{4... | collective-permute-start | bytes 1572872 | tf_op jit(solution)/shard_map/ppermute | solution.py:170
  2.7 38.9 %collective-permute-start.4 = (bf16[2,128,512]{2,1,0:T(8,128)(2,1)S(1)}, bf16[2,128,512]{2,1,0:T(8,128)(2,1)S(1)}, u32[]{:S(2)}, u32[]{:S(2)}) collective-permute-start(bf16[2,128,512]{2,1,0:T(8,128)(2,1)S(1)} %join.1.own.refs_4_.refs_3_), channel_id=1, source_target_pairs={{1,4},{3,6},{4,1},{5,8},{6,3},{7,10},{8,5},{9,12},{10,7},{11,14},{... | collective-permute-start | bytes 786440 | tf_op jit(solution)/shard_map/ppermute | solution.py:168
  5.5 14.4 %collective-permute-start.1 = (bf16[2,128,512]{2,1,0:T(8,128)(2,1)S(1)}, bf16[2,128,512]{2,1,0:T(8,128)(2,1)S(1)}, u32[]{:S(2)}, u32[]{:S(2)}) collective-permute-start(bf16[2,128,512]{2,1,0:T(8,128)(2,1)S(1)} %join.1.own.refs_4_.refs_3_), channel_id=1, source_target_pairs={{2,0},{3,1},{4,2},{5,3},{6,4},{7,5},{8,6},{9,7},{10,8},{11,9},{12,... | collective-permute-start | bytes 786440 | tf_op jit(solution)/shard_map/ppermute | solution.py:166
  7.4 16.0 %collective-permute-start = (bf16[2,128,512]{2,1,0:T(8,128)(2,1)S(1)}, bf16[2,128,512]{2,1,0:T(8,128)(2,1)S(1)}, u32[]{:S(2)}, u32[]{:S(2)}) collective-permute-start(bf16[2,128,512]{2,1,0:T(8,128)(2,1)S(1)} %join.1.own.refs_4_.refs_3_), channel_id=1, source_target_pairs={{0,2},{1,3},{2,4},{3,5},{4,6},{5,7},{6,8},{7,9},{8,10},{9,11},{10,... | collective-permute-start | bytes 786440 | tf_op jit(solution)/shard_map/ppermute | solution.py:165
  15.6 26.1 %collective-permute-start.5 = (bf16[128,2048]{1,0:T(8,128)(2,1)S(1)}, bf16[128,2048]{1,0:T(8,128)(2,1)S(1)}, u32[]{:S(2)}, u32[]{:S(2)}) collective-permute-start(bf16[128,2048]{1,0:T(8,128)(2,1)S(1)} %get-tuple-element.37), channel_id=1, source_target_pairs={{32,0},{64,32},{96,64},{128,96},{160,128},{192,160},{224,192},{288... | collective-permute-start | bytes 1572872 | tf_op jit(solution)/shard_map/ppermute | solution.py:168
  19.2 22.6 %collective-permute-start.7 = (bf16[128,2048]{1,0:T(8,128)(2,1)S(1)}, bf16[128,2048]{1,0:T(8,128)(2,1)S(1)}, u32[]{:S(2)}, u32[]{:S(2)}) collective-permute-start(bf16[128,2048]{1,0:T(8,128)(2,1)S(1)} %hold.5), channel_id=1, source_target_pairs={{0,224},{256,480},{1,225},{257,481},{2,226},{258,482},{3,227},{259... | collective-permute-start | bytes 1572872 | tf_op jit(solution)/shard_map/ppermute | solution.py:174
  23.5 28.9 %collective-permute-start.3 = (bf16[128,2048]{1,0:T(8,128)(2,1)S(1)}, bf16[128,2048]{1,0:T(8,128)(2,1)S(1)}, u32[]{:S(2)}, u32[]{:S(2)}) collective-permute-start(bf16[128,2048]{1,0:T(8,128)(2,1)S(1)} %get-tuple-element.19), channel_id=1, source_target_pairs={{0,480},{32,0},{64,32},{96,64},{128,96},{160,128},{192,160},{224,1... | collective-permute-start | bytes 1572872 | tf_op jit(solution)/shard_map/ppermute | solution.py:173
  39.8 4.2 %collective-permute-start.6 = (bf16[2,384,512]{2,1,0:T(8,128)(2,1)S(1)}, bf16[2,384,512]{2,1,0:T(8,128)(2,1)S(1)}, u32[]{:S(2)}, u32[]{:S(2)}) collective-permute-start(bf16[2,384,512]{2,1,0:T(8,128)(2,1)S(1)} %bundle.1), channel_id=1, source_target_pairs={{0,1},{1,0},{2,3},{3,2},{4,5},{5,4},{6,7},{7,6},{8,9},{9,8},{10,11... | collective-permute-start | bytes 2359304 | tf_op jit(solution)/shard_map/ppermute | solution.py:172
  41.7 2.2 %copy-start.2 = (bf16[1,128,4096]{2,1,0:T(8,128)(2,1)S(1)}, bf16[1,128,4096]{2,1,0:T(8,128)(2,1)}, u32[]{:S(2)}) copy-start(bf16[1,128,4096]{2,1,0:T(8,128)(2,1)} %param.5) | copy-start | bytes 3145732
  41.7 2.2 %copy-start.3 = (s32[1,7]{1,0:T(1,128)S(1)}, s32[1,7]{1,0:T(1,128)}, u32[]{:S(2)}) copy-start(s32[1,7]{1,0:T(1,128)} %refs_0_.3) | copy-start | bytes 88
  60.9 4.2 %collective-permute-start.8 = (bf16[2,384,512]{2,1,0:T(8,128)(2,1)S(1)}, bf16[2,384,512]{2,1,0:T(8,128)(2,1)S(1)}, u32[]{:S(2)}, u32[]{:S(2)}) collective-permute-start(bf16[2,384,512]{2,1,0:T(8,128)(2,1)S(1)} %get-tuple-element.30), channel_id=1, source_target_pairs={{0,1},{1,0},{2,3},{3,2},{4,5},{5,4},{6,7},{7,6},{8,9},{9,8},{10,11... | collective-permute-start | bytes 2359304 | tf_op jit(solution)/shard_map/ppermute | solution.py:181
  63.0 9.2 %collective-permute-start.9 = (bf16[2,128,512]{2,1,0:T(8,128)(2,1)S(1)}, bf16[2,128,512]{2,1,0:T(8,128)(2,1)S(1)}, u32[]{:S(2)}, u32[]{:S(2)}) collective-permute-start(bf16[2,128,512]{2,1,0:T(8,128)(2,1)S(1)} %get-tuple-element.31), channel_id=1, source_target_pairs={{1,4},{3,6},{4,1},{5,8},{6,3},{7,10},{8,5},{9,12},{10,7},{11,14},{... | collective-permute-start | bytes 786440 | tf_op jit(solution)/shard_map/ppermute | solution.py:180
  65.4 10.3 %collective-permute-start.11 = (bf16[2,128,512]{2,1,0:T(8,128)(2,1)S(1)}, bf16[2,128,512]{2,1,0:T(8,128)(2,1)S(1)}, u32[]{:S(2)}, u32[]{:S(2)}) collective-permute-start(bf16[2,128,512]{2,1,0:T(8,128)(2,1)S(1)} %get-tuple-element.39), channel_id=1, source_target_pairs={{0,2},{1,3},{2,4},{3,5},{4,6},{5,7},{6,8},{7,9},{8,10},{9,11},{10,... | collective-permute-start | bytes 786440 | tf_op jit(solution)/shard_map/ppermute | solution.py:185
  67.3 22.4 %collective-permute-start.10 = (bf16[2,128,512]{2,1,0:T(8,128)(2,1)S(1)}, bf16[2,128,512]{2,1,0:T(8,128)(2,1)S(1)}, u32[]{:S(2)}, u32[]{:S(2)}) collective-permute-start(bf16[2,128,512]{2,1,0:T(8,128)(2,1)S(1)} %get-tuple-element.40), channel_id=1, source_target_pairs={{2,0},{3,1},{4,2},{5,3},{6,4},{7,5},{8,6},{9,7},{10,8},{11,9},{12,... | collective-permute-start | bytes 786440 | tf_op jit(solution)/shard_map/ppermute | solution.py:184

commit v11 on v10

--- a/solution.py
+++ b/solution.py
@@ -159,7 +159,7 @@
     half = HQ * HD // 2
     turn = sections // 2
     cot = section_cotangent[0]
-    low, high = cot[:, :half], cot[:, half:]
+    low = cot[:, :half]
     before = [(i, (i - 1) % sections) for i in range(sections)]
     own = join(key_heads[0], value_heads[0])
     left = lax.ppermute(own, "seq", shift_pairs(count, 2))
@@ -168,9 +168,10 @@
         lax.ppermute(own, "seq", far_pairs(count)), lax.ppermute(low, "section", [(i, i - 1) for i in range(sections) if i % turn]), flops=1 << 33
     )
     (turned,) = hold(lax.ppermute(low, "section", [(0, turn), (turn, 0)]), flops=1 << 33)
-    left, right, late, _ = lax.optimization_barrier((left, right, high, turned))
+    left, right, _ = lax.optimization_barrier((left, right, turned))
     mate = lax.ppermute(bundle(own, left, right), "seq", mate_pairs(count))
-    grad_high = lax.ppermute(late, "section", before)
+    mate, cot = lax.optimization_barrier((mate, cot))
+    grad_high = lax.ppermute(cot[:, half:], "section", before)
     (grad_wrap,) = hold(lax.ppermute(turned, "section", [(0, turn - 1), (turn, sections - 1)]), flops=1 << 33)
     slots = (own, left, right, far, mate)
     kept = attention_backward(block_mask, query_heads[0], (grad_low, grad_wrap), slots, 0, 2, ())

time: 91.1 us -> 95.2 us (1.045)
  the two profiles are of different devices: /device:TPU:206 before, /device:TPU:135 now
where the time goes in v11:
time: 95.2 us; the launch traced here: 94.7 us
  starting transfers between devices  46 us (48%)
  waiting for transfers between devices  26.6 us (28%)
  Pallas kernels  17.1 us (18%)
  local copies, waits for them, and re-layouts  3.7 us (4%)
    pallas_call x2, Pallas kernels, attention_backward(): pl.pallas_call(functools.partial(backward_body, len(grads), len(kept)), g...  17 us
    ppermute x1, waiting for transfers between devices, shards(): lax.ppermute(sums[:, 2 * BL:].astype(B16), 'seq', shift_pairs(count, 2))  8.65 us
    ppermute x1, starting transfers between devices, shards(): lax.ppermute(sums[:, 2 * BL:].astype(B16), 'seq', shift_pairs(count, 2))  8.04 us
    ppermute x1, starting transfers between devices, shards(): lax.ppermute(own, 'seq', far_pairs(count))  7.8 us
    ppermute x1, starting transfers between devices, shards(): left = lax.ppermute(own, 'seq', shift_pairs(count, 2))  7.58 us
    ppermute x1, waiting for transfers between devices, shards(): lax.ppermute(sums[:, BL:2 * BL].astype(B16), 'seq', shift_pairs(count, -2))  6.89 us
    ppermute x1, waiting for transfers between devices, shards(): grad_high = lax.ppermute(cot[:, half:], 'section', before)  4.82 us
    ppermute x1, starting transfers between devices, shards(): lax.ppermute(turned, 'section', [(0, turn - 1), (turn, sections - 1)])  4.15 us
  transfers between devices with their start and end apart: 12, of which 6 were waited for; matrix products, arithmetic and copies ran while one was open for 0% of the time, Pallas kernels for 9%

profile of v11, /device:TPU:135, one launch (start us, length us, event | category | flops | bytes accessed | tf_op | source)
XLA Modules:
  0.0 94.7 jit_solution(8811304412130571032)
XLA Ops:
  0.6 1.1 %slice.30 = bf16[128,2048]{1,0:T(8,128)(2,1)S(1)} slice(bf16[128,4096]{1,0:T(8,128)(2,1)} %bitcast.9), slice={[0:128], [0:2048]} | slice | bytes 1048576 | tf_op jit(solution)/shard_map/slice | solution.py:162
  1.7 4.0 %collective-permute-start.2 = (bf16[128,2048]{1,0:T(8,128)(2,1)S(1)}, bf16[128,2048]{1,0:T(8,128)(2,1)S(1)}, u32[]{:S(2)}, u32[]{:S(2)}) collective-permute-start(bf16[128,2048]{1,0:T(8,128)(2,1)S(1)} %slice.30), channel_id=1, source_target_pairs={{0,256},{256,0},{1,257},{257,1},{2,258},{258,2},{3,259},{259,3},{4... | collective-permute-start | bytes 1572872 | tf_op jit(solution)/shard_map/ppermute | solution.py:170
  5.7 0.0 copy-start
  5.7 0.9 copy-done
  6.6 0.9 copy-done.1
  7.6 7.8 %collective-permute-start.5 = (bf16[2,128,512]{2,1,0:T(8,128)(2,1)S(1)}, bf16[2,128,512]{2,1,0:T(8,128)(2,1)S(1)}, u32[]{:S(2)}, u32[]{:S(2)}) collective-permute-start(bf16[2,128,512]{2,1,0:T(8,128)(2,1)S(1)} %join.1.own.refs_4_.refs_3_), channel_id=1, source_target_pairs={{1,4},{3,6},{4,1},{5,8},{6,3},{7,10},{8,5},{9,12},{10,7},{11,14},{... | collective-permute-start | bytes 786440 | tf_op jit(solution)/shard_map/ppermute | solution.py:168
  15.4 1.9 %collective-permute-start.1 = (bf16[2,128,512]{2,1,0:T(8,128)(2,1)S(1)}, bf16[2,128,512]{2,1,0:T(8,128)(2,1)S(1)}, u32[]{:S(2)}, u32[]{:S(2)}) collective-permute-start(bf16[2,128,512]{2,1,0:T(8,128)(2,1)S(1)} %join.1.own.refs_4_.refs_3_), channel_id=1, source_target_pairs={{2,0},{3,1},{4,2},{5,3},{6,4},{7,5},{8,6},{9,7},{10,8},{11,9},{12,... | collective-permute-start | bytes 786440 | tf_op jit(solution)/shard_map/ppermute | solution.py:166
  17.3 7.6 %collective-permute-start = (bf16[2,128,512]{2,1,0:T(8,128)(2,1)S(1)}, bf16[2,128,512]{2,1,0:T(8,128)(2,1)S(1)}, u32[]{:S(2)}, u32[]{:S(2)}) collective-permute-start(bf16[2,128,512]{2,1,0:T(8,128)(2,1)S(1)} %join.1.own.refs_4_.refs_3_), channel_id=1, source_target_pairs={{0,2},{1,3},{2,4},{3,5},{4,6},{5,7},{6,8},{7,9},{8,10},{9,11},{10,... | collective-permute-start | bytes 786440 | tf_op jit(solution)/shard_map/ppermute | solution.py:165
  24.9 1.3 %collective-permute-start.6 = (bf16[128,2048]{1,0:T(8,128)(2,1)S(1)}, bf16[128,2048]{1,0:T(8,128)(2,1)S(1)}, u32[]{:S(2)}, u32[]{:S(2)}) collective-permute-start(bf16[128,2048]{1,0:T(8,128)(2,1)S(1)} %slice.30), channel_id=1, source_target_pairs={{32,0},{64,32},{96,64},{128,96},{160,128},{192,160},{224,192},{288... | collective-permute-start | bytes 1572872 | tf_op jit(solution)/shard_map/ppermute | solution.py:168
  26.2 4.2 %collective-permute-start.7 = (bf16[128,2048]{1,0:T(8,128)(2,1)S(1)}, bf16[128,2048]{1,0:T(8,128)(2,1)S(1)}, u32[]{:S(2)}, u32[]{:S(2)}) collective-permute-start(bf16[128,2048]{1,0:T(8,128)(2,1)S(1)} %hold.5), channel_id=1, source_target_pairs={{0,224},{256,480},{1,225},{257,481},{2,226},{258,482},{3,227},{259... | collective-permute-start | bytes 1572872 | tf_op jit(solution)/shard_map/ppermute | solution.py:175
  30.4 4.0 %collective-permute-done.left.refs_5_.refs_4_ = bf16[2,128,512]{2,1,0:T(8,128)(2,1)S(1)} collective-permute-done((bf16[2,128,512]{2,1,0:T(8,128)(2,1)S(1)}, bf16[2,128,512]{2,1,0:T(8,128)(2,1)S(1)}, u32[]{:S(2)}, u32[]{:S(2)}) %collective-permute-start) | collective-permute-done | bytes 262176 | tf_op jit(solution)/shard_map/ppermute | solution.py:165
  34.3 0.1 bundle.1
  34.4 0.0 copy-start.4
  34.4 2.1 %collective-permute-start.3 = (bf16[2,384,512]{2,1,0:T(8,128)(2,1)S(1)}, bf16[2,384,512]{2,1,0:T(8,128)(2,1)S(1)}, u32[]{:S(2)}, u32[]{:S(2)}) collective-permute-start(bf16[2,384,512]{2,1,0:T(8,128)(2,1)S(1)} %bundle.1), channel_id=1, source_target_pairs={{0,1},{1,0},{2,3},{3,2},{4,5},{5,4},{6,7},{7,6},{8,9},{9,8},{10,11... | collective-permute-start | bytes 2359304 | tf_op jit(solution)/shard_map/ppermute | solution.py:172
  36.5 0.0 collective-permute-done.5.refs_0_
  36.5 0.6 collective-permute-done.6.refs_1_
  37.1 1.6 %collective-permute-done.3.refs_8_.refs_7_ = bf16[2,384,512]{2,1,0:T(8,128)(2,1)S(1)} collective-permute-done((bf16[2,384,512]{2,1,0:T(8,128)(2,1)S(1)}, bf16[2,384,512]{2,1,0:T(8,128)(2,1)S(1)}, u32[]{:S(2)}, u32[]{:S(2)}) %collective-permute-start.3) | collective-permute-done | bytes 786464 | tf_op jit(solution)/shard_map/ppermute | solution.py:172
  38.8 0.0 copy-start.2
  38.8 0.0 copy-start.3
  38.8 2.1 %collective-permute-start.4 = (bf16[128,2048]{1,0:T(8,128)(2,1)S(1)}, bf16[128,2048]{1,0:T(8,128)(2,1)S(1)}, u32[]{:S(2)}, u32[]{:S(2)}) collective-permute-start(bf16[128,2048]{1,0:T(8,128)(2,1)S(1)} %slice.24), channel_id=1, source_target_pairs={{0,480},{32,0},{64,32},{96,64},{128,96},{160,128},{192,160},{224,1... | collective-permute-start | bytes 1572872 | tf_op jit(solution)/shard_map/ppermute | solution.py:174
  40.9 8.5 %attention_backward.2 = (bf16[128,4096]{1,0:T(8,128)(2,1)}, f32[2,384,512]{2,1,0:T(8,128)S(1)}, bf16[2,384,512]{2,1,0:T(8,128)(2,1)S(1)}, bf16[2,128,512]{2,1,0:T(8,128)(2,1)S(1)}) custom-call(s32[1,7]{1,0:T(1,128)S(1)} %copy-done.3, bf16[128,4096]{1,0:T(8,128)(2,1)S(1)} %bitcast.7, bf16[128,2048]{1,0:T(8,128)(2,1)S(1)} %get-tuple-element.25.refs_2_, ...), custom_call_target="tpu_custom_call" | custom-call | flops 2147483648 | bytes 2097152 | tf_op jit(solution)/shard_map/attention_backward/pallas_call | solution.py:79
  49.4 4.8 %collective-permute-done.4.refs_2_ = bf16[128,2048]{1,0:T(8,128)(2,1)S(1)} collective-permute-done((bf16[128,2048]{1,0:T(8,128)(2,1)S(1)}, bf16[128,2048]{1,0:T(8,128)(2,1)S(1)}, u32[]{:S(2)}, u32[]{:S(2)}) %collective-permute-start.4) | collective-permute-done | bytes 524320 | tf_op jit(solution)/shard_map/ppermute | solution.py:174
  54.2 8.5 %attention_backward.3 = (bf16[128,4096]{1,0:T(8,128)(2,1)}, f32[2,384,512]{2,1,0:T(8,128)S(1)}, bf16[2,384,512]{2,1,0:T(8,128)(2,1)S(1)}, bf16[2,128,512]{2,1,0:T(8,128)(2,1)S(1)}) custom-call(s32[1,7]{1,0:T(1,128)S(1)} %copy-done.3, bf16[128,4096]{1,0:T(8,128)(2,1)S(1)} %bitcast.8, ...), custom_call_target="tpu_custom_call", output_to_operand_aliasing={{0}: (8, {}), {1}: (9, {}), {2}: (10, {}), {3}: (11, {})} | custom-call | flops 2147483648 | bytes 2097152 | tf_op jit(solution)/shard_map/attention_backward/pallas_call | solution.py:79
  62.7 2.9 %collective-permute-start.8 = (bf16[2,384,512]{2,1,0:T(8,128)(2,1)S(1)}, bf16[2,384,512]{2,1,0:T(8,128)(2,1)S(1)}, u32[]{:S(2)}, u32[]{:S(2)}) collective-permute-start(bf16[2,384,512]{2,1,0:T(8,128)(2,1)S(1)} %get-tuple-element.32), channel_id=1, source_target_pairs={{0,1},{1,0},{2,3},{3,2},{4,5},{5,4},{6,7},{7,6},{8,9},{9,8},{10,11... | collective-permute-start | bytes 2359304 | tf_op jit(solution)/shard_map/ppermute | solution.py:182
  65.6 1.9 %collective-permute-start.9 = (bf16[2,128,512]{2,1,0:T(8,128)(2,1)S(1)}, bf16[2,128,512]{2,1,0:T(8,128)(2,1)S(1)}, u32[]{:S(2)}, u32[]{:S(2)}) collective-permute-start(bf16[2,128,512]{2,1,0:T(8,128)(2,1)S(1)} %get-tuple-element.33), channel_id=1, source_target_pairs={{1,4},{3,6},{4,1},{5,8},{6,3},{7,10},{8,5},{9,12},{10,7},{11,14},{... | collective-permute-start | bytes 786440 | tf_op jit(solution)/shard_map/ppermute | solution.py:181
  67.5 0.3 fusion.3
  67.8 8.0 %collective-permute-start.11 = (bf16[2,128,512]{2,1,0:T(8,128)(2,1)S(1)}, bf16[2,128,512]{2,1,0:T(8,128)(2,1)S(1)}, u32[]{:S(2)}, u32[]{:S(2)}) collective-permute-start(bf16[2,128,512]{2,1,0:T(8,128)(2,1)S(1)} %get-tuple-element.39), channel_id=1, source_target_pairs={{0,2},{1,3},{2,4},{3,5},{4,6},{5,7},{6,8},{7,9},{8,10},{9,11},{10,... | collective-permute-start | bytes 786440 | tf_op jit(solution)/shard_map/ppermute | solution.py:186
  75.9 2.4 %collective-permute-start.10 = (bf16[2,128,512]{2,1,0:T(8,128)(2,1)S(1)}, bf16[2,128,512]{2,1,0:T(8,128)(2,1)S(1)}, u32[]{:S(2)}, u32[]{:S(2)}) collective-permute-start(bf16[2,128,512]{2,1,0:T(8,128)(2,1)S(1)} %get-tuple-element.40), channel_id=1, source_target_pairs={{2,0},{3,1},{4,2},{5,3},{6,4},{7,5},{8,6},{9,7},{10,8},{11,9},{12,... | collective-permute-start | bytes 786440 | tf_op jit(solution)/shard_map/ppermute | solution.py:185
  78.3 8.7 %collective-permute-done.11.refs_2_ = bf16[2,128,512]{2,1,0:T(8,128)(2,1)S(1)} collective-permute-done((bf16[2,128,512]{2,1,0:T(8,128)(2,1)S(1)}, bf16[2,128,512]{2,1,0:T(8,128)(2,1)S(1)}, u32[]{:S(2)}, u32[]{:S(2)}) %collective-permute-start.11) | collective-permute-done | bytes 262176 | tf_op jit(solution)/shard_map/ppermute | solution.py:186
  86.9 6.9 %collective-permute-done.10.refs_1_ = bf16[2,128,512]{2,1,0:T(8,128)(2,1)S(1)} collective-permute-done((bf16[2,128,512]{2,1,0:T(8,128)(2,1)S(1)}, bf16[2,128,512]{2,1,0:T(8,128)(2,1)S(1)}, u32[]{:S(2)}, u32[]{:S(2)}) %collective-permute-start.10) | collective-permute-done | bytes 262176 | tf_op jit(solution)/shard_map/ppermute | solution.py:185
  93.8 0.2 fusion.2
  94.0 0.7 fusion.5
  (17 shorter events, 0.1 us)
Async XLA Ops:
  1.7 24.5 %collective-permute-start.2 = (bf16[128,2048]{1,0:T(8,128)(2,1)S(1)}, bf16[128,2048]{1,0:T(8,128)(2,1)S(1)}, u32[]{:S(2)}, u32[]{:S(2)}) collective-permute-start(bf16[128,2048]{1,0:T(8,128)(2,1)S(1)} %slice.30), channel_id=1, source_target_pairs={{0,256},{256,0},{1,257},{257,1},{2,258},{258,2},{3,259},{259,3},{4... | collective-permute-start | bytes 1572872 | tf_op jit(solution)/shard_map/ppermute | solution.py:170
  5.7 0.9 copy-start
  6.6 0.9 copy-start.1
  7.6 28.9 %collective-permute-start.5 = (bf16[2,128,512]{2,1,0:T(8,128)(2,1)S(1)}, bf16[2,128,512]{2,1,0:T(8,128)(2,1)S(1)}, u32[]{:S(2)}, u32[]{:S(2)}) collective-permute-start(bf16[2,128,512]{2,1,0:T(8,128)(2,1)S(1)} %join.1.own.refs_4_.refs_3_), channel_id=1, source_target_pairs={{1,4},{3,6},{4,1},{5,8},{6,3},{7,10},{8,5},{9,12},{10,7},{11,14},{... | collective-permute-start | bytes 786440 | tf_op jit(solution)/shard_map/ppermute | solution.py:168
  15.4 15.0 %collective-permute-start.1 = (bf16[2,128,512]{2,1,0:T(8,128)(2,1)S(1)}, bf16[2,128,512]{2,1,0:T(8,128)(2,1)S(1)}, u32[]{:S(2)}, u32[]{:S(2)}) collective-permute-start(bf16[2,128,512]{2,1,0:T(8,128)(2,1)S(1)} %join.1.own.refs_4_.refs_3_), channel_id=1, source_target_pairs={{2,0},{3,1},{4,2},{5,3},{6,4},{7,5},{8,6},{9,7},{10,8},{11,9},{12,... | collective-permute-start | bytes 786440 | tf_op jit(solution)/shard_map/ppermute | solution.py:166
  17.3 17.0 %collective-permute-start = (bf16[2,128,512]{2,1,0:T(8,128)(2,1)S(1)}, bf16[2,128,512]{2,1,0:T(8,128)(2,1)S(1)}, u32[]{:S(2)}, u32[]{:S(2)}) collective-permute-start(bf16[2,128,512]{2,1,0:T(8,128)(2,1)S(1)} %join.1.own.refs_4_.refs_3_), channel_id=1, source_target_pairs={{0,2},{1,3},{2,4},{3,5},{4,6},{5,7},{6,8},{7,9},{8,10},{9,11},{10,... | collective-permute-start | bytes 786440 | tf_op jit(solution)/shard_map/ppermute | solution.py:165
  24.9 12.2 %collective-permute-start.6 = (bf16[128,2048]{1,0:T(8,128)(2,1)S(1)}, bf16[128,2048]{1,0:T(8,128)(2,1)S(1)}, u32[]{:S(2)}, u32[]{:S(2)}) collective-permute-start(bf16[128,2048]{1,0:T(8,128)(2,1)S(1)} %slice.30), channel_id=1, source_target_pairs={{32,0},{64,32},{96,64},{128,96},{160,128},{192,160},{224,192},{288... | collective-permute-start | bytes 1572872 | tf_op jit(solution)/shard_map/ppermute | solution.py:168
  26.2 14.7 %collective-permute-start.7 = (bf16[128,2048]{1,0:T(8,128)(2,1)S(1)}, bf16[128,2048]{1,0:T(8,128)(2,1)S(1)}, u32[]{:S(2)}, u32[]{:S(2)}) collective-permute-start(bf16[128,2048]{1,0:T(8,128)(2,1)S(1)} %hold.5), channel_id=1, source_target_pairs={{0,224},{256,480},{1,225},{257,481},{2,226},{258,482},{3,227},{259... | collective-permute-start | bytes 1572872 | tf_op jit(solution)/shard_map/ppermute | solution.py:175
  34.4 4.3 %copy-start.4 = (bf16[1,128,4096]{2,1,0:T(8,128)(2,1)S(1)}, bf16[1,128,4096]{2,1,0:T(8,128)(2,1)}, u32[]{:S(2)}) copy-start(bf16[1,128,4096]{2,1,0:T(8,128)(2,1)} %param.8) | copy-start | bytes 3145732
  34.4 4.3 %collective-permute-start.3 = (bf16[2,384,512]{2,1,0:T(8,128)(2,1)S(1)}, bf16[2,384,512]{2,1,0:T(8,128)(2,1)S(1)}, u32[]{:S(2)}, u32[]{:S(2)}) collective-permute-start(bf16[2,384,512]{2,1,0:T(8,128)(2,1)S(1)} %bundle.1), channel_id=1, source_target_pairs={{0,1},{1,0},{2,3},{3,2},{4,5},{5,4},{6,7},{7,6},{8,9},{9,8},{10,11... | collective-permute-start | bytes 2359304 | tf_op jit(solution)/shard_map/ppermute | solution.py:172
  38.8 2.1 %copy-start.2 = (bf16[1,128,4096]{2,1,0:T(8,128)(2,1)S(1)}, bf16[1,128,4096]{2,1,0:T(8,128)(2,1)}, u32[]{:S(2)}) copy-start(bf16[1,128,4096]{2,1,0:T(8,128)(2,1)} %param.5) | copy-start | bytes 3145732
  38.8 2.1 %copy-start.3 = (s32[1,7]{1,0:T(1,128)S(1)}, s32[1,7]{1,0:T(1,128)}, u32[]{:S(2)}) copy-start(s32[1,7]{1,0:T(1,128)} %refs_0_.3) | copy-start | bytes 88
  38.8 15.4 %collective-permute-start.4 = (bf16[128,2048]{1,0:T(8,128)(2,1)S(1)}, bf16[128,2048]{1,0:T(8,128)(2,1)S(1)}, u32[]{:S(2)}, u32[]{:S(2)}) collective-permute-start(bf16[128,2048]{1,0:T(8,128)(2,1)S(1)} %slice.24), channel_id=1, source_target_pairs={{0,480},{32,0},{64,32},{96,64},{128,96},{160,128},{192,160},{224,1... | collective-permute-start | bytes 1572872 | tf_op jit(solution)/shard_map/ppermute | solution.py:174
  62.7 4.8 %collective-permute-start.8 = (bf16[2,384,512]{2,1,0:T(8,128)(2,1)S(1)}, bf16[2,384,512]{2,1,0:T(8,128)(2,1)S(1)}, u32[]{:S(2)}, u32[]{:S(2)}) collective-permute-start(bf16[2,384,512]{2,1,0:T(8,128)(2,1)S(1)} %get-tuple-element.32), channel_id=1, source_target_pairs={{0,1},{1,0},{2,3},{3,2},{4,5},{5,4},{6,7},{7,6},{8,9},{9,8},{10,11... | collective-permute-start | bytes 2359304 | tf_op jit(solution)/shard_map/ppermute | solution.py:182
  65.6 12.7 %collective-permute-start.9 = (bf16[2,128,512]{2,1,0:T(8,128)(2,1)S(1)}, bf16[2,128,512]{2,1,0:T(8,128)(2,1)S(1)}, u32[]{:S(2)}, u32[]{:S(2)}) collective-permute-start(bf16[2,128,512]{2,1,0:T(8,128)(2,1)S(1)} %get-tuple-element.33), channel_id=1, source_target_pairs={{1,4},{3,6},{4,1},{5,8},{6,3},{7,10},{8,5},{9,12},{10,7},{11,14},{... | collective-permute-start | bytes 786440 | tf_op jit(solution)/shard_map/ppermute | solution.py:181
  67.8 19.1 %collective-permute-start.11 = (bf16[2,128,512]{2,1,0:T(8,128)(2,1)S(1)}, bf16[2,128,512]{2,1,0:T(8,128)(2,1)S(1)}, u32[]{:S(2)}, u32[]{:S(2)}) collective-permute-start(bf16[2,128,512]{2,1,0:T(8,128)(2,1)S(1)} %get-tuple-element.39), channel_id=1, source_target_pairs={{0,2},{1,3},{2,4},{3,5},{4,6},{5,7},{6,8},{7,9},{8,10},{9,11},{10,... | collective-permute-start | bytes 786440 | tf_op jit(solution)/shard_map/ppermute | solution.py:186
  75.9 18.0 %collective-permute-start.10 = (bf16[2,128,512]{2,1,0:T(8,128)(2,1)S(1)}, bf16[2,128,512]{2,1,0:T(8,128)(2,1)S(1)}, u32[]{:S(2)}, u32[]{:S(2)}) collective-permute-start(bf16[2,128,512]{2,1,0:T(8,128)(2,1)S(1)} %get-tuple-element.40), channel_id=1, source_target_pairs={{2,0},{3,1},{4,2},{5,3},{6,4},{7,5},{8,6},{9,7},{10,8},{11,9},{12,... | collective-permute-start | bytes 786440 | tf_op jit(solution)/shard_map/ppermute | solution.py:185

commit v12 on v11

--- a/solution.py
+++ b/solution.py
@@ -169,8 +169,8 @@
     )
     (turned,) = hold(lax.ppermute(low, "section", [(0, turn), (turn, 0)]), flops=1 << 33)
     left, right, _ = lax.optimization_barrier((left, right, turned))
-    mate = lax.ppermute(bundle(own, left, right), "seq", mate_pairs(count))
-    mate, cot = lax.optimization_barrier((mate, cot))
+    joined, cot = lax.optimization_barrier((bundle(own, left, right), cot))
+    (mate,) = hold(lax.ppermute(joined, "seq", mate_pairs(count)), flops=1 << 32)
     grad_high = lax.ppermute(cot[:, half:], "section", before)
     (grad_wrap,) = hold(lax.ppermute(turned, "section", [(0, turn - 1), (turn, sections - 1)]), flops=1 << 33)
     slots = (own, left, right, far, mate)

time: 95.2 us -> 91.1 us (0.957)
  waiting for transfers between devices: 26.6 us -> 23.3 us
  starting transfers between devices: 46 us -> 44.1 us
  local copies, waits for them, and re-layouts: 3.7 us -> 4.9 us
    ppermute x1, waiting for transfers between devices: 4.82 us -> 0.01 us  [shards(): grad_high = lax.ppermute(cot[:, half:], 'section', before)]
    ppermute x1, waiting for transfers between devices: 0.01 us -> 2.83 us  [shards(): lax.ppermute(turned, 'section', [(0, turn - 1), (turn, sections - 1)])]
    ppermute x1, waiting for transfers between devices: 1.64 us -> 0.01 us  [shards(): mate, = hold(lax.ppermute(joined, 'seq', mate_pairs(count)), flops=1 << 32)]
    ppermute x1, starting transfers between devices: 8.04 us -> 6.49 us  [shards(): lax.ppermute(sums[:, 2 * BL:].astype(B16), 'seq', shift_pairs(count, 2))]
    ppermute x1, waiting for transfers between devices: 6.89 us -> 8.16 us  [shards(): lax.ppermute(sums[:, BL:2 * BL].astype(B16), 'seq', shift_pairs(count, -2))]
    unnamed x10, local copies, waits for them, and re-layouts: 1.82 us -> 3.03 us
  transfers between devices with their start and end apart: 12 -> 12, of which waited for: 6 -> 5; matrix products, arithmetic and copies ran while one was open for 0% -> 0% of each run, Pallas kernels for 9% -> 9%
where the time goes in v12:
time: 91.1 us; the launch traced here: 90.6 us
  starting transfers between devices  44.1 us (48%)
  waiting for transfers between devices  23.3 us (26%)
  Pallas kernels  17 us (19%)
  local copies, waits for them, and re-layouts  4.9 us (5%)
    pallas_call x2, Pallas kernels, attention_backward(): pl.pallas_call(functools.partial(backward_body, len(grads), len(kept)), g...  17 us
    ppermute x1, waiting for transfers between devices, shards(): lax.ppermute(sums[:, BL:2 * BL].astype(B16), 'seq', shift_pairs(count, -2))  8.16 us
    ppermute x1, waiting for transfers between devices, shards(): lax.ppermute(sums[:, 2 * BL:].astype(B16), 'seq', shift_pairs(count, 2))  7.95 us
    ppermute x1, starting transfers between devices, shards(): lax.ppermute(own, 'seq', far_pairs(count))  7.8 us
    ppermute x1, starting transfers between devices, shards(): left = lax.ppermute(own, 'seq', shift_pairs(count, 2))  7.58 us
    ppermute x1, starting transfers between devices, shards(): lax.ppermute(sums[:, 2 * BL:].astype(B16), 'seq', shift_pairs(count, 2))  6.49 us
    ppermute x1, starting transfers between devices, shards(): lax.ppermute(turned, 'section', [(0, turn - 1), (turn, sections - 1)])  4.28 us
    ppermute x1, starting transfers between devices, shards(): lax.ppermute(low, 'section', [(0, turn), (turn, 0)])  4 us
  transfers between devices with their start and end apart: 12, of which 5 were waited for; matrix products, arithmetic and copies ran while one was open for 0% of the time, Pallas kernels for 9%

profile of v12, /device:TPU:135, one launch (start us, length us, event | category | flops | bytes accessed | tf_op | source)
XLA Modules:
  0.0 90.6 jit_solution(2931501103760788299)
XLA Ops:
  0.6 1.1 %slice.30 = bf16[128,2048]{1,0:T(8,128)(2,1)S(1)} slice(bf16[128,4096]{1,0:T(8,128)(2,1)} %bitcast.9), slice={[0:128], [0:2048]} | slice | bytes 1048576 | tf_op jit(solution)/shard_map/slice | solution.py:162
  1.7 4.0 %collective-permute-start.2 = (bf16[128,2048]{1,0:T(8,128)(2,1)S(1)}, bf16[128,2048]{1,0:T(8,128)(2,1)S(1)}, u32[]{:S(2)}, u32[]{:S(2)}) collective-permute-start(bf16[128,2048]{1,0:T(8,128)(2,1)S(1)} %slice.30), channel_id=1, source_target_pairs={{0,256},{256,0},{1,257},{257,1},{2,258},{258,2},{3,259},{259,3},{4... | collective-permute-start | bytes 1572872 | tf_op jit(solution)/shard_map/ppermute | solution.py:170
  5.7 0.0 copy-start
  5.7 0.9 copy-done
  6.6 0.9 copy-done.1
  7.6 7.8 %collective-permute-start.4 = (bf16[2,128,512]{2,1,0:T(8,128)(2,1)S(1)}, bf16[2,128,512]{2,1,0:T(8,128)(2,1)S(1)}, u32[]{:S(2)}, u32[]{:S(2)}) collective-permute-start(bf16[2,128,512]{2,1,0:T(8,128)(2,1)S(1)} %join.1.own.refs_4_.refs_3_), channel_id=1, source_target_pairs={{1,4},{3,6},{4,1},{5,8},{6,3},{7,10},{8,5},{9,12},{10,7},{11,14},{... | collective-permute-start | bytes 786440 | tf_op jit(solution)/shard_map/ppermute | solution.py:168
  15.4 1.9 %collective-permute-start.1 = (bf16[2,128,512]{2,1,0:T(8,128)(2,1)S(1)}, bf16[2,128,512]{2,1,0:T(8,128)(2,1)S(1)}, u32[]{:S(2)}, u32[]{:S(2)}) collective-permute-start(bf16[2,128,512]{2,1,0:T(8,128)(2,1)S(1)} %join.1.own.refs_4_.refs_3_), channel_id=1, source_target_pairs={{2,0},{3,1},{4,2},{5,3},{6,4},{7,5},{8,6},{9,7},{10,8},{11,9},{12,... | collective-permute-start | bytes 786440 | tf_op jit(solution)/shard_map/ppermute | solution.py:166
  17.3 7.6 %collective-permute-start = (bf16[2,128,512]{2,1,0:T(8,128)(2,1)S(1)}, bf16[2,128,512]{2,1,0:T(8,128)(2,1)S(1)}, u32[]{:S(2)}, u32[]{:S(2)}) collective-permute-start(bf16[2,128,512]{2,1,0:T(8,128)(2,1)S(1)} %join.1.own.refs_4_.refs_3_), channel_id=1, source_target_pairs={{0,2},{1,3},{2,4},{3,5},{4,6},{5,7},{6,8},{7,9},{8,10},{9,11},{10,... | collective-permute-start | bytes 786440 | tf_op jit(solution)/shard_map/ppermute | solution.py:165
  24.9 1.3 %collective-permute-start.5 = (bf16[128,2048]{1,0:T(8,128)(2,1)S(1)}, bf16[128,2048]{1,0:T(8,128)(2,1)S(1)}, u32[]{:S(2)}, u32[]{:S(2)}) collective-permute-start(bf16[128,2048]{1,0:T(8,128)(2,1)S(1)} %slice.30), channel_id=1, source_target_pairs={{32,0},{64,32},{96,64},{128,96},{160,128},{192,160},{224,192},{288... | collective-permute-start | bytes 1572872 | tf_op jit(solution)/shard_map/ppermute | solution.py:168
  26.2 0.0 collective-permute-done.2.refs_0_
  26.2 0.0 copy-start.4
  26.2 4.3 %collective-permute-start.7 = (bf16[128,2048]{1,0:T(8,128)(2,1)S(1)}, bf16[128,2048]{1,0:T(8,128)(2,1)S(1)}, u32[]{:S(2)}, u32[]{:S(2)}) collective-permute-start(bf16[128,2048]{1,0:T(8,128)(2,1)S(1)} %hold.6), channel_id=1, source_target_pairs={{0,224},{256,480},{1,225},{257,481},{2,226},{258,482},{3,227},{259... | collective-permute-start | bytes 1572872 | tf_op jit(solution)/shard_map/ppermute | solution.py:175
  30.5 0.0 collective-permute-done.1.right.refs_6_.refs_5_
  30.5 3.8 %collective-permute-done.left.refs_5_.refs_4_ = bf16[2,128,512]{2,1,0:T(8,128)(2,1)S(1)} collective-permute-done((bf16[2,128,512]{2,1,0:T(8,128)(2,1)S(1)}, bf16[2,128,512]{2,1,0:T(8,128)(2,1)S(1)}, u32[]{:S(2)}, u32[]{:S(2)}) %collective-permute-start) | collective-permute-done | bytes 262176 | tf_op jit(solution)/shard_map/ppermute | solution.py:165
  34.3 0.1 bundle.1
  34.5 1.9 %collective-permute-start.3 = (bf16[128,2048]{1,0:T(8,128)(2,1)S(1)}, bf16[128,2048]{1,0:T(8,128)(2,1)S(1)}, u32[]{:S(2)}, u32[]{:S(2)}) collective-permute-start(bf16[128,2048]{1,0:T(8,128)(2,1)S(1)} %slice.24), channel_id=1, source_target_pairs={{0,480},{32,0},{64,32},{96,64},{128,96},{160,128},{192,160},{224,1... | collective-permute-start | bytes 1572872 | tf_op jit(solution)/shard_map/ppermute | solution.py:174
  36.4 1.9 %collective-permute-start.6 = (bf16[2,384,512]{2,1,0:T(8,128)(2,1)S(1)}, bf16[2,384,512]{2,1,0:T(8,128)(2,1)S(1)}, u32[]{:S(2)}, u32[]{:S(2)}) collective-permute-start(bf16[2,384,512]{2,1,0:T(8,128)(2,1)S(1)} %bundle.1), channel_id=1, source_target_pairs={{0,1},{1,0},{2,3},{3,2},{4,5},{5,4},{6,7},{7,6},{8,9},{9,8},{10,11... | collective-permute-start | bytes 2359304 | tf_op jit(solution)/shard_map/ppermute | solution.py:173
  38.3 0.0 collective-permute-done.4.refs_0_
  38.3 2.8 %collective-permute-done.7.refs_0_ = bf16[128,2048]{1,0:T(8,128)(2,1)S(1)} collective-permute-done((bf16[128,2048]{1,0:T(8,128)(2,1)S(1)}, bf16[128,2048]{1,0:T(8,128)(2,1)S(1)}, u32[]{:S(2)}, u32[]{:S(2)}) %collective-permute-start.7) | collective-permute-done | bytes 524320 | tf_op jit(solution)/shard_map/ppermute | solution.py:175
  41.2 1.2 %copy-done.2 = bf16[1,128,4096]{2,1,0:T(8,128)(2,1)S(1)} copy-done((bf16[1,128,4096]{2,1,0:T(8,128)(2,1)S(1)}, bf16[1,128,4096]{2,1,0:T(8,128)(2,1)}, u32[]{:S(2)}) %copy-start.2) | copy-done | bytes 1048600
  42.4 8.5 %attention_backward.2 = (bf16[128,4096]{1,0:T(8,128)(2,1)}, f32[2,384,512]{2,1,0:T(8,128)S(1)}, bf16[2,384,512]{2,1,0:T(8,128)(2,1)S(1)}, bf16[2,128,512]{2,1,0:T(8,128)(2,1)S(1)}) custom-call(s32[1,7]{1,0:T(1,128)S(1)} %copy-done.3, bf16[128,4096]{1,0:T(8,128)(2,1)S(1)} %bitcast.7, bf16[128,2048]{1,0:T(8,128)(2,1)S(1)} %get-tuple-element.25.refs_2_, ...), custom_call_target="tpu_custom_call" | custom-call | flops 2147483648 | bytes 2097152 | tf_op jit(solution)/shard_map/attention_backward/pallas_call | solution.py:79
  50.9 8.5 %attention_backward.3 = (bf16[128,4096]{1,0:T(8,128)(2,1)}, f32[2,384,512]{2,1,0:T(8,128)S(1)}, bf16[2,384,512]{2,1,0:T(8,128)(2,1)S(1)}, bf16[2,128,512]{2,1,0:T(8,128)(2,1)S(1)}) custom-call(s32[1,7]{1,0:T(1,128)S(1)} %copy-done.3, bf16[128,4096]{1,0:T(8,128)(2,1)S(1)} %bitcast.8, ...), custom_call_target="tpu_custom_call", output_to_operand_aliasing={{0}: (8, {}), {1}: (9, {}), {2}: (10, {}), {3}: (11, {})} | custom-call | flops 2147483648 | bytes 2097152 | tf_op jit(solution)/shard_map/attention_backward/pallas_call | solution.py:79
  59.4 1.9 %collective-permute-start.8 = (bf16[2,384,512]{2,1,0:T(8,128)(2,1)S(1)}, bf16[2,384,512]{2,1,0:T(8,128)(2,1)S(1)}, u32[]{:S(2)}, u32[]{:S(2)}) collective-permute-start(bf16[2,384,512]{2,1,0:T(8,128)(2,1)S(1)} %get-tuple-element.32), channel_id=1, source_target_pairs={{0,1},{1,0},{2,3},{3,2},{4,5},{5,4},{6,7},{7,6},{8,9},{9,8},{10,11... | collective-permute-start | bytes 2359304 | tf_op jit(solution)/shard_map/ppermute | solution.py:182
  61.3 2.4 %collective-permute-start.9 = (bf16[2,128,512]{2,1,0:T(8,128)(2,1)S(1)}, bf16[2,128,512]{2,1,0:T(8,128)(2,1)S(1)}, u32[]{:S(2)}, u32[]{:S(2)}) collective-permute-start(bf16[2,128,512]{2,1,0:T(8,128)(2,1)S(1)} %get-tuple-element.33), channel_id=1, source_target_pairs={{1,4},{3,6},{4,1},{5,8},{6,3},{7,10},{8,5},{9,12},{10,7},{11,14},{... | collective-permute-start | bytes 786440 | tf_op jit(solution)/shard_map/ppermute | solution.py:181
  63.7 0.3 fusion.3
  64.0 6.5 %collective-permute-start.11 = (bf16[2,128,512]{2,1,0:T(8,128)(2,1)S(1)}, bf16[2,128,512]{2,1,0:T(8,128)(2,1)S(1)}, u32[]{:S(2)}, u32[]{:S(2)}) collective-permute-start(bf16[2,128,512]{2,1,0:T(8,128)(2,1)S(1)} %get-tuple-element.39), channel_id=1, source_target_pairs={{0,2},{1,3},{2,4},{3,5},{4,6},{5,7},{6,8},{7,9},{8,10},{9,11},{10,... | collective-permute-start | bytes 786440 | tf_op jit(solution)/shard_map/ppermute | solution.py:186
  70.5 2.6 %collective-permute-start.10 = (bf16[2,128,512]{2,1,0:T(8,128)(2,1)S(1)}, bf16[2,128,512]{2,1,0:T(8,128)(2,1)S(1)}, u32[]{:S(2)}, u32[]{:S(2)}) collective-permute-start(bf16[2,128,512]{2,1,0:T(8,128)(2,1)S(1)} %get-tuple-element.40), channel_id=1, source_target_pairs={{2,0},{3,1},{4,2},{5,3},{6,4},{7,5},{8,6},{9,7},{10,8},{11,9},{12,... | collective-permute-start | bytes 786440 | tf_op jit(solution)/shard_map/ppermute | solution.py:185
  73.1 0.5 collective-permute-done.9.refs_0_
  73.6 8.0 %collective-permute-done.11.refs_2_ = bf16[2,128,512]{2,1,0:T(8,128)(2,1)S(1)} collective-permute-done((bf16[2,128,512]{2,1,0:T(8,128)(2,1)S(1)}, bf16[2,128,512]{2,1,0:T(8,128)(2,1)S(1)}, u32[]{:S(2)}, u32[]{:S(2)}) %collective-permute-start.11) | collective-permute-done | bytes 262176 | tf_op jit(solution)/shard_map/ppermute | solution.py:186
  81.6 8.2 %collective-permute-done.10.refs_1_ = bf16[2,128,512]{2,1,0:T(8,128)(2,1)S(1)} collective-permute-done((bf16[2,128,512]{2,1,0:T(8,128)(2,1)S(1)}, bf16[2,128,512]{2,1,0:T(8,128)(2,1)S(1)}, u32[]{:S(2)}, u32[]{:S(2)}) %collective-permute-start.10) | collective-permute-done | bytes 262176 | tf_op jit(solution)/shard_map/ppermute | solution.py:185
  89.8 0.2 fusion.2
  89.9 0.7 fusion.5
  (18 shorter events, 0.1 us)
Async XLA Ops:
  1.7 24.5 %collective-permute-start.2 = (bf16[128,2048]{1,0:T(8,128)(2,1)S(1)}, bf16[128,2048]{1,0:T(8,128)(2,1)S(1)}, u32[]{:S(2)}, u32[]{:S(2)}) collective-permute-start(bf16[128,2048]{1,0:T(8,128)(2,1)S(1)} %slice.30), channel_id=1, source_target_pairs={{0,256},{256,0},{1,257},{257,1},{2,258},{258,2},{3,259},{259,3},{4... | collective-permute-start | bytes 1572872 | tf_op jit(solution)/shard_map/ppermute | solution.py:170
  5.7 0.9 %copy-start = (bf16[1,128,512]{2,1,0:T(8,128)(2,1)S(1)}, bf16[1,128,512]{2,1,0:T(8,128)(2,1)}, u32[]{:S(2)}) copy-start(bf16[1,128,512]{2,1,0:T(8,128)(2,1)} %param.6) | copy-start | bytes 393220
  6.6 0.9 copy-start.1
  7.6 30.8 %collective-permute-start.4 = (bf16[2,128,512]{2,1,0:T(8,128)(2,1)S(1)}, bf16[2,128,512]{2,1,0:T(8,128)(2,1)S(1)}, u32[]{:S(2)}, u32[]{:S(2)}) collective-permute-start(bf16[2,128,512]{2,1,0:T(8,128)(2,1)S(1)} %join.1.own.refs_4_.refs_3_), channel_id=1, source_target_pairs={{1,4},{3,6},{4,1},{5,8},{6,3},{7,10},{8,5},{9,12},{10,7},{11,14},{... | collective-permute-start | bytes 786440 | tf_op jit(solution)/shard_map/ppermute | solution.py:168
  15.4 15.1 %collective-permute-start.1 = (bf16[2,128,512]{2,1,0:T(8,128)(2,1)S(1)}, bf16[2,128,512]{2,1,0:T(8,128)(2,1)S(1)}, u32[]{:S(2)}, u32[]{:S(2)}) collective-permute-start(bf16[2,128,512]{2,1,0:T(8,128)(2,1)S(1)} %join.1.own.refs_4_.refs_3_), channel_id=1, source_target_pairs={{2,0},{3,1},{4,2},{5,3},{6,4},{7,5},{8,6},{9,7},{10,8},{11,9},{12,... | collective-permute-start | bytes 786440 | tf_op jit(solution)/shard_map/ppermute | solution.py:166
  17.3 17.0 %collective-permute-start = (bf16[2,128,512]{2,1,0:T(8,128)(2,1)S(1)}, bf16[2,128,512]{2,1,0:T(8,128)(2,1)S(1)}, u32[]{:S(2)}, u32[]{:S(2)}) collective-permute-start(bf16[2,128,512]{2,1,0:T(8,128)(2,1)S(1)} %join.1.own.refs_4_.refs_3_), channel_id=1, source_target_pairs={{0,2},{1,3},{2,4},{3,5},{4,6},{5,7},{6,8},{7,9},{8,10},{9,11},{10,... | collective-permute-start | bytes 786440 | tf_op jit(solution)/shard_map/ppermute | solution.py:165
  24.9 13.4 %collective-permute-start.5 = (bf16[128,2048]{1,0:T(8,128)(2,1)S(1)}, bf16[128,2048]{1,0:T(8,128)(2,1)S(1)}, u32[]{:S(2)}, u32[]{:S(2)}) collective-permute-start(bf16[128,2048]{1,0:T(8,128)(2,1)S(1)} %slice.30), channel_id=1, source_target_pairs={{32,0},{64,32},{96,64},{128,96},{160,128},{192,160},{224,192},{288... | collective-permute-start | bytes 1572872 | tf_op jit(solution)/shard_map/ppermute | solution.py:168
  26.2 8.2 %copy-start.4 = (bf16[1,128,4096]{2,1,0:T(8,128)(2,1)S(1)}, bf16[1,128,4096]{2,1,0:T(8,128)(2,1)}, u32[]{:S(2)}) copy-start(bf16[1,128,4096]{2,1,0:T(8,128)(2,1)} %param.8) | copy-start | bytes 3145732
  26.2 15.0 %collective-permute-start.7 = (bf16[128,2048]{1,0:T(8,128)(2,1)S(1)}, bf16[128,2048]{1,0:T(8,128)(2,1)S(1)}, u32[]{:S(2)}, u32[]{:S(2)}) collective-permute-start(bf16[128,2048]{1,0:T(8,128)(2,1)S(1)} %hold.6), channel_id=1, source_target_pairs={{0,224},{256,480},{1,225},{257,481},{2,226},{258,482},{3,227},{259... | collective-permute-start | bytes 1572872 | tf_op jit(solution)/shard_map/ppermute | solution.py:175
  34.5 16.4 %collective-permute-start.3 = (bf16[128,2048]{1,0:T(8,128)(2,1)S(1)}, bf16[128,2048]{1,0:T(8,128)(2,1)S(1)}, u32[]{:S(2)}, u32[]{:S(2)}) collective-permute-start(bf16[128,2048]{1,0:T(8,128)(2,1)S(1)} %slice.24), channel_id=1, source_target_pairs={{0,480},{32,0},{64,32},{96,64},{128,96},{160,128},{192,160},{224,1... | collective-permute-start | bytes 1572872 | tf_op jit(solution)/shard_map/ppermute | solution.py:174
  36.4 4.8 %collective-permute-start.6 = (bf16[2,384,512]{2,1,0:T(8,128)(2,1)S(1)}, bf16[2,384,512]{2,1,0:T(8,128)(2,1)S(1)}, u32[]{:S(2)}, u32[]{:S(2)}) collective-permute-start(bf16[2,384,512]{2,1,0:T(8,128)(2,1)S(1)} %bundle.1), channel_id=1, source_target_pairs={{0,1},{1,0},{2,3},{3,2},{4,5},{5,4},{6,7},{7,6},{8,9},{9,8},{10,11... | collective-permute-start | bytes 2359304 | tf_op jit(solution)/shard_map/ppermute | solution.py:173
  41.2 1.2 %copy-start.2 = (bf16[1,128,4096]{2,1,0:T(8,128)(2,1)S(1)}, bf16[1,128,4096]{2,1,0:T(8,128)(2,1)}, u32[]{:S(2)}) copy-start(bf16[1,128,4096]{2,1,0:T(8,128)(2,1)} %param.5) | copy-start | bytes 3145732
  41.2 1.2 %copy-start.3 = (s32[1,7]{1,0:T(1,128)S(1)}, s32[1,7]{1,0:T(1,128)}, u32[]{:S(2)}) copy-start(s32[1,7]{1,0:T(1,128)} %refs_0_.3) | copy-start | bytes 88
  59.4 4.3 %collective-permute-start.8 = (bf16[2,384,512]{2,1,0:T(8,128)(2,1)S(1)}, bf16[2,384,512]{2,1,0:T(8,128)(2,1)S(1)}, u32[]{:S(2)}, u32[]{:S(2)}) collective-permute-start(bf16[2,384,512]{2,1,0:T(8,128)(2,1)S(1)} %get-tuple-element.32), channel_id=1, source_target_pairs={{0,1},{1,0},{2,3},{3,2},{4,5},{5,4},{6,7},{7,6},{8,9},{9,8},{10,11... | collective-permute-start | bytes 2359304 | tf_op jit(solution)/shard_map/ppermute | solution.py:182
  61.3 12.4 %collective-permute-start.9 = (bf16[2,128,512]{2,1,0:T(8,128)(2,1)S(1)}, bf16[2,128,512]{2,1,0:T(8,128)(2,1)S(1)}, u32[]{:S(2)}, u32[]{:S(2)}) collective-permute-start(bf16[2,128,512]{2,1,0:T(8,128)(2,1)S(1)} %get-tuple-element.33), channel_id=1, source_target_pairs={{1,4},{3,6},{4,1},{5,8},{6,3},{7,10},{8,5},{9,12},{10,7},{11,14},{... | collective-permute-start | bytes 786440 | tf_op jit(solution)/shard_map/ppermute | solution.py:181
  64.0 17.6 %collective-permute-start.11 = (bf16[2,128,512]{2,1,0:T(8,128)(2,1)S(1)}, bf16[2,128,512]{2,1,0:T(8,128)(2,1)S(1)}, u32[]{:S(2)}, u32[]{:S(2)}) collective-permute-start(bf16[2,128,512]{2,1,0:T(8,128)(2,1)S(1)} %get-tuple-element.39), channel_id=1, source_target_pairs={{0,2},{1,3},{2,4},{3,5},{4,6},{5,7},{6,8},{7,9},{8,10},{9,11},{10,... | collective-permute-start | bytes 786440 | tf_op jit(solution)/shard_map/ppermute | solution.py:186
  70.5 19.2 %collective-permute-start.10 = (bf16[2,128,512]{2,1,0:T(8,128)(2,1)S(1)}, bf16[2,128,512]{2,1,0:T(8,128)(2,1)S(1)}, u32[]{:S(2)}, u32[]{:S(2)}) collective-permute-start(bf16[2,128,512]{2,1,0:T(8,128)(2,1)S(1)} %get-tuple-element.40), channel_id=1, source_target_pairs={{2,0},{3,1},{4,2},{5,3},{6,4},{7,5},{8,6},{9,7},{10,8},{11,9},{12,... | collective-permute-start | bytes 786440 | tf_op jit(solution)/shard_map/ppermute | solution.py:185
